TPU v7x, 32 devices: a whole 2x2x4 slice. The times are simulated.
32 devices in a mesh: ctx: 16 (over z, y, core), head: 2 (over x).
Axes of the slice: x: 2, y: 2, z: 4, core: 2. Of those that a mesh axis runs over, the one named last changes fastest.
Arguments:
- queries: bfloat16 [16, 8192, 128], P('head', 'ctx'), may hold values from -20 to 20
- keys: bfloat16 [16, 8192, 128], P('head', 'ctx'), may hold values from -20 to 20
- values: bfloat16 [16, 8192, 128], P('head', 'ctx'), may hold values from -60 to 60
- out_grad: bfloat16 [16, 8192, 128], P('head', 'ctx'), may hold values from -6 to 6
- norm_gain: float32 [16, 128], P('head'), may hold values from 0.25 to 1.75
- doc_start: int32 [8192], replicated, may hold values from 0 to 1536, as said below
- head_offsets: int32 [16], P('head'), may hold values from 0 to 31
Outputs:
- normed: bfloat16 [16, 8192, 128], P('head', 'ctx')
- grad_queries: bfloat16 [16, 8192, 128], P('head', 'ctx')
- grad_keys: bfloat16 [16, 8192, 128], P('head', 'ctx')
- grad_values: bfloat16 [16, 8192, 128], P('head', 'ctx')
Inputs may be any that keep to these rules, and one draw needn't show every extreme that they name: `doc_start`: each entry is the first position of its token's document: the token's own position or the previous token's entry; the window holds 4 documents, the last of which starts at (3) * 512.
All inputs are finite; a program needn't handle non-finite values.
Results may differ from a plain program's by a relative error of at most 0.023.
Values may be sent and summed in bfloat16 or wider, within the bound.
No kernel may reach another device: no remote copies, remote signals or barrier semaphores. Data moves between devices by JAX's collectives and lax.ppermute only.
A program may use at most 128 MiB of HBM per device.

v0:
```python
import math

import jax
import jax.numpy as jnp
from jax import lax
from jax.sharding import PartitionSpec as P

HEADS = 16
SEL = 256


theta_base = 10000.0
eps_norm = 1e-06


def from_behind(array, axis, by):
    devices = lax.axis_size(axis)
    pairs = [(i, i + by) for i in range(devices) if 0 <= i + by < devices]
    return lax.ppermute(array, axis, pairs)


def rotate(field, rel, sign):
    half = field.shape[-1] // 2
    freq = theta_base ** (-2.0 * jnp.arange(half).astype(rel.dtype) / field.shape[-1])
    angle = rel[:, None] * freq[None, :]
    cosine = jnp.cos(angle)
    sine = sign * jnp.sin(angle)
    first = field[..., :half]
    second = field[..., half:]
    return jnp.concatenate(
        [first * cosine - second * sine, second * cosine + first * sine], axis=-1
    )


def body(queries, keys, values, out_grad, norm_gain, doc_start, head_offsets):
    f32 = jnp.float32
    bf16 = jnp.bfloat16
    heads_local, tok_local, width = queries.shape
    ctx_count = lax.axis_size("ctx")
    rate = ctx_count * tok_local // SEL
    blocks = tok_local // rate
    scale = 1.0 / math.sqrt(width)
    index = lax.axis_index("ctx")
    base = index * tok_local
    local = jnp.arange(tok_local, dtype=jnp.int32)
    global_pos = base + local
    starts = lax.dynamic_slice_in_dim(doc_start, base, tok_local)
    rel = (global_pos - starts).astype(f32)
    q_rot = rotate(queries.astype(f32), rel, 1.0).astype(bf16)
    k_rot = rotate(keys.astype(f32), rel, 1.0).astype(bf16)
    prev_keys, prev_values = from_behind((k_rot, values), "ctx", 1)
    lanes = jnp.arange(rate, dtype=jnp.int32)
    pick_mask = head_offsets[:, None] == lanes[None, :]
    pick_b = pick_mask.astype(bf16)

    def select(field):
        grid = field.reshape(heads_local, blocks, rate, width)
        return jnp.einsum("hard,hr->had", grid, pick_b, preferred_element_type=f32).astype(bf16)

    def place(dense, sparse):
        grid = dense.reshape(heads_local, blocks, rate, width)
        grid = grid + jnp.where(pick_mask[:, None, :, None], sparse[:, :, None, :], 0.0)
        return grid.reshape(heads_local, tok_local, width)

    q_sel = select(q_rot)
    k_sel = select(k_rot)
    v_sel = select(values)
    all_keys, all_values = (
        lax.all_gather(k_sel, "ctx", axis=1, tiled=True),
        lax.all_gather(v_sel, "ctx", axis=1, tiled=True),
    )
    row_block = jnp.arange(blocks, dtype=jnp.int32)
    query_pos = base + row_block[None, :] * rate + head_offsets[:, None]
    query_start = jnp.take(doc_start, query_pos)
    key_order = jnp.arange(all_keys.shape[1], dtype=jnp.int32)
    key_pos = head_offsets[:, None] + rate * key_order[None, :]
    query_order = index * blocks + row_block
    sparse_mask = (key_order[None, None, :] <= query_order[None, :, None]) & (
        key_pos[:, None, :] >= query_start[:, :, None]
    )
    pair_index = jnp.arange(2 * tok_local, dtype=jnp.int32)
    pair_pos = base - tok_local + pair_index
    head_first = lax.axis_index("head") * heads_local
    head_phase = (head_first + jnp.arange(heads_local, dtype=jnp.int32)) % 2
    reads_prev = (index + head_phase) % 2 == 1
    base_mask = (pair_pos[None, :] <= global_pos[:, None]) & (pair_pos[None, :] >= starts[:, None])
    pair_mask = base_mask[None] & (
        (pair_index >= tok_local)[None, None, :] | reads_prev[:, None, None]
    )
    keys_pair = jnp.concatenate([prev_keys, k_rot], axis=1)
    values_pair = jnp.concatenate([prev_values, values], axis=1)

    def near_scores(q_h, k_h, mask_h):
        score = jnp.einsum("id,jd->ij", q_h, k_h, preferred_element_type=f32) * scale
        return jnp.where(mask_h, score, -jnp.inf)

    def far_scores(q1_h, k1_h, mask1_h):
        score = jnp.einsum("id,jd->ij", q1_h, k1_h, preferred_element_type=f32) * scale
        return jnp.where(mask1_h, score, -jnp.inf)

    def forward_head(item):
        q_h, k_h, v_h, mask_h, q1_h, k1_h, v1_h, mask1_h, pick_h = item
        z_near = near_scores(q_h, k_h, mask_h)
        lse_near = jax.nn.logsumexp(z_near, axis=1)
        z_far = far_scores(q1_h, k1_h, mask1_h)
        lse_far = jax.nn.logsumexp(z_far, axis=1)
        grid = lse_near.reshape(blocks, rate)
        lse_one = jnp.logaddexp(jnp.sum(jnp.where(pick_h[None, :], grid, 0.0), axis=1), lse_far)
        lse_all = jnp.where(pick_h[None, :], lse_one[:, None], grid).reshape(tok_local)
        p_near = jnp.exp(z_near - lse_all[:, None]).astype(bf16)
        p_far = jnp.exp(z_far - lse_one[:, None]).astype(bf16)
        o_near = jnp.dot(p_near, v_h, preferred_element_type=f32)
        o_far = jnp.dot(p_far, v1_h, preferred_element_type=f32)
        total = o_near.reshape(blocks, rate, width) + jnp.where(
            pick_h[None, :, None], o_far[:, None, :], 0.0
        )
        return (total.reshape(tok_local, width).astype(bf16), lse_all, lse_one)

    attn, lse_all, lse_sel = lax.map(
        forward_head,
        (
            q_rot,
            keys_pair,
            values_pair,
            pair_mask,
            q_sel,
            all_keys,
            all_values,
            sparse_mask,
            pick_mask,
        ),
    )
    attn_f = attn.astype(f32)
    gain = norm_gain[:, None, :]
    scaled_grad = gain * out_grad.astype(f32)
    feats = HEADS * width
    square_sum, cross_sum = lax.psum(
        (jnp.sum(attn_f * attn_f, axis=(0, 2)), jnp.sum(scaled_grad * attn_f, axis=(0, 2))), "head"
    )
    rinv = lax.rsqrt(square_sum / feats + eps_norm)
    attn_grad = (
        rinv[None, :, None]
        * (scaled_grad - attn_f * (rinv * rinv * cross_sum / feats)[None, :, None])
    ).astype(bf16)
    normed = (attn_f * rinv[None, :, None] * gain).astype(bf16)
    delta = jnp.sum(attn_grad.astype(f32) * attn_f, axis=2)
    grad_sel = select(attn_grad)
    grid = delta.reshape(heads_local, blocks, rate)
    delta_sel = jnp.sum(jnp.where(pick_mask[:, None, :], grid, 0.0), axis=2)

    def backward_head(item):
        (
            q_h,
            k_h,
            v_h,
            mask_h,
            q1_h,
            k1_h,
            v1_h,
            mask1_h,
            lse_h,
            lse1_h,
            grad_h,
            delta_h,
            grad1_h,
            delta1_h,
        ) = item
        p_near = jnp.exp(near_scores(q_h, k_h, mask_h) - lse_h[:, None]).astype(bf16)
        dp_near = jnp.einsum("id,jd->ij", grad_h, v_h, preferred_element_type=f32)
        ds_near = (p_near.astype(f32) * (dp_near - delta_h[:, None])).astype(bf16)
        dq_near = jnp.dot(ds_near, k_h, preferred_element_type=f32) * scale
        dk_near = jnp.einsum("ij,id->jd", ds_near, q_h, preferred_element_type=f32) * scale
        dv_near = jnp.einsum("ij,id->jd", p_near, grad_h, preferred_element_type=f32)
        p_far = jnp.exp(far_scores(q1_h, k1_h, mask1_h) - lse1_h[:, None]).astype(bf16)
        dp_far = jnp.einsum("id,jd->ij", grad1_h, v1_h, preferred_element_type=f32)
        ds_far = (p_far.astype(f32) * (dp_far - delta1_h[:, None])).astype(bf16)
        dq_far = jnp.dot(ds_far, k1_h, preferred_element_type=f32) * scale
        return (dq_near, dk_near, dv_near, dq_far, ds_far, p_far)

    dq_near, dk_near, dv_near, dq_far, ds_far, p_far = lax.map(
        backward_head,
        (
            q_rot,
            keys_pair,
            values_pair,
            pair_mask,
            q_sel,
            all_keys,
            all_values,
            sparse_mask,
            lse_all,
            lse_sel,
            attn_grad,
            delta,
            grad_sel,
            delta_sel,
        ),
    )
    dq_total = place(dq_near, dq_far)
    back_k, back_v = from_behind(
        (dk_near[:, :tok_local].astype(bf16), dv_near[:, :tok_local].astype(bf16)), "ctx", -1
    )
    key_total = dk_near[:, tok_local:] + back_k.astype(f32)
    value_total = dv_near[:, tok_local:] + back_v.astype(f32)
    dk_part = jnp.einsum("haj,had->jhd", ds_far, q_sel, preferred_element_type=f32) * scale
    dv_part = jnp.einsum("haj,had->jhd", p_far, grad_sel, preferred_element_type=f32)
    summed = lax.psum_scatter(
        jnp.stack([dk_part, dv_part], axis=1), "ctx", scatter_dimension=0, tiled=True
    )
    sparse_k = jnp.swapaxes(summed[:, 0], 0, 1)
    sparse_v = jnp.swapaxes(summed[:, 1], 0, 1)
    key_total = place(key_total, sparse_k)
    value_total = place(value_total, sparse_v)
    grad_queries = rotate(dq_total, rel, -1.0).astype(bf16)
    grad_keys = rotate(key_total, rel, -1.0).astype(bf16)
    grad_values = value_total.astype(bf16)
    return (normed, grad_queries, grad_keys, grad_values)


def solution(mesh):
    return jax.shard_map(
        body,
        mesh=mesh,
        in_specs=(
            P("head", "ctx", None),
            P("head", "ctx", None),
            P("head", "ctx", None),
            P("head", "ctx", None),
            P("head", None),
            P(),
            P("head"),
        ),
        out_specs=(
            P("head", "ctx", None),
            P("head", "ctx", None),
            P("head", "ctx", None),
            P("head", "ctx", None),
        ),
        check_vma=False,
    )
```

profile of v0, /device:TPU:0, one launch (start us, length us, event | category | flops | bytes accessed | tf_op | source)
XLA Modules:
  0.0 382.5 jit_solution(2084287606520976319)
XLA Ops:
  10.3 1.7 broadcast_multiply_fusion
  12.0 5.0 %subtract_convert_fusion.2 = (bf16[8,512,64]{2,1,0:T(8,128)(2,1)S(1)}, bf16[8,512,64]{2,1,0:T(8,128)(2,1)S(1)}, bf16[8,512,64]{2,1,0:T(8,128)(2,1)}, bf16[8,512,64]{2,1,0:T(8,128)(2,1)}) fusion(f32[8,512,128]{2,1,0:T(8,128)S(1)} %convert_element_type.104, f32[512,64]{1,0:T(8,128)S(1)} %get-tuple-element.301, f32[512,64]{1,0:T(8,128)S(1)} %get-tuple-element.302, ...), kind=kLoop, calls=%fused_computation.143 | loop fusion | flops 4194304 | bytes 6553600 | tf_op jit(solution)/shard_map/convert.14
  19.5 3.4 collective-permute-start
  22.9 4.6 %collective-permute-start.1 = (bf16[8,512,128]{2,1,0:T(8,128)(2,1)}, bf16[8,512,128]{2,1,0:T(8,128)(2,1)}, u32[]{:S(2)}, u32[]{:S(2)}) collective-permute-start(bf16[8,512,128]{2,1,0:T(8,128)(2,1)} %param.13), channel_id=1, source_target_pairs={{0,2},{2,4},{4,6},{6,8},{8,10},{10,12},{12,14},{14,16},{16,18},{18... | collective-permute-start | bytes 3145736 | tf_op jit(solution)/shard_map/ppermute | solution.py:19
  30.9 3.9 %broadcast_and_fusion = pred[8,512,1024]{2,1,0:T(32,128)(4,1)} fusion(pred[8,1024]{1,0:T(8,128)(4,1)S(1)} %broadcast_or_fusion, pred[512,1024]{1,0:T(8,128)(4,1)S(1)} %compare_and_fusion), kind=kLoop, calls=%fused_computation.112 | loop fusion | flops 4194304 | bytes 4726784 | tf_op jit(solution)/shard_map/and | solution.py:87
  42.8 22.1 %all_gather.6 = bf16[8,256,128]{2,1,0:T(8,128)(2,1)} all-gather(bf16[8,16,128]{2,1,0:T(8,128)(2,1)S(1)} %convert_element_type.106), channel_id=1, replica_groups=mesh['ctx'=16,'head'=2] {'ctx'}, dimensions={1}, use_global_device_ids=true | all-gather | bytes 557056 | tf_op jit(solution)/shard_map/all_gather | solution.py:69
  64.9 22.4 %all_gather.7 = bf16[8,256,128]{2,1,0:T(8,128)(2,1)} all-gather(bf16[8,16,128]{2,1,0:T(8,128)(2,1)S(1)} %convert_element_type.107), channel_id=1, replica_groups=mesh['ctx'=16,'head'=2] {'ctx'}, dimensions={1}, use_global_device_ids=true | all-gather | bytes 557056 | tf_op jit(solution)/shard_map/all_gather | solution.py:70
  87.3 2.4 constant_dynamic-update-slice_fusion.1
  89.7 2.4 constant_dynamic-update-slice_fusion
  92.1 3.2 maximum_maximum_fusion
  95.3 83.1 %while.36 = (s32[]{:T(128)}, bf16[8,512,128]{2,1,0:T(8,128)(2,1)}, f32[8,512]{1,0:T(8,128)}, f32[8,16]{1,0:T(8,128)}, pred[8,512,1024]{2,1,0:T(32,128)(4,1)}, /*...) while((s32[]{:T(128)}, bf16[8,512,128]{2,1,0:T(8,128)(2,1)}, ...), condition=%wide.region_6.7_spmd.clone, body=%wide.region_0.6_spmd.sunk.clone | while | flops 274435968 | bytes 10233789 | solution.py:119
  95.3 1.7 fusion.184
  105.7 1.7 fusion.184
  116.1 1.7 fusion.184
  126.5 1.7 fusion.184
  136.8 1.7 fusion.184
  147.2 1.7 fusion.184
  157.6 1.7 fusion.184
  168.0 1.7 fusion.184
  178.4 2.2 fusion.78
  180.6 4.9 %all-reduce = (f32[512]{0:T(512)S(1)}, f32[512]{0:T(512)S(1)}) all-reduce(f32[512]{0:T(512)S(1)} %get-tuple-element.195, f32[512]{0:T(512)S(1)} %get-tuple-element.194), channel_id=1, replica_groups=mesh['ctx'=16,'head'=2] {'head'}, use_global_device_ids=true, to_apply=%region_8.9 | all-reduce | flops 1024 | bytes 8192 | tf_op jit(solution)/shard_map/psum | solution.py:137
  185.5 3.2 fusion.82
  189.1 112.0 %while.37 = (s32[]{:T(128)}, f32[8,512,128]{2,1,0:T(8,128)}, f32[8,1024,128]{2,1,0:T(8,128)}, f32[8,1024,128]{2,1,0:T(8,128)}, f32[8,16,128]{2,1,0:T(8,128)}, /*...) while((s32[]{:T(128)}, f32[8,512,128]{2,1,0:T(8,128)}, ...), condition=%wide.region_14.15_spmd.clone, body=%wide.region_13.14_spmd.sunk.clone | while | flops 678660096 | bytes 9726925 | solution.py:180
  189.9 1.8 exponential_convert_fusion.12
  193.1 2.1 fusion.203
  203.9 1.8 exponential_convert_fusion.12
  207.1 2.1 fusion.203
  217.9 1.8 exponential_convert_fusion.12
  221.1 2.1 fusion.203
  226.4 1.6 bitcast_dynamic-update-slice_fusion.10
  231.9 1.8 exponential_convert_fusion.12
  235.1 2.1 fusion.203
  245.9 1.8 exponential_convert_fusion.12
  249.1 2.1 fusion.203
  254.4 1.6 bitcast_dynamic-update-slice_fusion.10
  259.9 1.8 exponential_convert_fusion.12
  263.1 2.1 fusion.203
  270.0 1.6 bitcast_dynamic-update-slice_fusion.11
  273.9 1.8 exponential_convert_fusion.12
  277.1 2.1 fusion.203
  282.4 1.6 bitcast_dynamic-update-slice_fusion.10
  287.8 1.8 exponential_convert_fusion.12
  291.0 2.1 fusion.203
  303.7 2.0 copy.15
  305.7 2.9 slice.94
  309.9 2.8 slice.95
  314.3 52.0 %reduce-scatter.2.cloned.1.call-done = f32[16,2,8,128]{3,2,1,0:T(8,128)} async-done(((f32[256,2,8,128]{3,2,1,0:T(8,128)}), f32[16,2,8,128]{3,2,1,0:T(8,128)}) %reduce-scatter.2.cloned.1.call-update) | async-done | bytes 131088 | tf_op jit(solution)/shard_map/reduce_scatter | solution.py:207
  367.3 3.8 fusion.84
  (359 shorter events, 171.5 us)
Async XLA Ops:
  7.2 1.5 copy-start.7
  7.2 359.2 %reduce-scatter.2.cloned.1.call-start = ((), (), s32[]{:S(2)}) async-start(), calls=%async_computation.1 | async-start | bytes 2228224 | tf_op jit(solution)/shard_map/reduce_scatter | solution.py:207
  8.7 1.5 copy-start
  17.0 1.0 copy-start.1
  17.0 10.5 %copy-start.13 = (s32[8]{0:T(128)S(1)}, s32[8]{0:T(128)}, u32[]{:S(2)}) copy-start(s32[8]{0:T(128)} %param.17) | copy-start | bytes 100
  19.5 72.6 %collective-permute-start = (bf16[8,512,128]{2,1,0:T(8,128)(2,1)}, bf16[8,512,128]{2,1,0:T(8,128)(2,1)}, u32[]{:S(2)}, u32[]{:S(2)}) collective-permute-start(bf16[8,512,128]{2,1,0:T(8,128)(2,1)} %pad_maximum_fusion.2), channel_id=1, source_target_pairs={{0,2},{2,4},{4,6},{6,8},{8,10},{10,12},{12,14},{14,16},{16,18},{18... | collective-permute-start | bytes 3145736 | tf_op jit(solution)/shard_map/ppermute | solution.py:19
  22.9 64.4 %collective-permute-start.1 = (bf16[8,512,128]{2,1,0:T(8,128)(2,1)}, bf16[8,512,128]{2,1,0:T(8,128)(2,1)}, u32[]{:S(2)}, u32[]{:S(2)}) collective-permute-start(bf16[8,512,128]{2,1,0:T(8,128)(2,1)} %param.13), channel_id=1, source_target_pairs={{0,2},{2,4},{4,6},{6,8},{8,10},{10,12},{12,14},{14,16},{16,18},{18... | collective-permute-start | bytes 3145736 | tf_op jit(solution)/shard_map/ppermute | solution.py:19
  30.9 5.5 %copy-start.3 = (bf16[8,512,64]{2,1,0:T(8,128)(2,1)S(1)}, bf16[8,512,64]{2,1,0:T(8,128)(2,1)}, u32[]{:S(2)}) copy-start(bf16[8,512,64]{2,1,0:T(8,128)(2,1)} %get-tuple-element.293) | copy-start | bytes 1572868
  30.9 5.4 %copy-start.4 = (bf16[8,512,64]{2,1,0:T(8,128)(2,1)S(1)}, bf16[8,512,64]{2,1,0:T(8,128)(2,1)}, u32[]{:S(2)}) copy-start(bf16[8,512,64]{2,1,0:T(8,128)(2,1)} %get-tuple-element.294) | copy-start | bytes 1572868
  34.8 2.9 copy-start.2
  39.0 3.0 copy-start.10
  92.1 3.2 copy-start.12
  95.3 83.1 %copy-start.11 = (f32[8,128]{1,0:T(8,128)S(1)}, f32[8,128]{1,0:T(8,128)}, u32[]{:S(2)}) copy-start(f32[8,128]{1,0:T(8,128)} %param.15) | copy-start | bytes 12292
  178.4 7.2 %copy-start.5 = (bf16[8,512,128]{2,1,0:T(8,128)(2,1)S(1)}, bf16[8,512,128]{2,1,0:T(8,128)(2,1)}, u32[]{:S(2)}) copy-start(bf16[8,512,128]{2,1,0:T(8,128)(2,1)} %param.14) | copy-start | bytes 3145732
  305.7 61.6 %copy-start.6 = (f32[8,512,128]{2,1,0:T(8,128)S(1)}, f32[8,512,128]{2,1,0:T(8,128)}, u32[]{:S(2)}) copy-start(f32[8,512,128]{2,1,0:T(8,128)} %get-tuple-element.188) | copy-start | bytes 6291460
  305.7 61.6 %copy-start.9 = (f32[8,16,128]{2,1,0:T(8,128)S(1)}, f32[8,16,128]{2,1,0:T(8,128)}, u32[]{:S(2)}) copy-start(f32[8,16,128]{2,1,0:T(8,128)} %get-tuple-element.189) | copy-start | bytes 196612
  308.6 58.7 %collective-permute-start.3 = (bf16[8,512,128]{2,1,0:T(8,128)(2,1)}, bf16[8,512,128]{2,1,0:T(8,128)(2,1)S(1)}, u32[]{:S(2)}, u32[]{:S(2)}) collective-permute-start(bf16[8,512,128]{2,1,0:T(8,128)(2,1)} %slice.94), channel_id=1, source_target_pairs={{2,0},{4,2},{6,4},{8,6},{10,8},{12,10},{14,12},{16,14},{18,16},{20... | collective-permute-start | bytes 3145736 | tf_op jit(solution)/shard_map/ppermute | solution.py:19
  312.7 54.6 %collective-permute-start.2 = (bf16[8,512,128]{2,1,0:T(8,128)(2,1)}, bf16[8,512,128]{2,1,0:T(8,128)(2,1)}, u32[]{:S(2)}, u32[]{:S(2)}) collective-permute-start(bf16[8,512,128]{2,1,0:T(8,128)(2,1)} %slice.95), channel_id=1, source_target_pairs={{2,0},{4,2},{6,4},{8,6},{10,8},{12,10},{14,12},{16,14},{18,16},{20... | collective-permute-start | bytes 3145736 | tf_op jit(solution)/shard_map/ppermute | solution.py:19
  367.3 3.8 copy-start.8
Sparse Core Ops, SparseCore 0:
  305.8 60.4 reduce-scatter.1
where the time goes:
time: 388 us; the launch traced here: 383 us
  matrix products  149 us (38%)
  local copies, waits for them, and re-layouts  58 us (15%)
  waiting for transfers between devices  52.1 us (13%)
  blocking collectives  49.4 us (13%)
  other arithmetic  48 us (12%)
  between operations  14.4 us (4%)
  starting transfers between devices  10.8 us (3%)
    reduce_scatter x1, waiting for transfers between devices, body(): lax.psum_scatter(jnp.stack([dk_part, dv_part], axis=1), 'ctx', scatter_di...  52 us
    dot_general x16, matrix products, near_scores(): jnp.einsum('id,jd->ij', q_h, k_h, preferred_element_type=f32) * scale  27.9 us
    dynamic_update_slice x24, local copies, waits for them, and re-layouts, body(): lax.map(forward_head, (q_rot, keys_pair, values_pair, pair_mask, q_sel, a...  26.3 us
    all_gather x1, blocking collectives, body(): lax.all_gather(v_sel, 'ctx', axis=1, tiled=True)  22.4 us
    all_gather x1, blocking collectives, body(): lax.all_gather(k_sel, 'ctx', axis=1, tiled=True)  22.1 us
    dot_general x16, matrix products, far_scores(): jnp.einsum('id,jd->ij', q1_h, k1_h, preferred_element_type=f32) * scale  21.5 us
    dot_general x8, matrix products, backward_head(): dq_near = jnp.dot(ds_near, k_h, preferred_element_type=f32) * scale  16.8 us
    dot_general x8, matrix products, backward_head(): dp_far = jnp.einsum('id,jd->ij', grad1_h, v1_h, preferred_element_type=f32)  12.7 us
  transfers between devices with their start and end apart: 5, of which 1 were waited for; matrix products, arithmetic and copies ran while one was open for 7% of the time, Pallas kernels for 0%

commit v1 on v0

v1 whole, which is shorter than its diff:
```python
import math

import jax
import jax.numpy as jnp
from jax import lax
from jax.experimental import pallas as pl
from jax.experimental.pallas import tpu as pltpu
from jax.sharding import PartitionSpec as P

HEADS = 16
SEL = 256
theta_base = 10000.0
eps_norm = 1e-06
NEG = -1e30
f32 = jnp.float32
bf16 = jnp.bfloat16


def dot_nn(a, b):
    return lax.dot_general(a, b, (((1,), (0,)), ((), ())), preferred_element_type=f32)


def dot_nt(a, b):
    return lax.dot_general(a, b, (((1,), (1,)), ((), ())), preferred_element_type=f32)


def dot_tn(a, b):
    return lax.dot_general(a, b, (((0,), (0,)), ((), ())), preferred_element_type=f32)


def lanes_of(shape):
    return lax.broadcasted_iota(jnp.int32, shape, len(shape) - 1)


def rows_of(shape):
    return lax.broadcasted_iota(jnp.int32, shape, len(shape) - 2)


def low_half(x):
    return jnp.where(lanes_of(x.shape) < 64, x, pltpu.roll(x, 64, 1))


def high_half(x):
    return jnp.where(lanes_of(x.shape) < 64, pltpu.roll(x, 64, 1), x)


def unpack_tables(cos_ref, sin_ref):
    c, s = cos_ref[...], sin_ref[...]
    cos = jnp.concatenate([low_half(c), high_half(c)], axis=0)
    sin = jnp.concatenate([low_half(s), high_half(s)], axis=0)
    sin = jnp.where(lanes_of(sin.shape) < 64, -sin, sin)
    return cos, sin


def rot(x, cos, sin):
    return x * cos + pltpu.roll(x, 64, 1) * sin


def spread(row):
    parts = []
    for i in range(row.shape[0]):
        parts.append(jnp.broadcast_to(row[i : i + 1, :], (128, 128)).T)
    return jnp.concatenate(parts, axis=0)


def compact(x):
    eye = rows_of((128, 128)) == lanes_of((128, 128))
    parts = []
    for i in range(x.shape[0] // 128):
        block = x[i * 128 : (i + 1) * 128, :]
        parts.append(jnp.sum(jnp.where(eye, block, 0.0), axis=0, keepdims=True))
    return jnp.concatenate(parts, axis=0)


def row_sum(x):
    return jnp.broadcast_to(jnp.sum(x, axis=1, keepdims=True), x.shape)


def prep_kernel(info, offs, q_ref, k_ref, v_ref, cos_ref, sin_ref, qr_ref, kr_ref, send_ref, rows_ref):
    g = pl.program_id(0)
    par = info[1]
    tok = q_ref.shape[1]
    nb = rows_ref.shape[2]
    rate = tok // nb
    cos, sin = unpack_tables(cos_ref, sin_ref)
    for hh in range(2):
        off = offs[2 * g + hh]
        hot = (lanes_of((nb, tok)) == off + rate * rows_of((nb, tok))).astype(bf16)
        qr = rot(q_ref[hh].astype(f32), cos, sin).astype(bf16)
        kr = rot(k_ref[hh].astype(f32), cos, sin).astype(bf16)
        qr_ref[hh] = qr
        kr_ref[hh] = kr
        rows_ref[0, hh] = dot_nn(hot, kr).astype(bf16)
        rows_ref[1, hh] = dot_nn(hot, v_ref[hh]).astype(bf16)
        rows_ref[2, hh] = dot_nn(hot, qr).astype(bf16)
    send_ref[0, 0] = kr_ref[par]
    send_ref[1, 0] = v_ref[par]


def own_kernel(start_ref, q_ref, k_ref, v_ref, e_ref, acc_ref, ml_ref, bias_ref):
    tok = q_ref.shape[1]
    half = tok // 2
    scale = 1.0 / math.sqrt(q_ref.shape[2])

    @pl.when(pl.program_id(0) == 0)
    def _():
        start = spread(start_ref[...])
        for c in range(tok // 128):
            key = lanes_of((tok, 128)) + c * 128
            ok = (key <= rows_of((tok, 128))) & (key.astype(f32) >= start)
            bias_ref[:, c * 128 : (c + 1) * 128] = jnp.where(ok, 0.0, NEG)

    vals = jnp.concatenate([v_ref[0], jnp.ones((tok, 128), bf16)], axis=1)
    for c in range(2):
        lo, n = c * half, (c + 1) * half
        z = dot_nt(q_ref[0, lo : lo + half, :], k_ref[0, :n, :]) * scale + bias_ref[lo : lo + half, :n]
        m = jnp.max(z, axis=1, keepdims=True)
        e = jnp.exp(z - m).astype(bf16)
        e_ref[0, lo : lo + half, :n] = e
        out = dot_nn(e, vals[:n])
        acc_ref[0, lo : lo + half, :] = out[:, :128]
        mb = jnp.broadcast_to(m, (half, 128))
        ml_ref[0, lo : lo + half, :] = jnp.where(lanes_of((half, 128)) < 64, mb, out[:, 128:])


def key_order(index, codes, nb, part, count):
    col = lanes_of((1, count)) + part * count
    slot = col // nb
    dev = jnp.full((1, count), index, jnp.int32)
    for b, code in enumerate(codes):
        dev = dev ^ (((slot >> b) & 1) * code)
    return dev * nb + col % nb


def make_join_kernel(codes):
    def join_kernel(
        info, offs, start_ref, q_ref, kv_ref, acc_ref, ml_ref, rows_ref, ga_ref, gb_ref, og_ref, gain_ref,
        e_ref, attn_ref, rr_ref, e1_ref, rs_ref, ar_ref, or_ref, stat_ref,
        bias_ref, start_s, m_s, l_s, acc_s, mp_s, sq_s, cr_s,
    ):
        g = pl.program_id(0)
        index, par, sel = info[0], info[1], info[2]
        tok = q_ref.shape[1]
        nb = rows_ref.shape[2]
        rate = tok // nb
        half = tok // 2
        count = ga_ref.shape[2]
        scale = 1.0 / math.sqrt(q_ref.shape[2])

        @pl.when(g == 0)
        def _():
            start = spread(start_ref[...])
            start_s[...] = start
            first = jnp.where(index == 0, float(tok), 0.0)
            for c in range(tok // 128):
                key = (lanes_of((tok, 128)) + c * 128).astype(f32)
                ok = (key - tok >= start) & (key >= first)
                bias_ref[:, c * 128 : (c + 1) * 128] = jnp.where(ok, 0.0, NEG)
            sq_s[...] = jnp.zeros_like(sq_s)
            cr_s[...] = jnp.zeros_like(cr_s)

        vals = jnp.concatenate([kv_ref[1, 0], jnp.ones((tok, 128), bf16)], axis=1)
        for c in range(2):
            lo = c * half
            z = dot_nt(q_ref[sel, lo : lo + half, :], kv_ref[0, 0]) * scale + bias_ref[lo : lo + half, :]
            m = jnp.max(z, axis=1, keepdims=True)
            e = jnp.exp(z - m).astype(bf16)
            e_ref[0, lo : lo + half, :] = e
            out = dot_nn(e, vals)
            acc_s[lo : lo + half, :] = out[:, :128]
            l_s[lo : lo + half, :] = out[:, 128:]
            mp_s[lo : lo + half, :] = jnp.broadcast_to(m, (half, 128))

        for hh in range(2):
            off = offs[2 * g + hh]
            rows = pl.ds(off, nb, stride=rate)
            here = sel == hh
            ml = ml_ref[hh]
            m_own = low_half(ml)
            l_own = high_half(ml)
            m_prev = jnp.where(here, mp_s[...], NEG)
            m = jnp.maximum(m_own, m_prev)
            a_own = jnp.exp(m_own - m)
            a_prev = jnp.where(here, jnp.exp(m_prev - m), 0.0)
            m_s[...] = m
            lsum = a_own * l_own + a_prev * l_s[...]
            total = a_own * acc_ref[hh] + a_prev * acc_s[...]

            q1 = rows_ref[2, hh]
            start1 = start_s[rows, :][:, :1]
            qb = index * nb + rows_of((nb, count))
            zs = []
            for part, ref in enumerate((ga_ref, gb_ref)):
                kb = key_order(index, codes, nb, part, count)
                pos = (off + rate * kb - index * tok).astype(f32)
                ok = (kb <= qb) & (pos >= start1)
                zs.append(jnp.where(ok, dot_nt(q1, ref[0, hh]) * scale, NEG))
            m1 = jnp.maximum(jnp.max(zs[0], axis=1, keepdims=True), jnp.max(zs[1], axis=1, keepdims=True))
            o1 = jnp.zeros((nb, 256), f32)
            for part, ref in enumerate((ga_ref, gb_ref)):
                e1 = jnp.exp(zs[part] - m1).astype(bf16)
                e1_ref[hh, :, part * count : (part + 1) * count] = e1
                v1 = jnp.concatenate([ref[1, hh], jnp.ones((count, 128), bf16)], axis=1)
                o1 = o1 + dot_nn(e1, v1)

            keep_l = l_s[...]
            keep_acc = acc_s[...]
            l_s[...] = lsum
            acc_s[...] = total
            mr = m_s[rows, :]
            lr = l_s[rows, :]
            ar = acc_s[rows, :]
            m1b = jnp.broadcast_to(m1, (nb, 128))
            mn = jnp.maximum(mr, m1b)
            b0 = jnp.exp(mr - mn)
            b1 = jnp.exp(m1b - mn)
            ln = b0 * lr + b1 * o1[:, 128:]
            inv1 = 1.0 / ln
            m_s[rows, :] = mn
            l_s[rows, :] = ln
            acc_s[rows, :] = b0 * ar + b1 * o1[:, :128]
            lse1 = mn + jnp.log(ln)
            rs_ref[hh] = jnp.where(lanes_of((nb, 128)) < 64, lse1, b1 * inv1)

            m = m_s[...]
            inv = 1.0 / l_s[...]
            attn = (acc_s[...] * inv).astype(bf16)
            attn_ref[hh] = attn
            r_own = jnp.exp(m_own - m) * inv
            r_prev = jnp.where(here, jnp.exp(m_prev - m) * inv, 0.0)
            rr_ref[hh] = jnp.where(lanes_of((tok, 128)) < 64, r_own, r_prev)
            af = attn.astype(f32)
            gd = og_ref[hh].astype(f32) * gain_ref[hh]
            sq_s[...] += af * af
            cr_s[...] += gd * af
            hot = (lanes_of((nb, tok)) == off + rate * rows_of((nb, tok))).astype(bf16)
            ar_ref[hh] = dot_nn(hot, attn).astype(bf16)
            or_ref[hh] = dot_nn(hot, og_ref[hh]).astype(bf16)
            l_s[...] = keep_l
            acc_s[...] = keep_acc

        @pl.when(g == pl.num_programs(0) - 1)
        def _():
            stat_ref[...] = jnp.concatenate([compact(row_sum(sq_s[...])), compact(row_sum(cr_s[...]))], axis=0)

    return join_kernel


def norm_terms(stat_ref, other_ref, feats):
    total = stat_ref[...] + other_ref[...]
    n = total.shape[0] // 2
    rinv = lax.rsqrt(total[:n] / feats + eps_norm)
    return rinv, rinv * rinv * total[n:] / feats


def split3(x):
    hi = x.astype(bf16).astype(f32)
    mid = (x - hi).astype(bf16).astype(f32)
    return hi, mid, x - hi - mid


def make_rows_kernel(feats):
    def rows_kernel(offs, stat_ref, other_ref, ar_ref, or_ref, gain_ref, rs_ref, out_ref, rinv_s, cc_s):
        nb = ar_ref.shape[1]
        rate = rinv_s.shape[0] // nb
        rinv, cc = norm_terms(stat_ref, other_ref, feats)
        rinv_s[...] = spread(rinv)
        cc_s[...] = spread(cc)
        for h in range(ar_ref.shape[0]):
            rows = pl.ds(offs[h], nb, stride=rate)
            ri = rinv_s[rows, :]
            cr = cc_s[rows, :]
            af = ar_ref[h].astype(f32)
            gd = or_ref[h].astype(f32) * gain_ref[h]
            ag = (ri * (gd - af * cr)).astype(bf16)
            delta = row_sum(ag.astype(f32) * af)
            out_ref[0, h] = ag
            lane = lanes_of((nb, 128))
            pack = jnp.zeros((nb, 128), f32)
            for i, x in enumerate(split3(low_half(rs_ref[h])) + split3(delta)):
                pack = jnp.where(lane == i, x, pack)
            out_ref[1, h] = pack.astype(bf16)

    return rows_kernel


def grad_terms(attn_ref, og_ref, gain_ref, rinv_s, cc_s):
    af = attn_ref[0].astype(f32)
    gd = og_ref[0].astype(f32) * gain_ref[0]
    rinv = rinv_s[...]
    ag = (rinv * (gd - af * cc_s[...])).astype(bf16).astype(f32)
    delta = row_sum(ag * af)
    return af, rinv, ag, delta


def make_back_prev_kernel(feats):
    def back_prev_kernel(
        info, stat_ref, other_ref, q_ref, attn_ref, og_ref, gain_ref, rr_ref, kv_ref, e_ref,
        back_ref, dq_ref, rinv_s, cc_s,
    ):
        tok = q_ref.shape[1]
        half = tok // 2
        scale = 1.0 / math.sqrt(q_ref.shape[2])

        @pl.when(pl.program_id(0) == 0)
        def _():
            rinv, cc = norm_terms(stat_ref, other_ref, feats)
            rinv_s[...] = spread(rinv)
            cc_s[...] = spread(cc)

        af, rinv, ag, delta = grad_terms(attn_ref, og_ref, gain_ref, rinv_s, cc_s)
        r = high_half(rr_ref[0])
        do = (ag * r).astype(bf16)
        dl = delta * r
        dk = jnp.zeros((128, tok), f32)
        dv = jnp.zeros((128, tok), f32)
        for c in range(2):
            sl = slice(c * half, (c + 1) * half)
            e = e_ref[0, sl, :]
            dp = dot_nt(do[sl], kv_ref[1, 0])
            ds = (e.astype(f32) * (dp - jnp.concatenate([dl[sl]] * (tok // 128), axis=1))).astype(bf16)
            dq_ref[0, sl, :] = dot_nn(ds, kv_ref[0, 0])
            dk = dk + dot_tn(q_ref[0, sl, :], ds)
            dv = dv + dot_tn(do[sl], e)
        back_ref[0, 0] = (dk * scale).T.astype(bf16)
        back_ref[1, 0] = dv.T.astype(bf16)

    return back_prev_kernel


def make_back_own_kernel(feats):
    def back_own_kernel(
        info, offs, stat_ref, other_ref, q_ref, k_ref, v_ref, attn_ref, og_ref, gain_ref, rr_ref, e_ref,
        dqp_ref, e1_ref, rs_ref, ga_ref, gb_ref, cos_ref, sin_ref,
        normed_ref, gq_ref, dk_ref, dv_ref, rinv_s, cc_s, ag_s, de_s, dq_s,
    ):
        h = pl.program_id(0)
        sel = info[2]
        tok = q_ref.shape[1]
        nb = e1_ref.shape[1]
        rate = tok // nb
        count = ga_ref.shape[2]
        half = tok // 2
        scale = 1.0 / math.sqrt(q_ref.shape[2])

        @pl.when(h == 0)
        def _():
            rinv, cc = norm_terms(stat_ref, other_ref, feats)
            rinv_s[...] = spread(rinv)
            cc_s[...] = spread(cc)

        af, rinv, ag, delta = grad_terms(attn_ref, og_ref, gain_ref, rinv_s, cc_s)
        normed_ref[0] = (af * rinv * gain_ref[0]).astype(bf16)
        ag_s[...] = ag
        de_s[...] = delta
        r = low_half(rr_ref[0])
        do = (ag * r).astype(bf16)
        dl = delta * r
        here = jnp.where(h % 2 == sel, 1.0, 0.0)
        dks = []
        for c in range(2):
            lo, n = c * half, (c + 1) * half
            sl = slice(lo, n)
            e = e_ref[0, sl, :n]
            dp = dot_nt(do[sl], v_ref[0, :n, :])
            ds = (e.astype(f32) * (dp - jnp.concatenate([dl[sl]] * (n // 128), axis=1))).astype(bf16)
            dq_s[sl, :] = dot_nn(ds, k_ref[0, :n, :]) + dqp_ref[0, sl, :] * here
            dks.append((dot_tn(q_ref[0, sl, :], ds), dot_tn(do[sl], e)))
        for i, ref in enumerate((dk_ref, dv_ref)):
            ref[0, :half, :] = (dks[0][i] + dks[1][i][:, :half]).T
            ref[0, half:, :] = dks[1][i][:, half:].T

        rows = pl.ds(offs[h], nb, stride=rate)
        r1 = high_half(rs_ref[0])
        g1 = (ag_s[rows, :] * r1).astype(bf16)
        d1 = (de_s[rows, :] * r1)[:, :1]
        dq1 = jnp.zeros((nb, 128), f32)
        for part, ref in enumerate((ga_ref, gb_ref)):
            dp1 = dot_nt(g1, ref[1, 0])
            ds1 = (e1_ref[0, :, part * count : (part + 1) * count].astype(f32) * (dp1 - d1)).astype(bf16)
            dq1 = dq1 + dot_nn(ds1, ref[0, 0])
        dq_s[rows, :] += dq1
        cos, sin = unpack_tables(cos_ref, sin_ref)
        gq_ref[0] = rot(dq_s[...] * scale, cos, -sin).astype(bf16)

    return back_own_kernel


def make_final_kernel(codes):
    def final_kernel(
        info, offs, start_ref, dk_ref, dv_ref, back_ref, rows_ref, ga_ref, gb_ref, sa_ref, sb_ref, cos_ref, sin_ref,
        gk_ref, gv_ref, dk_s, dv_s,
    ):
        h = pl.program_id(0)
        index, par = info[0], info[1]
        tok = dk_ref.shape[1]
        nb = rows_ref.shape[2]
        rate = tok // nb
        count = ga_ref.shape[2]
        scale = 1.0 / math.sqrt(dk_ref.shape[2])
        off = offs[h]
        here = (h % 2 == par) & (index < info[3] - 1)
        back = jnp.where(here, back_ref[0, 0].astype(f32), 0.0)
        dk_s[...] = dk_ref[0] * scale + back
        dv_s[...] = dv_ref[0] + jnp.where(here, back_ref[1, 0].astype(f32), 0.0)

        k1 = rows_ref[0, 0]
        v1 = rows_ref[1, 0]
        kb = index * nb + rows_of((nb, count))
        kpos = off + rate * kb
        pick = (rows_of((16, 128)) == lanes_of((16, 128))).astype(bf16)
        dk1 = jnp.zeros((nb, 128), f32)
        dv1 = jnp.zeros((nb, 128), f32)
        for part, (g, s) in enumerate(((ga_ref, sa_ref), (gb_ref, sb_ref))):
            qb = key_order(index, codes, nb, part, count)
            start = start_ref[0, part : part + 1, :]
            st = dot_nt(pick, s[1, 0])
            lse = st[0:1] + st[1:2] + st[2:3]
            delta = st[3:4] + st[4:5] + st[5:6]
            ok = (kb <= qb) & (kpos >= start)
            z = jnp.where(ok, dot_nt(k1, g[0, 0]) * scale - lse, NEG)
            p = jnp.exp(z).astype(bf16)
            dp = dot_nt(v1, s[0, 0])
            ds = (p.astype(f32) * (dp - delta)).astype(bf16)
            dk1 = dk1 + dot_nn(ds, g[0, 0])
            dv1 = dv1 + dot_nn(p, s[0, 0])
        rows = pl.ds(off, nb, stride=rate)
        dk_s[rows, :] += dk1 * scale
        dv_s[rows, :] += dv1
        cos, sin = unpack_tables(cos_ref, sin_ref)
        gk_ref[0] = rot(dk_s[...], cos, -sin).astype(bf16)
        gv_ref[0] = dv_s[...].astype(bf16)

    return final_kernel


def call(kernel, prefetch, grid, ins, outs, scratch=()):
    arrays = [a for a, _, _ in ins]
    in_specs = [pl.BlockSpec(b, m) for _, b, m in ins]
    return pl.pallas_call(
        kernel,
        out_shape=[jax.ShapeDtypeStruct(s, d) for s, d, _, _ in outs],
        grid_spec=pltpu.PrefetchScalarGridSpec(
            num_scalar_prefetch=len(prefetch),
            grid=grid,
            in_specs=in_specs,
            out_specs=[pl.BlockSpec(b, m) for _, _, b, m in outs],
            scratch_shapes=list(scratch),
        ),
        compiler_params=pltpu.CompilerParams(
            dimension_semantics=("arbitrary",) * len(grid), vmem_limit_bytes=56 << 20
        ),
    )(*prefetch, *arrays)


def body(queries, keys, values, out_grad, norm_gain, doc_start, head_offsets):
    heads, tok, width = queries.shape
    ctx = lax.axis_size("ctx")
    rate = ctx * tok // SEL
    nb = tok // rate
    feats = float(HEADS * width)
    pairs = heads // 2
    index = lax.axis_index("ctx")
    base = index * tok
    codes = [1 << b for b in range(1, ctx.bit_length() - 1)] + [1]

    starts = lax.dynamic_slice_in_dim(doc_start, base, tok)
    position = base + jnp.arange(tok, dtype=jnp.int32)
    rel = (position - starts).astype(f32)
    freq = theta_base ** (-2.0 * jnp.arange(width // 2).astype(f32) / width)
    angle = jnp.concatenate([rel[: tok // 2, None] * freq[None, :], rel[tok // 2 :, None] * freq[None, :]], axis=1)
    cos, sin = jnp.cos(angle), jnp.sin(angle)
    start_rel = (starts - base).astype(f32).reshape(tok // 128, 128)
    info = jnp.stack([index, index % 2, (index + 1) % 2, jnp.int32(ctx)]).astype(jnp.int32)
    gain = norm_gain.reshape(heads, 1, width)

    sp = (tok // 128, 128)
    tab = (tok // 2, 128)
    pair3 = (2, tok, width)
    one3 = (1, tok, width)

    def const(n):
        return lambda i, *s: (0,) * n

    q_rot, k_rot, send, rows = call(
        prep_kernel, (info, head_offsets), (pairs,),
        [
            (queries, pair3, lambda g, *s: (g, 0, 0)),
            (keys, pair3, lambda g, *s: (g, 0, 0)),
            (values, pair3, lambda g, *s: (g, 0, 0)),
            (cos, tab, const(2)),
            (sin, tab, const(2)),
        ],
        [
            (queries.shape, bf16, pair3, lambda g, *s: (g, 0, 0)),
            (queries.shape, bf16, pair3, lambda g, *s: (g, 0, 0)),
            ((2, pairs, tok, width), bf16, (2, 1, tok, width), lambda g, *s: (0, g, 0, 0)),
            ((3, heads, nb, width), bf16, (3, 2, nb, width), lambda g, *s: (0, g, 0, 0)),
        ],
    )
    recv = lax.ppermute(send, "ctx", [(i, i + 1) for i in range(ctx - 1)])

    def exchange(x):
        for code in codes[:-1]:
            x = jnp.concatenate([x, lax.ppermute(x, "ctx", [(i, i ^ code) for i in range(ctx)])], axis=2)
        return x, lax.ppermute(x, "ctx", [(i, i ^ codes[-1]) for i in range(ctx)])

    ga, gb = exchange(rows)
    half_count = SEL // 2

    e_own, acc_own, ml_own = call(
        own_kernel, (), (heads,),
        [
            (start_rel, sp, const(2)),
            (q_rot, one3, lambda h, *s: (h, 0, 0)),
            (k_rot, one3, lambda h, *s: (h, 0, 0)),
            (values, one3, lambda h, *s: (h, 0, 0)),
        ],
        [
            ((heads, tok, tok), bf16, (1, tok, tok), lambda h, *s: (h, 0, 0)),
            (queries.shape, f32, one3, lambda h, *s: (h, 0, 0)),
            (queries.shape, f32, one3, lambda h, *s: (h, 0, 0)),
        ],
        [pltpu.VMEM((tok, tok), f32)],
    )

    g4 = lambda g, *s: (0, g, 0, 0)
    gp = lambda g, *s: (g, 0, 0)
    e_prev, attn, rr, e1, rs, attn_rows, og_rows, stat = call(
        make_join_kernel(codes), (info, head_offsets), (pairs,),
        [
            (start_rel, sp, const(2)),
            (q_rot, pair3, gp),
            (recv, (2, 1, tok, width), g4),
            (acc_own, pair3, gp),
            (ml_own, pair3, gp),
            (rows, (3, 2, nb, width), g4),
            (ga, (3, 2, half_count, width), g4),
            (gb, (3, 2, half_count, width), g4),
            (out_grad, pair3, gp),
            (gain, (2, 1, width), gp),
        ],
        [
            ((pairs, tok, tok), bf16, (1, tok, tok), gp),
            (queries.shape, bf16, pair3, gp),
            (queries.shape, f32, pair3, gp),
            ((heads, nb, SEL), bf16, (2, nb, SEL), gp),
            ((heads, nb, width), f32, (2, nb, width), gp),
            ((heads, nb, width), bf16, (2, nb, width), gp),
            ((heads, nb, width), bf16, (2, nb, width), gp),
            ((2 * tok // 128, 128), f32, (2 * tok // 128, 128), const(2)),
        ],
        [pltpu.VMEM((tok, tok), f32)] + [pltpu.VMEM((tok, 128), f32)] * 7,
    )
    other = lax.ppermute(stat, "head", [(0, 1), (1, 0)])

    whole = lambda a: (a, a.shape, const(a.ndim))
    (grad_rows,) = call(
        make_rows_kernel(feats), (head_offsets,), (1,),
        [whole(stat), whole(other), whole(attn_rows), whole(og_rows), whole(gain), whole(rs)],
        [((2, heads, nb, width), bf16, (2, heads, nb, width), const(4))],
        [pltpu.VMEM((tok, 128), f32)] * 2,
    )
    sa, sb = exchange(grad_rows)

    gsel = lambda g, s, *_: (2 * g + s[2], 0, 0)
    back, dq_prev = call(
        make_back_prev_kernel(feats), (info,), (pairs,),
        [
            whole(stat), whole(other),
            (q_rot, one3, gsel),
            (attn, one3, gsel),
            (out_grad, one3, gsel),
            (gain, (1, 1, width), gsel),
            (rr, one3, gsel),
            (recv, (2, 1, tok, width), g4),
            (e_prev, (1, tok, tok), gp),
        ],
        [
            ((2, pairs, tok, width), bf16, (2, 1, tok, width), g4),
            ((pairs, tok, width), f32, one3, gp),
        ],
        [pltpu.VMEM((tok, 128), f32)] * 2,
    )
    back = lax.ppermute(back, "ctx", [(i + 1, i) for i in range(ctx - 1)])

    hp = lambda h, *s: (h, 0, 0)
    hg = lambda h, *s: (0, h, 0, 0)
    normed, grad_queries, dk_own, dv_own = call(
        make_back_own_kernel(feats), (info, head_offsets), (heads,),
        [
            whole(stat), whole(other),
            (q_rot, one3, hp),
            (k_rot, one3, hp),
            (values, one3, hp),
            (attn, one3, hp),
            (out_grad, one3, hp),
            (gain, (1, 1, width), hp),
            (rr, one3, hp),
            (e_own, (1, tok, tok), hp),
            (dq_prev, one3, lambda h, *s: (h // 2, 0, 0)),
            (e1, (1, nb, SEL), hp),
            (rs, (1, nb, width), hp),
            (ga, (2, 1, half_count, width), hg),
            (gb, (2, 1, half_count, width), hg),
            whole(cos), whole(sin),
        ],
        [
            (queries.shape, bf16, one3, hp),
            (queries.shape, bf16, one3, hp),
            (queries.shape, f32, one3, hp),
            (queries.shape, f32, one3, hp),
        ],
        [pltpu.VMEM((tok, 128), f32)] * 5,
    )

    slot = jnp.arange(ctx, dtype=jnp.int32)
    dev = jnp.full((ctx,), index, jnp.int32)
    for b, code in enumerate(codes):
        dev = dev ^ (((slot >> b) & 1) * code)
    qb = (dev[:, None] * nb + jnp.arange(nb, dtype=jnp.int32)[None, :]).reshape(-1)
    query_pos = head_offsets[:, None] + rate * qb[None, :]
    query_start = jnp.take(doc_start, query_pos).reshape(heads, 2, half_count)

    grad_keys, grad_values = call(
        make_final_kernel(codes), (info, head_offsets), (heads,),
        [
            (query_start, (1, 2, half_count), hp),
            (dk_own, one3, hp),
            (dv_own, one3, hp),
            (back, (2, 1, tok, width), lambda h, *s: (0, h // 2, 0, 0)),
            (rows, (2, 1, nb, width), hg),
            (ga, (1, 1, half_count, width), lambda h, *s: (2, h, 0, 0)),
            (gb, (1, 1, half_count, width), lambda h, *s: (2, h, 0, 0)),
            (sa, (2, 1, half_count, width), hg),
            (sb, (2, 1, half_count, width), hg),
            whole(cos), whole(sin),
        ],
        [
            (queries.shape, bf16, one3, hp),
            (queries.shape, bf16, one3, hp),
        ],
        [pltpu.VMEM((tok, 128), f32)] * 2,
    )
    return (normed, grad_queries, grad_keys, grad_values)


def solution(mesh):
    return jax.shard_map(
        body,
        mesh=mesh,
        in_specs=(
            P("head", "ctx", None),
            P("head", "ctx", None),
            P("head", "ctx", None),
            P("head", "ctx", None),
            P("head", None),
            P(),
            P("head"),
        ),
        out_specs=(
            P("head", "ctx", None),
            P("head", "ctx", None),
            P("head", "ctx", None),
            P("head", "ctx", None),
        ),
        check_vma=False,
    )
```

time: 388 us -> 142 us (0.37); the launches traced: 383 us -> 141 us
  matrix products: 149 us -> 0 us
  Pallas kernels: 0 us -> 60.8 us
  blocking collectives: 49.4 us -> 0 us
  local copies, waits for them, and re-layouts: 58 us -> 16.1 us
  other arithmetic: 48 us -> 6.93 us
  between operations: 14.4 us -> 0.9 us
  waiting for transfers between devices: 52.1 us -> 40.3 us
  starting transfers between devices: 10.8 us -> 16 us
    dot_general x102 -> x0, matrix products: 149 us -> none  [the longest x16 27.9 us: near_scores(): jnp.einsum('id,jd->ij', q_h, k_h, preferred_element_type=f32) * scale]
    pallas_call x0 -> x7, Pallas kernels: none -> 60.8 us  [call(): pl.pallas_call(kernel, out_shape=[jax.ShapeDtypeStruct(s, d) for s, d, _,...]
    reduce_scatter x1 -> x0, waiting for transfers between devices: 52 us -> none  [body(): lax.psum_scatter(jnp.stack([dk_part, dv_part], axis=1), 'ctx', scatter_di...]
    all_gather x2 -> x0, blocking collectives: 44.5 us -> none  [the longest x1 22.4 us: body(): lax.all_gather(v_sel, 'ctx', axis=1, tiled=True)]
    ppermute x4 -> x11, waiting for transfers between devices: 0.01 us -> 40.3 us  [the longest x6 37 us: exchange(): lax.ppermute(x, 'ctx', [(i, i ^ code) for i in range(ctx)])]
    dynamic_update_slice x24 -> x0, local copies, waits for them, and re-layouts: 26.3 us -> none  [body(): lax.map(forward_head, (q_rot, keys_pair, values_pair, pair_mask, q_sel, a...]
    reduce_sum x27 -> x0, other arithmetic: 11.7 us -> none  [the longest x8 3.8 us: forward_head(): lse_near = jax.nn.logsumexp(z_near, axis=1)]
    gather x2 -> x1, local copies, waits for them, and re-layouts: 1.23 us -> 11.8 us  [body(): query_start = jnp.take(doc_start, query_pos).reshape(heads, 2, half_count)]
  transfers between devices with their start and end apart: 5 -> 11, of which waited for: 1 -> 6; matrix products, arithmetic and copies ran while one was open for 7% -> 10% of each run, Pallas kernels for 0% -> 23%
where the time goes in v1:
time: 142 us; the launch traced here: 141 us
  Pallas kernels  60.8 us (43%)
  waiting for transfers between devices  40.3 us (28%)
  local copies, waits for them, and re-layouts  16.1 us (11%)
  starting transfers between devices  16 us (11%)
  other arithmetic  6.93 us (5%)
    pallas_call x7, Pallas kernels, call(): pl.pallas_call(kernel, out_shape=[jax.ShapeDtypeStruct(s, d) for s, d, _,...  60.8 us
    ppermute x6, waiting for transfers between devices, exchange(): lax.ppermute(x, 'ctx', [(i, i ^ code) for i in range(ctx)])  37 us
    ppermute x6, starting transfers between devices, exchange(): lax.ppermute(x, 'ctx', [(i, i ^ code) for i in range(ctx)])  12.6 us
    gather x1, local copies, waits for them, and re-layouts, body(): query_start = jnp.take(doc_start, query_pos).reshape(heads, 2, half_count)  11.8 us
    unnamed x24, local copies, waits for them, and re-layouts  3.91 us
    ppermute x1, waiting for transfers between devices, body(): other = lax.ppermute(stat, 'head', [(0, 1), (1, 0)])  3.29 us
  transfers between devices with their start and end apart: 11, of which 6 were waited for; matrix products, arithmetic and copies ran while one was open for 10% of the time, Pallas kernels for 23%

profile of v1, /device:TPU:0, one launch (start us, length us, event | category | flops | bytes accessed | tf_op | source)
XLA Modules:
  0.0 141.0 jit_solution(1459034383094193660)
XLA Ops:
  0.7 1.3 subtract_convert_fusion
  2.0 0.1 broadcast_multiply_fusion.1
  2.1 1.3 fusion
  3.4 0.6 pad_add_fusion.info
  4.0 5.6 %shard_map.102 = (bf16[8,512,128]{2,1,0:T(8,128)(2,1)}, bf16[8,512,128]{2,1,0:T(8,128)(2,1)}, bf16[2,4,512,128]{3,2,1,0:T(8,128)(2,1)}, bf16[3,8,16,128]{3,2,1,0:T(8,128)(2,1)}) custom-call(s32[4]{0:T(128)} %pad_add_fusion.info, s32[8]{0:T(128)} %offs.9, bf16[8,512,128]{2,1,0:T(8,128)(2,1)} %q_ref.1, bf16[8,512,128]{2,1,0:T(8,128)(2,1)} %k_ref.1, ...), custom_call_target="tpu_custom_call" | custom-call | tf_op jit(solution)/shard_map/pallas_call | solution.py:440
  9.6 3.0 %collective-permute-start.1 = (bf16[3,8,16,128]{3,2,1,0:T(8,128)(2,1)}, bf16[3,8,16,128]{3,2,1,0:T(8,128)(2,1)S(1)}, u32[]{:S(2)}, u32[]{:S(2)}) collective-permute-start(bf16[3,8,16,128]{3,2,1,0:T(8,128)(2,1)} %get-tuple-element.32.rows_ref), channel_id=1, source_target_pairs={{0,4},{2,6},{4,0},{6,2},{8,12},{10,14},{12,8},{14,10},{16,20},{18,... | collective-permute-start | bytes 294920 | tf_op jit(solution)/shard_map/ppermute | solution.py:505
  12.6 3.0 %collective-permute-done.1 = bf16[3,8,16,128]{3,2,1,0:T(8,128)(2,1)S(1)} collective-permute-done((bf16[3,8,16,128]{3,2,1,0:T(8,128)(2,1)}, bf16[3,8,16,128]{3,2,1,0:T(8,128)(2,1)S(1)}, u32[]{:S(2)}, u32[]{:S(2)}) %collective-permute-start.1) | collective-permute-done | bytes 98336 | tf_op jit(solution)/shard_map/ppermute | solution.py:505
  15.6 0.9 pad_maximum_fusion.3
  16.5 1.9 %collective-permute-start.2 = (bf16[3,8,32,128]{3,2,1,0:T(8,128)(2,1)S(1)}, bf16[3,8,32,128]{3,2,1,0:T(8,128)(2,1)S(1)}, u32[]{:S(2)}, u32[]{:S(2)}) collective-permute-start(bf16[3,8,32,128]{3,2,1,0:T(8,128)(2,1)S(1)} %pad_maximum_fusion.3), channel_id=1, source_target_pairs={{0,8},{2,10},{4,12},{6,14},{8,0},{10,2},{12,4},{14,6},{16,24},{18,... | collective-permute-start | bytes 589832 | tf_op jit(solution)/shard_map/ppermute | solution.py:505
  18.5 4.2 %collective-permute-done.2 = bf16[3,8,32,128]{3,2,1,0:T(8,128)(2,1)S(1)} collective-permute-done((bf16[3,8,32,128]{3,2,1,0:T(8,128)(2,1)S(1)}, bf16[3,8,32,128]{3,2,1,0:T(8,128)(2,1)S(1)}, u32[]{:S(2)}, u32[]{:S(2)}) %collective-permute-start.2) | collective-permute-done | bytes 196640 | tf_op jit(solution)/shard_map/ppermute | solution.py:505
  22.7 0.9 pad_maximum_fusion.1
  23.6 2.6 %collective-permute-start.3 = (bf16[3,8,64,128]{3,2,1,0:T(8,128)(2,1)S(1)}, bf16[3,8,64,128]{3,2,1,0:T(8,128)(2,1)S(1)}, u32[]{:S(2)}, u32[]{:S(2)}) collective-permute-start(bf16[3,8,64,128]{3,2,1,0:T(8,128)(2,1)S(1)} %pad_maximum_fusion.1), channel_id=1, source_target_pairs={{0,16},{2,18},{4,20},{6,22},{8,24},{10,26},{12,28},{14,30},{16,0},... | collective-permute-start | bytes 1179656 | tf_op jit(solution)/shard_map/ppermute | solution.py:505
  26.1 1.3 collective-permute-start
  27.5 0.9 constant_dynamic-update-slice_fusion.3
  28.5 13.9 %collective-permute-done.3 = bf16[3,8,64,128]{3,2,1,0:T(8,128)(2,1)S(1)} collective-permute-done((bf16[3,8,64,128]{3,2,1,0:T(8,128)(2,1)S(1)}, bf16[3,8,64,128]{3,2,1,0:T(8,128)(2,1)S(1)}, u32[]{:S(2)}, u32[]{:S(2)}) %collective-permute-start.3) | collective-permute-done | bytes 393248 | tf_op jit(solution)/shard_map/ppermute | solution.py:505
  42.4 0.1 constant_dynamic-update-slice_fusion.ga_ref
  42.5 0.1 collective-permute-start.4
  42.5 9.9 %shard_map.103 = (bf16[8,512,512]{2,1,0:T(8,128)(2,1)}, f32[8,512,128]{2,1,0:T(8,128)}, f32[8,512,128]{2,1,0:T(8,128)}) custom-call(f32[4,128]{1,0:T(4,128)} %get-tuple-element.53.start_ref, bf16[8,512,128]{2,1,0:T(8,128)(2,1)} %get-tuple-element.27.q_ref, bf16[8,512,128]{2,1,0:T(8,128)(2,1)} %get-tuple-element.29.k_ref, bf16[8,512,128]{2,1,0:T(8,128)(2,1)} %v_ref.5), custom_call_target="tpu_custom_call" | custom-call | tf_op jit(solution)/shard_map/pallas_call | solution.py:440
  52.5 0.0 collective-permute-done.4.gb_ref
  52.5 0.9 copy-done.3
  53.5 0.3 copy-done.2
  53.7 11.3 %shard_map.104 = (bf16[4,512,512]{2,1,0:T(8,128)(2,1)}, bf16[8,512,128]{2,1,0:T(8,128)(2,1)}, f32[8,512,128]{2,1,0:T(8,128)}, bf16[8,16,256]{2,1,0:T(8,128)(2,1)...) custom-call(s32[4]{0:T(128)} %pad_add_fusion.info, ...), custom_call_target="tpu_custom_call" | custom-call | tf_op jit(solution)/shard_map/pallas_call | solution.py:440
  65.1 0.6 collective-permute-start.5
  65.7 3.3 %collective-permute-done.5.other_ref = f32[8,128]{1,0:T(8,128)S(1)} collective-permute-done((f32[8,128]{1,0:T(8,128)}, f32[8,128]{1,0:T(8,128)S(1)}, u32[]{:S(2)}, u32[]{:S(2)}) %collective-permute-start.5) | collective-permute-done | bytes 4128 | tf_op jit(solution)/shard_map/ppermute | solution.py:555
  69.0 0.6 copy-done.8
  69.5 2.7 %shard_map.107 = bf16[2,8,16,128]{3,2,1,0:T(8,128)(2,1)} custom-call(s32[8]{0:T(128)} %offs.9, f32[8,128]{1,0:T(8,128)} %get-tuple-element.33.stat_ref, f32[8,128]{1,0:T(8,128)} %copy-done.8, bf16[8,16,128]{2,1,0:T(8,128)(2,1)} %get-tuple-element.46.ar_ref, bf16[8,16,128]{2,1,0:T(8,128)(2,1)} %get-tuple-element.47.or_ref, f32[8,1,128]{2,1,0:T(1,128)} %bitcast.12, ...), custom_call_target="tpu_custom_call" | custom-call | tf_op jit(solution)/shard_map/pallas_call | solution.py:440
  72.3 0.6 collective-permute-start.7
  72.8 3.9 %collective-permute-done.7 = bf16[2,8,16,128]{3,2,1,0:T(8,128)(2,1)S(1)} collective-permute-done((bf16[2,8,16,128]{3,2,1,0:T(8,128)(2,1)}, bf16[2,8,16,128]{3,2,1,0:T(8,128)(2,1)S(1)}, u32[]{:S(2)}, u32[]{:S(2)}) %collective-permute-start.7) | collective-permute-done | bytes 65568 | tf_op jit(solution)/shard_map/ppermute | solution.py:505
  76.7 0.8 pad_maximum_fusion.5
  77.6 0.1 collective-permute-start.8
  77.7 0.1 add_multiply_fusion
  77.7 0.1 mul.110
  77.8 7.7 %shard_map.105 = (bf16[2,4,512,128]{3,2,1,0:T(8,128)(2,1)}, f32[4,512,128]{2,1,0:T(8,128)}) custom-call(s32[4]{0:T(128)} %pad_add_fusion.info, f32[8,128]{1,0:T(8,128)} %get-tuple-element.33.stat_ref, f32[8,128]{1,0:T(8,128)} %copy-done.8, bf16[8,512,128]{2,1,0:T(8,128)(2,1)} %get-tuple-element.27.q_ref, bf16[8,512,128]{2,1,0:T(8,128)(2,1)} %get-tuple-element.34.attn_ref, ...), custom_call_target="tpu_custom_call" | custom-call | tf_op jit(solution)/shard_map/pallas_call | solution.py:440
  85.5 1.3 collective-permute-start.6
  86.8 0.0 collective-permute-done.8
  86.9 4.5 %collective-permute-start.9 = (bf16[2,8,64,128]{3,2,1,0:T(8,128)(2,1)S(1)}, bf16[2,8,64,128]{3,2,1,0:T(8,128)(2,1)S(1)}, u32[]{:S(2)}, u32[]{:S(2)}) collective-permute-start(bf16[2,8,64,128]{3,2,1,0:T(8,128)(2,1)S(1)} %pad_maximum_fusion.2), channel_id=1, source_target_pairs={{0,16},{2,18},{4,20},{6,22},{8,24},{10,26},{12,28},{14,30},{16,0},... | collective-permute-start | bytes 786440 | tf_op jit(solution)/shard_map/ppermute | solution.py:505
  91.3 0.1 fusion.2
  91.4 11.8 %gather_fusion = s32[2048]{0:T(1024)S(1)} fusion(s32[8192]{0:T(1024)S(1)} %copy-done, s32[2048]{0:T(1024)S(1)} %broadcast_clamp_fusion), kind=kCustom, calls=%fused_computation | custom fusion | bytes 24576 | tf_op jit(solution)/shard_map/jit(_take)/gather | solution.py:623
  103.2 11.9 %collective-permute-done.9 = bf16[2,8,64,128]{3,2,1,0:T(8,128)(2,1)S(1)} collective-permute-done((bf16[2,8,64,128]{3,2,1,0:T(8,128)(2,1)S(1)}, bf16[2,8,64,128]{3,2,1,0:T(8,128)(2,1)S(1)}, u32[]{:S(2)}, u32[]{:S(2)}) %collective-permute-start.9) | collective-permute-done | bytes 262176 | tf_op jit(solution)/shard_map/ppermute | solution.py:505
  115.2 0.1 collective-permute-start.10
  115.3 0.1 add.108
  115.4 0.1 add.109
  115.5 0.1 add.111
  115.5 0.7 and_select_fusion.start_ref
  116.2 14.6 %shard_map.106 = (bf16[8,512,128]{2,1,0:T(8,128)(2,1)}, bf16[8,512,128]{2,1,0:T(8,128)(2,1)}, f32[8,512,128]{2,1,0:T(8,128)}, f32[8,512,128]{2,1,0:T(8,128)}) custom-call(s32[4]{0:T(128)} %pad_add_fusion.info, s32[8]{0:T(128)} %offs.9, f32[8,128]{1,0:T(8,128)} %get-tuple-element.33.stat_ref, f32[8,128]{1,0:T(8,128)} %copy-done.8, ...), custom_call_target="tpu_custom_call" | custom-call | tf_op jit(solution)/shard_map/pallas_call | solution.py:440
  130.9 0.9 copy-done.7
  131.7 0.3 copy-done.5
  132.0 9.0 %shard_map.108 = (bf16[8,512,128]{2,1,0:T(8,128)(2,1)}, bf16[8,512,128]{2,1,0:T(8,128)(2,1)}) custom-call(s32[4]{0:T(128)} %pad_add_fusion.info, s32[8]{0:T(128)} %offs.9, s32[8,2,128]{2,1,0:T(2,128)} %and_select_fusion.start_ref, f32[8,512,128]{2,1,0:T(8,128)} %get-tuple-element.43.dk_ref, f32[8,512,128]{2,1,0:T(8,128)} %get-tuple-element.44.dv_ref, ...), custom_call_target="tpu_custom_call" | custom-call | tf_op jit(solution)/shard_map/pallas_call | solution.py:440
  (30 shorter events, 0.2 us)
Async XLA Ops:
  9.6 6.0 %collective-permute-start.1 = (bf16[3,8,16,128]{3,2,1,0:T(8,128)(2,1)}, bf16[3,8,16,128]{3,2,1,0:T(8,128)(2,1)S(1)}, u32[]{:S(2)}, u32[]{:S(2)}) collective-permute-start(bf16[3,8,16,128]{3,2,1,0:T(8,128)(2,1)} %get-tuple-element.32.rows_ref), channel_id=1, source_target_pairs={{0,4},{2,6},{4,0},{6,2},{8,12},{10,14},{12,8},{14,10},{16,20},{18,... | collective-permute-start | bytes 294920 | tf_op jit(solution)/shard_map/ppermute | solution.py:505
  16.5 6.1 %collective-permute-start.2 = (bf16[3,8,32,128]{3,2,1,0:T(8,128)(2,1)S(1)}, bf16[3,8,32,128]{3,2,1,0:T(8,128)(2,1)S(1)}, u32[]{:S(2)}, u32[]{:S(2)}) collective-permute-start(bf16[3,8,32,128]{3,2,1,0:T(8,128)(2,1)S(1)} %pad_maximum_fusion.3), channel_id=1, source_target_pairs={{0,8},{2,10},{4,12},{6,14},{8,0},{10,2},{12,4},{14,6},{16,24},{18,... | collective-permute-start | bytes 589832 | tf_op jit(solution)/shard_map/ppermute | solution.py:505
  23.6 18.8 %collective-permute-start.3 = (bf16[3,8,64,128]{3,2,1,0:T(8,128)(2,1)S(1)}, bf16[3,8,64,128]{3,2,1,0:T(8,128)(2,1)S(1)}, u32[]{:S(2)}, u32[]{:S(2)}) collective-permute-start(bf16[3,8,64,128]{3,2,1,0:T(8,128)(2,1)S(1)} %pad_maximum_fusion.1), channel_id=1, source_target_pairs={{0,16},{2,18},{4,20},{6,22},{8,24},{10,26},{12,28},{14,30},{16,0},... | collective-permute-start | bytes 1179656 | tf_op jit(solution)/shard_map/ppermute | solution.py:505
  26.1 26.3 %collective-permute-start = (bf16[2,4,512,128]{3,2,1,0:T(8,128)(2,1)}, bf16[2,4,512,128]{3,2,1,0:T(8,128)(2,1)S(1)}, u32[]{:S(2)}, u32[]{:S(2)}) collective-permute-start(bf16[2,4,512,128]{3,2,1,0:T(8,128)(2,1)} %get-tuple-element.28), channel_id=1, source_target_pairs={{0,2},{2,4},{4,6},{6,8},{8,10},{10,12},{12,14},{14,16},{16,18},{18... | collective-permute-start | bytes 3145736 | tf_op jit(solution)/shard_map/ppermute | solution.py:501
  42.5 10.1 %copy-start.1 = (bf16[3,8,128,128]{3,2,1,0:T(8,128)(2,1)}, bf16[3,8,128,128]{3,2,1,0:T(8,128)(2,1)S(1)}, u32[]{:S(2)}) copy-start(bf16[3,8,128,128]{3,2,1,0:T(8,128)(2,1)S(1)} %constant_dynamic-update-slice_fusion.ga_ref) | copy-start | bytes 2359300
  42.5 10.0 %collective-permute-start.4 = (bf16[3,8,128,128]{3,2,1,0:T(8,128)(2,1)S(1)}, bf16[3,8,128,128]{3,2,1,0:T(8,128)(2,1)S(1)}, u32[]{:S(2)}, u32[]{:S(2)}) collective-permute-start(bf16[3,8,128,128]{3,2,1,0:T(8,128)(2,1)S(1)} %constant_dynamic-update-slice_fusion.ga_ref), channel_id=1, source_target_pairs={{0,2},{2,0},{4,6},{6,4},{8,10},{10,8},{12,14},{14,12},{16,18},{18,... | collective-permute-start | bytes 2359304 | tf_op jit(solution)/shard_map/ppermute | solution.py:506
  52.5 1.0 copy-start.3
  52.5 1.2 copy-start.2
  65.1 3.9 %collective-permute-start.5 = (f32[8,128]{1,0:T(8,128)}, f32[8,128]{1,0:T(8,128)S(1)}, u32[]{:S(2)}, u32[]{:S(2)}) collective-permute-start(f32[8,128]{1,0:T(8,128)} %get-tuple-element.33.stat_ref), channel_id=1, source_target_pairs={{0,1},{1,0},{2,3},{3,2},{4,5},{5,4},{6,7},{7,6},{8,9},{9,8},{10,11... | collective-permute-start | bytes 12296 | tf_op jit(solution)/shard_map/ppermute | solution.py:555
  69.0 0.6 copy-start.8
  72.3 4.5 %collective-permute-start.7 = (bf16[2,8,16,128]{3,2,1,0:T(8,128)(2,1)}, bf16[2,8,16,128]{3,2,1,0:T(8,128)(2,1)S(1)}, u32[]{:S(2)}, u32[]{:S(2)}) collective-permute-start(bf16[2,8,16,128]{3,2,1,0:T(8,128)(2,1)} %shard_map.107), channel_id=1, source_target_pairs={{0,4},{2,6},{4,0},{6,2},{8,12},{10,14},{12,8},{14,10},{16,20},{18,... | collective-permute-start | bytes 196616 | tf_op jit(solution)/shard_map/ppermute | solution.py:505
  77.6 9.2 %collective-permute-start.8 = (bf16[2,8,32,128]{3,2,1,0:T(8,128)(2,1)S(1)}, bf16[2,8,32,128]{3,2,1,0:T(8,128)(2,1)S(1)}, u32[]{:S(2)}, u32[]{:S(2)}) collective-permute-start(bf16[2,8,32,128]{3,2,1,0:T(8,128)(2,1)S(1)} %pad_maximum_fusion.5), channel_id=1, source_target_pairs={{0,8},{2,10},{4,12},{6,14},{8,0},{10,2},{12,4},{14,6},{16,24},{18,... | collective-permute-start | bytes 393224 | tf_op jit(solution)/shard_map/ppermute | solution.py:505
  77.8 9.0 %copy-start.6 = (bf16[2,8,16,128]{3,2,1,0:T(8,128)(2,1)S(1)}, bf16[2,8,16,128]{3,2,1,0:T(8,128)(2,1)}, u32[]{:S(2)}) copy-start(bf16[2,8,16,128]{3,2,1,0:T(8,128)(2,1)} %shard_map.107) | copy-start | bytes 196612
  77.8 13.5 %copy-start.9 = (s32[8]{0:T(128)S(1)}, s32[8]{0:T(128)}, u32[]{:S(2)}) copy-start(s32[8]{0:T(128)} %offs.9) | copy-start | bytes 100
  85.5 5.9 %copy-start = (s32[8192]{0:T(1024)S(1)}, s32[8192]{0:T(1024)}, u32[]{:S(2)}) copy-start(s32[8192]{0:T(1024)} %param.12) | copy-start | bytes 98308
  85.5 45.3 %collective-permute-start.6 = (bf16[2,4,512,128]{3,2,1,0:T(8,128)(2,1)}, bf16[2,4,512,128]{3,2,1,0:T(8,128)(2,1)S(1)}, u32[]{:S(2)}, u32[]{:S(2)}) collective-permute-start(bf16[2,4,512,128]{3,2,1,0:T(8,128)(2,1)} %get-tuple-element.45), channel_id=1, source_target_pairs={{2,0},{4,2},{6,4},{8,6},{10,8},{12,10},{14,12},{16,14},{18,16},{20... | collective-permute-start | bytes 3145736 | tf_op jit(solution)/shard_map/ppermute | solution.py:585
  86.9 28.3 %collective-permute-start.9 = (bf16[2,8,64,128]{3,2,1,0:T(8,128)(2,1)S(1)}, bf16[2,8,64,128]{3,2,1,0:T(8,128)(2,1)S(1)}, u32[]{:S(2)}, u32[]{:S(2)}) collective-permute-start(bf16[2,8,64,128]{3,2,1,0:T(8,128)(2,1)S(1)} %pad_maximum_fusion.2), channel_id=1, source_target_pairs={{0,16},{2,18},{4,20},{6,22},{8,24},{10,26},{12,28},{14,30},{16,0},... | collective-permute-start | bytes 786440 | tf_op jit(solution)/shard_map/ppermute | solution.py:505
  115.2 15.6 %copy-start.4 = (bf16[2,8,128,128]{3,2,1,0:T(8,128)(2,1)}, bf16[2,8,128,128]{3,2,1,0:T(8,128)(2,1)S(1)}, u32[]{:S(2)}) copy-start(bf16[2,8,128,128]{3,2,1,0:T(8,128)(2,1)S(1)} %pad_maximum_fusion.sa_ref) | copy-start | bytes 1572868
  115.2 15.6 %collective-permute-start.10 = (bf16[2,8,128,128]{3,2,1,0:T(8,128)(2,1)S(1)}, bf16[2,8,128,128]{3,2,1,0:T(8,128)(2,1)S(1)}, u32[]{:S(2)}, u32[]{:S(2)}) collective-permute-start(bf16[2,8,128,128]{3,2,1,0:T(8,128)(2,1)S(1)} %pad_maximum_fusion.sa_ref), channel_id=1, source_target_pairs={{0,2},{2,0},{4,6},{6,4},{8,10},{10,8},{12,14},{14,12},{16,18},{18,... | collective-permute-start | bytes 1572872 | tf_op jit(solution)/shard_map/ppermute | solution.py:506
  130.8 0.9 copy-start.7
  130.9 1.1 copy-start.5

commit v2 on v1

v2 whole, which is shorter than its diff:
```python
import math

import jax
import jax.numpy as jnp
from jax import lax
from jax.experimental import pallas as pl
from jax.experimental.pallas import tpu as pltpu
from jax.sharding import PartitionSpec as P

HEADS = 16
SEL = 256
theta_base = 10000.0
eps_norm = 1e-06
NEG = -1e30
f32 = jnp.float32
bf16 = jnp.bfloat16


def dot_nn(a, b):
    return lax.dot_general(a, b, (((1,), (0,)), ((), ())), preferred_element_type=f32)


def dot_nt(a, b):
    return lax.dot_general(a, b, (((1,), (1,)), ((), ())), preferred_element_type=f32)


def dot_tn(a, b):
    return lax.dot_general(a, b, (((0,), (0,)), ((), ())), preferred_element_type=f32)


def lanes_of(shape):
    return lax.broadcasted_iota(jnp.int32, shape, len(shape) - 1)


def rows_of(shape):
    return lax.broadcasted_iota(jnp.int32, shape, len(shape) - 2)


def low_half(x):
    return jnp.where(lanes_of(x.shape) < 64, x, pltpu.roll(x, 64, 1))


def high_half(x):
    return jnp.where(lanes_of(x.shape) < 64, pltpu.roll(x, 64, 1), x)


def unpack_tables(cos_ref, sin_ref):
    c, s = cos_ref[...], sin_ref[...]
    cos = jnp.concatenate([low_half(c), high_half(c)], axis=0)
    sin = jnp.concatenate([low_half(s), high_half(s)], axis=0)
    sin = jnp.where(lanes_of(sin.shape) < 64, -sin, sin)
    return cos, sin


def rot(x, cos, sin):
    return x * cos + pltpu.roll(x, 64, 1) * sin


def spread(row):
    parts = []
    for i in range(row.shape[0]):
        parts.append(jnp.broadcast_to(row[i : i + 1, :], (128, 128)).T)
    return jnp.concatenate(parts, axis=0)


def compact(x):
    eye = rows_of((128, 128)) == lanes_of((128, 128))
    parts = []
    for i in range(x.shape[0] // 128):
        block = x[i * 128 : (i + 1) * 128, :]
        parts.append(jnp.sum(jnp.where(eye, block, 0.0), axis=0, keepdims=True))
    return jnp.concatenate(parts, axis=0)


def row_sum(x):
    return jnp.broadcast_to(jnp.sum(x, axis=1, keepdims=True), x.shape)


def prep_kernel(info, offs, k_ref, v_ref, cos_ref, sin_ref, kr_ref, vv_ref, send_ref, rows_ref):
    g = pl.program_id(0)
    par = info[1]
    tok = k_ref.shape[1]
    nb = rows_ref.shape[2]
    rate = tok // nb
    cos, sin = unpack_tables(cos_ref, sin_ref)
    for hh in range(2):
        h = 2 * g + hh
        hot = (lanes_of((nb, tok)) == offs[h] + rate * rows_of((nb, tok))).astype(bf16)
        kr = rot(k_ref[hh].astype(f32), cos, sin).astype(bf16)
        kr_ref[h] = kr
        vv_ref[h] = v_ref[hh]
        rows_ref[0, hh] = dot_nn(hot, kr).astype(bf16)
        rows_ref[1, hh] = dot_nn(hot, v_ref[hh]).astype(bf16)
    send_ref[0, 0] = kr_ref[2 * g + par]
    send_ref[1, 0] = v_ref[par]


def make_own_kernel(first, aliased):
    def own_kernel(info, offs, start_ref, q_ref, k_ref, v_ref, cos_ref, sin_ref, *refs):
        refs = refs[aliased:]
        qr_ref, e_ref, acc_ref, m_ref, l_ref, rows_ref, bias_ref = refs
        tok = q_ref.shape[1]
        nb = rows_ref.shape[1]
        rate = tok // nb
        half = tok // 2
        scale = 1.0 / math.sqrt(q_ref.shape[2])

        @pl.when(pl.program_id(0) == 0)
        def _():
            start = spread(start_ref[...])
            for c in range(tok // 128):
                key = lanes_of((tok, 128)) + c * 128
                ok = (key <= rows_of((tok, 128))) & (key.astype(f32) >= start)
                bias_ref[:, c * 128 : (c + 1) * 128] = jnp.where(ok, 0.0, NEG)

        cos, sin = unpack_tables(cos_ref, sin_ref)
        for hh in range(2):
            h = 2 * (pl.program_id(0) + first) + hh
            q = rot(q_ref[hh].astype(f32), cos, sin).astype(bf16)
            qr_ref[h] = q
            hot = (lanes_of((nb, tok)) == offs[h] + rate * rows_of((nb, tok))).astype(bf16)
            rows_ref[hh] = dot_nn(hot, q).astype(bf16)
            vals = jnp.concatenate([v_ref[h], jnp.ones((tok, 128), bf16)], axis=1)
            for c in range(2):
                lo, n = c * half, (c + 1) * half
                z = dot_nt(q[lo:n], k_ref[h, :n, :]) * scale + bias_ref[lo:n, :n]
                m = jnp.max(z, axis=1, keepdims=True)
                e = jnp.exp(z - m).astype(bf16)
                e_ref[h, lo:n, :n] = e
                out = dot_nn(e, vals[:n])
                acc_ref[h, lo:n, :] = out[:, :128]
                l_ref[h, lo:n, :] = out[:, 128:]
                m_ref[h, lo:n, :] = jnp.broadcast_to(m, (half, 128))

    return own_kernel


def prev_kernel(info, start_ref, q_ref, kv_ref, acc_in, m_ref, l_in, acc_ref, l_ref, mn_ref, e_ref, mp_ref, bias_ref):
    g = pl.program_id(0)
    index, sel = info[0], info[2]
    tok = q_ref.shape[1]
    half = tok // 2
    scale = 1.0 / math.sqrt(q_ref.shape[2])
    h = 2 * g + sel

    @pl.when(g == 0)
    def _():
        start = spread(start_ref[...])
        first = jnp.where(index == 0, float(tok), 0.0)
        for c in range(tok // 128):
            key = (lanes_of((tok, 128)) + c * 128).astype(f32)
            ok = (key - tok >= start) & (key >= first)
            bias_ref[:, c * 128 : (c + 1) * 128] = jnp.where(ok, 0.0, NEG)

    vals = jnp.concatenate([kv_ref[1, 0], jnp.ones((tok, 128), bf16)], axis=1)
    for c in range(2):
        sl = slice(c * half, (c + 1) * half)
        z = dot_nt(q_ref[h, sl, :], kv_ref[0, 0]) * scale + bias_ref[sl, :]
        m = jnp.max(z, axis=1, keepdims=True)
        e = jnp.exp(z - m).astype(bf16)
        e_ref[g, sl, :] = e
        out = dot_nn(e, vals)
        m_prev = jnp.broadcast_to(m, (half, 128))
        m_own = m_ref[h, sl, :]
        mn = jnp.maximum(m_own, m_prev)
        a_own = jnp.exp(m_own - mn)
        a_prev = jnp.exp(m_prev - mn)
        mp_ref[g, sl, :] = m_prev
        mn_ref[g, sl, :] = mn
        acc_ref[h, sl, :] = a_own * acc_in[h, sl, :] + a_prev * out[:, :128]
        l_ref[h, sl, :] = a_own * l_in[h, sl, :] + a_prev * out[:, 128:]


def key_order(index, codes, nb, part, count):
    col = lanes_of((1, count)) + part * count
    slot = col // nb
    dev = jnp.full((1, count), index, jnp.int32)
    for b, code in enumerate(codes):
        dev = dev ^ (((slot >> b) & 1) * code)
    return dev * nb + col % nb


def make_join_kernel(codes):
    def join_kernel(
        info, offs, start_ref, acc_ref, m_ref, l_ref, mn_ref, mp_ref, q1_ref, ga_ref, gb_ref, og_ref, gain_ref,
        attn_ref, rr_ref, e1_ref, rs_ref, ar_ref, or_ref, stat_ref,
        start_s, m_s, l_s, acc_s, sq_s, cr_s,
    ):
        g = pl.program_id(0)
        index, sel = info[0], info[2]
        tok = og_ref.shape[1]
        nb = q1_ref.shape[1]
        rate = tok // nb
        count = ga_ref.shape[2]
        scale = 1.0 / math.sqrt(og_ref.shape[2])

        @pl.when(g == 0)
        def _():
            start_s[...] = spread(start_ref[...])
            sq_s[...] = jnp.zeros_like(sq_s)
            cr_s[...] = jnp.zeros_like(cr_s)

        for hh in range(2):
            h = 2 * g + hh
            off = offs[h]
            rows = pl.ds(off, nb, stride=rate)
            here = sel == hh
            m_own = m_ref[h]
            m0 = jnp.where(here, mn_ref[g], m_own)
            m_s[hh] = m0
            l_s[hh] = l_ref[h]
            acc_s[hh] = acc_ref[h]

            q1 = q1_ref[hh]
            start1 = start_s[rows, :][:, :1]
            qb = index * nb + rows_of((nb, count))
            zs = []
            for part, ref in enumerate((ga_ref, gb_ref)):
                kb = key_order(index, codes, nb, part, count)
                pos = (off + rate * kb - index * tok).astype(f32)
                ok = (kb <= qb) & (pos >= start1)
                zs.append(jnp.where(ok, dot_nt(q1, ref[0, hh]) * scale, NEG))
            m1 = jnp.maximum(jnp.max(zs[0], axis=1, keepdims=True), jnp.max(zs[1], axis=1, keepdims=True))
            o1 = jnp.zeros((nb, 256), f32)
            for part, ref in enumerate((ga_ref, gb_ref)):
                e1 = jnp.exp(zs[part] - m1).astype(bf16)
                e1_ref[hh, :, part * count : (part + 1) * count] = e1
                v1 = jnp.concatenate([ref[1, hh], jnp.ones((count, 128), bf16)], axis=1)
                o1 = o1 + dot_nn(e1, v1)

            mr = m_s[hh, rows, :]
            lr = l_s[hh, rows, :]
            ar = acc_s[hh, rows, :]
            m1b = jnp.broadcast_to(m1, (nb, 128))
            mn = jnp.maximum(mr, m1b)
            b0 = jnp.exp(mr - mn)
            b1 = jnp.exp(m1b - mn)
            ln = b0 * lr + b1 * o1[:, 128:]
            m_s[hh, rows, :] = mn
            l_s[hh, rows, :] = ln
            acc_s[hh, rows, :] = b0 * ar + b1 * o1[:, :128]
            lse1 = mn + jnp.log(ln)
            rs_ref[hh] = jnp.where(lanes_of((nb, 128)) < 64, lse1, b1 / ln)

            inv = 1.0 / l_s[hh]
            attn = (acc_s[hh] * inv).astype(bf16)
            attn_ref[h] = attn
            both = jnp.where((lanes_of((tok, 128)) < 64) | jnp.logical_not(here), m_own, mp_ref[g])
            rr_ref[h] = jnp.exp(both - m_s[hh]) * inv
            af = attn.astype(f32)
            gd = og_ref[hh].astype(f32) * gain_ref[hh]
            sq_s[...] += af * af
            cr_s[...] += gd * af
            hot = (lanes_of((nb, tok)) == off + rate * rows_of((nb, tok))).astype(bf16)
            ar_ref[hh] = dot_nn(hot, attn).astype(bf16)
            or_ref[hh] = dot_nn(hot, og_ref[hh]).astype(bf16)

        @pl.when(g == pl.num_programs(0) - 1)
        def _():
            stat_ref[...] = jnp.concatenate([compact(row_sum(sq_s[...])), compact(row_sum(cr_s[...]))], axis=0)

    return join_kernel


def norm_terms(stat_ref, other_ref, feats):
    total = stat_ref[...] + other_ref[...]
    n = total.shape[0] // 2
    rinv = lax.rsqrt(total[:n] / feats + eps_norm)
    return rinv, rinv * rinv * total[n:] / feats


def split3(x):
    hi = x.astype(bf16).astype(f32)
    mid = (x - hi).astype(bf16).astype(f32)
    return hi, mid, x - hi - mid


def split3(x):
    hi = x.astype(bf16).astype(f32)
    mid = (x - hi).astype(bf16).astype(f32)
    return hi, mid, x - hi - mid


def split3(x):
    hi = x.astype(bf16).astype(f32)
    mid = (x - hi).astype(bf16).astype(f32)
    return hi, mid, x - hi - mid


def split3(x):
    hi = x.astype(bf16).astype(f32)
    mid = (x - hi).astype(bf16).astype(f32)
    return hi, mid, x - hi - mid


def split3(x):
    hi = x.astype(bf16).astype(f32)
    mid = (x - hi).astype(bf16).astype(f32)
    return hi, mid, x - hi - mid


def split3(x):
    hi = x.astype(bf16).astype(f32)
    mid = (x - hi).astype(bf16).astype(f32)
    return hi, mid, x - hi - mid


def split3(x):
    hi = x.astype(bf16).astype(f32)
    mid = (x - hi).astype(bf16).astype(f32)
    return hi, mid, x - hi - mid


def split3(x):
    hi = x.astype(bf16).astype(f32)
    mid = (x - hi).astype(bf16).astype(f32)
    return hi, mid, x - hi - mid


def make_rows_kernel(feats):
    def rows_kernel(offs, begin_ref, stat_ref, other_ref, ar_ref, or_ref, q1_ref, gain_ref, rs_ref, out_ref, rinv_s, cc_s, st_s):
        nb = ar_ref.shape[1]
        rate = rinv_s.shape[0] // nb
        rinv, cc = norm_terms(stat_ref, other_ref, feats)
        rinv_s[...] = spread(rinv)
        cc_s[...] = spread(cc)
        st_s[...] = spread(begin_ref[...])
        for h in range(ar_ref.shape[0]):
            rows = pl.ds(offs[h], nb, stride=rate)
            af = ar_ref[h].astype(f32)
            gd = or_ref[h].astype(f32) * gain_ref[h]
            ag = (rinv_s[rows, :] * (gd - af * cc_s[rows, :])).astype(bf16)
            delta = row_sum(ag.astype(f32) * af)
            out_ref[0, h] = ag
            lane = lanes_of((nb, 128))
            pack = jnp.zeros((nb, 128), f32)
            for i, x in enumerate(split3(low_half(rs_ref[h])) + split3(delta) + split3(st_s[rows, :])):
                pack = jnp.where(lane == i, x, pack)
            out_ref[1, h] = pack.astype(bf16)
            out_ref[2, h] = q1_ref[h]

    return rows_kernel


def grad_terms(attn, og, gain, rinv, cc):
    af = attn.astype(f32)
    gd = og.astype(f32) * gain
    ag = (rinv * (gd - af * cc)).astype(bf16).astype(f32)
    return af, ag, row_sum(ag * af)


def make_back_prev_kernel(feats):
    def back_prev_kernel(
        info, stat_ref, other_ref, q_ref, attn_ref, rr_ref, e_ref, og_ref, gain_ref, kv_ref,
        back_ref, dq_ref, rinv_s, cc_s,
    ):
        g = pl.program_id(0)
        h = 2 * g + info[2]
        tok = q_ref.shape[1]
        half = tok // 2
        scale = 1.0 / math.sqrt(q_ref.shape[2])

        @pl.when(g == 0)
        def _():
            rinv, cc = norm_terms(stat_ref, other_ref, feats)
            rinv_s[...] = spread(rinv)
            cc_s[...] = spread(cc)

        af, ag, delta = grad_terms(attn_ref[h], og_ref[0], gain_ref[0], rinv_s[...], cc_s[...])
        r = high_half(rr_ref[h])
        do = (ag * r).astype(bf16)
        dl = delta * r
        dk = jnp.zeros((128, tok), f32)
        dv = jnp.zeros((128, tok), f32)
        for c in range(2):
            sl = slice(c * half, (c + 1) * half)
            e = e_ref[g, sl, :]
            dp = dot_nt(do[sl], kv_ref[1, 0])
            ds = (e.astype(f32) * (dp - jnp.concatenate([dl[sl]] * (tok // 128), axis=1))).astype(bf16)
            dq_ref[g, sl, :] = dot_nn(ds, kv_ref[0, 0])
            dk = dk + dot_tn(q_ref[h, sl, :], ds)
            dv = dv + dot_tn(do[sl], e)
        back_ref[0, 0] = (dk * scale).T.astype(bf16)
        back_ref[1, 0] = dv.T.astype(bf16)

    return back_prev_kernel


def make_back_own_kernel(feats, first, aliased):
    def back_own_kernel(
        info, offs, stat_ref, other_ref, q_ref, k_ref, v_ref, attn_ref, rr_ref, e_ref, dqp_ref,
        og_ref, gain_ref, e1_ref, rs_ref, ga_ref, gb_ref, cos_ref, sin_ref, *refs
    ):
        normed_ref, gq_ref, dk_ref, dv_ref, rinv_s, cc_s, ag_s, de_s, dq_s = refs[aliased:]
        step = pl.program_id(0)
        h = step + first
        sel = info[2]
        tok = q_ref.shape[1]
        nb = e1_ref.shape[1]
        rate = tok // nb
        count = ga_ref.shape[2]
        half = tok // 2
        scale = 1.0 / math.sqrt(q_ref.shape[2])

        @pl.when(step == 0)
        def _():
            rinv, cc = norm_terms(stat_ref, other_ref, feats)
            rinv_s[...] = spread(rinv)
            cc_s[...] = spread(cc)

        rinv = rinv_s[...]
        af, ag, delta = grad_terms(attn_ref[h], og_ref[0], gain_ref[0], rinv, cc_s[...])
        normed_ref[0] = (af * rinv * gain_ref[0]).astype(bf16)
        ag_s[...] = ag
        de_s[...] = delta
        r = low_half(rr_ref[h])
        do = (ag * r).astype(bf16)
        dl = delta * r
        here = jnp.where(h % 2 == sel, 1.0, 0.0)
        dks = []
        for c in range(2):
            lo, n = c * half, (c + 1) * half
            sl = slice(lo, n)
            e = e_ref[h, sl, :n]
            dp = dot_nt(do[sl], v_ref[h, :n, :])
            ds = (e.astype(f32) * (dp - jnp.concatenate([dl[sl]] * (n // 128), axis=1))).astype(bf16)
            dq_s[sl, :] = dot_nn(ds, k_ref[h, :n, :]) + dqp_ref[h // 2, sl, :] * here
            dks.append((dot_tn(q_ref[h, sl, :], ds), dot_tn(do[sl], e)))
        for i, ref in enumerate((dk_ref, dv_ref)):
            ref[h, :half, :] = (dks[0][i] + dks[1][i][:, :half]).T
            ref[h, half:, :] = dks[1][i][:, half:].T

        rows = pl.ds(offs[h], nb, stride=rate)
        r1 = high_half(rs_ref[0])
        g1 = (ag_s[rows, :] * r1).astype(bf16)
        d1 = (de_s[rows, :] * r1)[:, :1]
        dq1 = jnp.zeros((nb, 128), f32)
        for part, ref in enumerate((ga_ref, gb_ref)):
            dp1 = dot_nt(g1, ref[1, 0])
            ds1 = (e1_ref[0, :, part * count : (part + 1) * count].astype(f32) * (dp1 - d1)).astype(bf16)
            dq1 = dq1 + dot_nn(ds1, ref[0, 0])
        dq_s[rows, :] += dq1
        cos, sin = unpack_tables(cos_ref, sin_ref)
        gq_ref[0] = rot(dq_s[...] * scale, cos, -sin).astype(bf16)

    return back_own_kernel


def make_final_kernel(codes):
    def final_kernel(
        info, offs, dk_ref, dv_ref, back_ref, rows_ref, sa_ref, sb_ref, cos_ref, sin_ref,
        gk_ref, gv_ref, dk_s, dv_s,
    ):
        g = pl.program_id(0)
        index, par = info[0], info[1]
        tok = dk_ref.shape[1]
        nb = rows_ref.shape[2]
        rate = tok // nb
        count = sa_ref.shape[2]
        scale = 1.0 / math.sqrt(dk_ref.shape[2])
        cos, sin = unpack_tables(cos_ref, sin_ref)
        kb = index * nb + rows_of((nb, count))
        pick = (rows_of((16, 128)) == lanes_of((16, 128))).astype(bf16)
        for hh in range(2):
            h = 2 * g + hh
            off = offs[h]
            here = (par == hh) & (index < info[3] - 1)
            dk_s[hh] = dk_ref[h] * scale + jnp.where(here, back_ref[0, 0].astype(f32), 0.0)
            dv_s[hh] = dv_ref[h] + jnp.where(here, back_ref[1, 0].astype(f32), 0.0)
            k1 = rows_ref[0, hh]
            v1 = rows_ref[1, hh]
            kpos = (off + rate * kb).astype(f32)
            dk1 = jnp.zeros((nb, 128), f32)
            dv1 = jnp.zeros((nb, 128), f32)
            for part, s in enumerate((sa_ref, sb_ref)):
                qb = key_order(index, codes, nb, part, count)
                st = dot_nt(pick, s[1, hh])
                lse = st[0:1] + st[1:2] + st[2:3]
                delta = st[3:4] + st[4:5] + st[5:6]
                start = st[6:7] + st[7:8] + st[8:9]
                ok = (kb <= qb) & (kpos >= start)
                z = jnp.where(ok, dot_nt(k1, s[2, hh]) * scale - lse, NEG)
                p = jnp.exp(z).astype(bf16)
                dp = dot_nt(v1, s[0, hh])
                ds = (p.astype(f32) * (dp - delta)).astype(bf16)
                dk1 = dk1 + dot_nn(ds, s[2, hh])
                dv1 = dv1 + dot_nn(p, s[0, hh])
            rows = pl.ds(off, nb, stride=rate)
            dk_s[hh, rows, :] += dk1 * scale
            dv_s[hh, rows, :] += dv1
            gk_ref[hh] = rot(dk_s[hh], cos, -sin).astype(bf16)
            gv_ref[hh] = dv_s[hh].astype(bf16)

    return final_kernel


def call(kernel, prefetch, grid, ins, outs, scratch=(), alias=(), cost=None):
    arrays, in_specs = [], []
    for a, b, m in ins:
        if b is None:
            arrays.append(pltpu.with_memory_space_constraint(a, pltpu.VMEM))
            in_specs.append(pl.BlockSpec(memory_space=pltpu.VMEM))
        else:
            arrays.append(a)
            in_specs.append(pl.BlockSpec(b, m))
    out_shape, out_specs = [], []
    for s, d, b, m in outs:
        if b is None:
            out_shape.append(pltpu.VMEM(s, d))
            out_specs.append(pl.BlockSpec(memory_space=pltpu.VMEM))
        else:
            out_shape.append(jax.ShapeDtypeStruct(s, d))
            out_specs.append(pl.BlockSpec(b, m))
    us = 4
    return pl.pallas_call(
        kernel,
        out_shape=out_shape,
        grid_spec=pltpu.PrefetchScalarGridSpec(
            num_scalar_prefetch=len(prefetch),
            grid=grid,
            in_specs=in_specs,
            out_specs=out_specs,
            scratch_shapes=list(scratch),
        ),
        input_output_aliases={len(prefetch) + i: o for i, o in alias},
        cost_estimate=pl.CostEstimate(flops=0, transcendentals=0, bytes_accessed=int(us * 3.0e6)),
        compiler_params=pltpu.CompilerParams(
            dimension_semantics=("arbitrary",) * len(grid), vmem_limit_bytes=24 << 20
        ),
    )(*prefetch, *arrays)


def after(x, *deps):
    return lax.optimization_barrier((x, *deps))[0]


def body(queries, keys, values, out_grad, norm_gain, doc_start, head_offsets):
    heads, tok, width = queries.shape
    ctx = lax.axis_size("ctx")
    rate = ctx * tok // SEL
    nb = tok // rate
    feats = float(HEADS * width)
    pairs = heads // 2
    index = lax.axis_index("ctx")
    base = index * tok
    codes = [1 << b for b in range(2, ctx.bit_length() - 1)] + [2, 1]

    starts = lax.dynamic_slice_in_dim(doc_start, base, tok)
    position = base + jnp.arange(tok, dtype=jnp.int32)
    rel = (position - starts).astype(f32)
    freq = theta_base ** (-2.0 * jnp.arange(width // 2).astype(f32) / width)
    angle = jnp.concatenate([rel[: tok // 2, None] * freq[None, :], rel[tok // 2 :, None] * freq[None, :]], axis=1)
    cos, sin = jnp.cos(angle), jnp.sin(angle)
    begin = starts.astype(f32).reshape(tok // 128, 128)
    start_rel = (starts - base).astype(f32).reshape(tok // 128, 128)
    info = jnp.stack([index, index % 2, (index + 1) % 2, jnp.int32(ctx)]).astype(jnp.int32)
    gain = norm_gain.reshape(heads, 1, width)

    pair3 = (2, tok, width)
    one3 = (1, tok, width)
    full = queries.shape
    const = lambda n: (lambda i, *s: (0,) * n)
    whole = lambda a: (a, a.shape, const(a.ndim))
    vm = lambda a: (a, None, None)
    gp = lambda g, *s: (g, 0, 0)
    g4 = lambda g, *s: (0, g, 0, 0)

    def swap(x, code):
        return lax.ppermute(x, "ctx", [(i, i ^ code) for i in range(ctx)])

    half_count = SEL // 2

    k_rot, vals, send, rows = call(
        prep_kernel, (info, head_offsets), (pairs,),
        [(keys, pair3, gp), (values, pair3, gp), whole(cos), whole(sin)],
        [
            (full, bf16, None, None),
            (full, bf16, None, None),
            ((2, pairs, tok, width), bf16, (2, 1, tok, width), g4),
            ((2, heads, nb, width), bf16, (2, 2, nb, width), g4),
        ],
    )
    lead, z_code, y_code, core = codes[:-3], codes[-3], codes[-2], codes[-1]
    recv = lax.ppermute(send, "ctx", [(i, i + 1) for i in range(ctx - 1)])

    def join2(x, code):
        return jnp.concatenate([x, swap(x, code)], axis=2)

    x = rows
    for code in lead:
        x = join2(x, code)

    def own(first, qs, prior):
        n = pairs // 2
        outs = [
            (full, bf16, None, None),
            ((heads, tok, tok), bf16, None, None),
            (full, f32, None, None),
            (full, f32, None, None),
            (full, f32, None, None),
            ((heads, nb, width), bf16, (2, nb, width), lambda g, *s: (g + first, 0, 0)),
        ]
        ins = [
            whole(start_rel),
            (qs, pair3, lambda g, *s: (g + first, 0, 0)),
            vm(k_rot), vm(vals), whole(cos), whole(sin),
        ]
        alias = []
        for i, a in enumerate(prior):
            alias.append((len(ins), i))
            ins.append(vm(a) if i < 5 else (a, (2, nb, width), lambda g, *s: (first, 0, 0)))
        return call(
            make_own_kernel(first, len(prior)), (info, head_offsets), (n,), ins, outs,
            [pltpu.VMEM((tok, tok), f32)], alias,
        )

    part = own(0, queries, [])
    x = after(x, part[3])
    y = join2(x, z_code)
    part = own(pairs // 2, after(queries, x), part)
    q_rot, e_own, acc, m_own, lsum, q1 = part
    y = after(y, m_own)
    ga = join2(y, y_code)

    acc, lsum, m_new, e_prev, m_prev = call(
        prev_kernel, (info,), (pairs,),
        [
            whole(start_rel), vm(after(q_rot, y)),
            (recv, (2, 1, tok, width), g4),
            vm(acc), vm(m_own), vm(lsum),
        ],
        [
            (full, f32, None, None),
            (full, f32, None, None),
            ((pairs, tok, width), f32, None, None),
            ((pairs, tok, tok), bf16, None, None),
            ((pairs, tok, width), f32, None, None),
        ],
        [pltpu.VMEM((tok, tok), f32)],
        [(3, 0), (5, 1)],
    )
    ga = after(ga, m_new)
    gb = swap(ga, core)

    attn, rr, e1, rs, attn_rows, og_rows, stat = call(
        make_join_kernel(codes), (info, head_offsets), (pairs,),
        [
            whole(start_rel), vm(acc), vm(m_own), vm(lsum), vm(m_new), vm(m_prev),
            (q1, (2, nb, width), gp),
            (ga, (2, 2, half_count, width), g4),
            (gb, (2, 2, half_count, width), g4),
            (out_grad, pair3, gp),
            (gain, (2, 1, width), gp),
        ],
        [
            (full, bf16, None, None),
            (full, f32, None, None),
            ((heads, nb, SEL), bf16, (2, nb, SEL), gp),
            ((heads, nb, width), f32, (2, nb, width), gp),
            ((heads, nb, width), bf16, (2, nb, width), gp),
            ((heads, nb, width), bf16, (2, nb, width), gp),
            ((2 * tok // 128, 128), f32, (2 * tok // 128, 128), const(2)),
        ],
        [pltpu.VMEM((tok, 128), f32)] + [pltpu.VMEM((2, tok, 128), f32)] * 3 + [pltpu.VMEM((tok, 128), f32)] * 2,
    )
    other = lax.ppermute(stat, "head", [(0, 1), (1, 0)])

    (x,) = call(
        make_rows_kernel(feats), (head_offsets,), (1,),
        [whole(begin), whole(stat), whole(other), whole(attn_rows), whole(og_rows), whole(q1), whole(gain), whole(rs)],
        [((3, heads, nb, width), bf16, (3, heads, nb, width), const(4))],
        [pltpu.VMEM((tok, 128), f32)] * 3,
    )
    rows1 = x
    for code in lead:
        x = join2(x, code)

    gsel = lambda g, s, *_: (2 * g + s[2], 0, 0)
    back, dq_prev = call(
        make_back_prev_kernel(feats), (info,), (pairs,),
        [
            whole(stat), whole(after(other, rows1)),
            vm(q_rot), vm(attn), vm(rr), vm(e_prev),
            (out_grad, one3, gsel),
            (gain, (1, 1, width), gsel),
            (recv, (2, 1, tok, width), g4),
        ],
        [
            ((2, pairs, tok, width), bf16, (2, 1, tok, width), g4),
            ((pairs, tok, width), f32, None, None),
        ],
        [pltpu.VMEM((tok, 128), f32)] * 2,
    )
    x = after(x, dq_prev)
    y = join2(x, z_code)
    back = lax.ppermute(back, "ctx", [(i + 1, i) for i in range(ctx - 1)])

    def back_own(first, dep, prior):
        n = heads // 2
        hp = lambda h, *s: (h + first, 0, 0)
        hg = lambda h, *s: (0, h + first, 0, 0)
        ins = [
            whole(stat), whole(after(other, dep)),
            vm(q_rot), vm(k_rot), vm(vals), vm(attn), vm(rr), vm(e_own), vm(dq_prev),
            (out_grad, one3, hp),
            (gain, (1, 1, width), hp),
            (e1, (1, nb, SEL), hp),
            (rs, (1, nb, width), hp),
            (ga, (2, 1, half_count, width), hg),
            (gb, (2, 1, half_count, width), hg),
            whole(cos), whole(sin),
        ]
        alias = []
        for i, a in enumerate(prior):
            alias.append((len(ins), i))
            ins.append(vm(a) if i >= 2 else (a, (1, 16, width), lambda h, *s: (first, 0, 0)))
        return call(
            make_back_own_kernel(feats, first, len(prior)), (info, head_offsets), (n,), ins,
            [
                (full, bf16, one3, hp),
                (full, bf16, one3, hp),
                (full, f32, None, None),
                (full, f32, None, None),
            ],
            [pltpu.VMEM((tok, 128), f32)] * 5,
            alias,
        )

    part = back_own(0, x, [])
    y = after(y, part[2])
    sa = join2(y, y_code)
    part = back_own(heads // 2, y, part)
    normed, grad_queries, dk_own, dv_own = part
    sa = after(sa, dk_own)
    sb = swap(sa, core)

    grad_keys, grad_values = call(
        make_final_kernel(codes), (info, head_offsets), (pairs,),
        [
            vm(dk_own), vm(dv_own),
            (back, (2, 1, tok, width), g4),
            (rows, (2, 2, nb, width), g4),
            (sa, (3, 2, half_count, width), g4),
            (sb, (3, 2, half_count, width), g4),
            whole(cos), whole(sin),
        ],
        [
            (full, bf16, pair3, gp),
            (full, bf16, pair3, gp),
        ],
        [pltpu.VMEM((2, tok, 128), f32)] * 2,
    )
    return (normed, grad_queries, grad_keys, grad_values)


def solution(mesh):
    return jax.shard_map(
        body,
        mesh=mesh,
        in_specs=(
            P("head", "ctx", None),
            P("head", "ctx", None),
            P("head", "ctx", None),
            P("head", "ctx", None),
            P("head", None),
            P(),
            P("head"),
        ),
        out_specs=(
            P("head", "ctx", None),
            P("head", "ctx", None),
            P("head", "ctx", None),
            P("head", "ctx", None),
        ),
        check_vma=False,
    )
```

time: 142 us -> 101 us (0.71)
  Pallas kernels: 60.8 us -> 43.3 us
  local copies, waits for them, and re-layouts: 16.1 us -> 3.13 us
  waiting for transfers between devices: 40.3 us -> 28.7 us
  starting transfers between devices: 16 us -> 22.9 us
  other arithmetic: 6.93 us -> 1.77 us
    pallas_call x7 -> x10, Pallas kernels: 60.8 us -> 43.3 us  [call(): pl.pallas_call(kernel, out_shape=out_shape, grid_spec=pltpu.PrefetchScala...]
    gather x1 -> x0, local copies, waits for them, and re-layouts: 11.8 us -> none  [body(): query_start = jnp.take(doc_start, query_pos).reshape(heads, 2, half_count)]
    ppermute x8, waiting for transfers between devices: 37 us -> 26.5 us  [swap(): return lax.ppermute(x, 'ctx', [(i, i ^ code) for i in range(ctx)])]
    ppermute x8, starting transfers between devices: 12.7 us -> 17.6 us  [swap(): return lax.ppermute(x, 'ctx', [(i, i ^ code) for i in range(ctx)])]
    concatenate x5 -> x6, other arithmetic: 2.74 us -> 0.17 us  [join2(): return jnp.concatenate([x, swap(x, code)], axis=2)]
    unnamed x24 -> x12, local copies, waits for them, and re-layouts: 3.91 us -> 3.12 us
  transfers between devices with their start and end apart: 11 -> 11, of which waited for: 6 -> 7; matrix products, arithmetic and copies ran while one was open for 10% -> 0% of each run, Pallas kernels for 23% -> 25%
where the time goes in v2:
time: 101 us
  Pallas kernels  43.3 us (43%)
  waiting for transfers between devices  28.7 us (28%)
  starting transfers between devices  22.9 us (23%)
  local copies, waits for them, and re-layouts  3.13 us (3%)
  other arithmetic  1.77 us (2%)
    pallas_call x10, Pallas kernels, call(): pl.pallas_call(kernel, out_shape=out_shape, grid_spec=pltpu.PrefetchScala...  43.3 us
    ppermute x8, waiting for transfers between devices, swap(): return lax.ppermute(x, 'ctx', [(i, i ^ code) for i in range(ctx)])  26.5 us
    ppermute x8, starting transfers between devices, swap(): return lax.ppermute(x, 'ctx', [(i, i ^ code) for i in range(ctx)])  17.6 us
    unnamed x12, local copies, waits for them, and re-layouts  3.12 us
    ppermute x1, starting transfers between devices, body(): recv = lax.ppermute(send, 'ctx', [(i, i + 1) for i in range(ctx - 1)])  2.47 us
    ppermute x1, waiting for transfers between devices, body(): other = lax.ppermute(stat, 'head', [(0, 1), (1, 0)])  2.12 us
  transfers between devices with their start and end apart: 11, of which 7 were waited for; matrix products, arithmetic and copies ran while one was open for 0% of the time, Pallas kernels for 25%

profile of v2, /device:TPU:0, one launch (start us, length us, event | category | flops | bytes accessed | tf_op | source)
XLA Modules:
  0.0 100.6 jit_solution(13749383933139383439)
XLA Ops:
  0.6 0.0 copy-start.1
  0.7 0.8 convert_bitcast_fusion
  1.5 0.1 broadcast_multiply_fusion.1
  1.7 0.5 fusion
  2.2 0.1 pad_add_fusion.info
  2.3 0.0 copy-start.2
  2.3 1.2 %copy-done.2 = bf16[8,512,128]{2,1,0:T(8,128)(2,1)S(1)} copy-done((bf16[8,512,128]{2,1,0:T(8,128)(2,1)S(1)}, bf16[8,512,128]{2,1,0:T(8,128)(2,1)}, u32[]{:S(2)}) %copy-start.2) | copy-done | bytes 1048600
  3.5 0.0 copy-start.3
  3.5 1.2 %copy-done.3 = bf16[8,512,128]{2,1,0:T(8,128)(2,1)S(1)} copy-done((bf16[8,512,128]{2,1,0:T(8,128)(2,1)S(1)}, bf16[8,512,128]{2,1,0:T(8,128)(2,1)}, u32[]{:S(2)}) %copy-start.3) | copy-done | bytes 1048600
  4.7 0.7 copy-done.5
  5.4 2.1 %shard_map.102 = (bf16[8,512,128]{2,1,0:T(8,128)(2,1)S(1)}, bf16[8,512,128]{2,1,0:T(8,128)(2,1)S(1)}, bf16[2,4,512,128]{3,2,1,0:T(8,128)(2,1)S(1)}, bf16[2,8,16,128]{3,2,1,0:T(8,128)(2,1)S(1)}) custom-call(s32[4]{0:T(128)S(1)} %pad_add_fusion.info, s32[8]{0:T(128)S(1)} %copy-done.5, bf16[8,512,128]{2,1,0:T(8,128)(2,1)S(1)} %copy-done.2, ...), custom_call_target="tpu_custom_call" | custom-call | bytes 12000000 | tf_op jit(solution)/shard_map/pallas_call | solution.py:515
  7.5 2.5 %collective-permute-start.2 = (bf16[2,4,512,128]{3,2,1,0:T(8,128)(2,1)S(1)}, bf16[2,4,512,128]{3,2,1,0:T(8,128)(2,1)S(1)}, u32[]{:S(2)}, u32[]{:S(2)}) collective-permute-start(bf16[2,4,512,128]{3,2,1,0:T(8,128)(2,1)S(1)} %get-tuple-element.70), channel_id=1, source_target_pairs={{0,2},{2,4},{4,6},{6,8},{8,10},{10,12},{12,14},{14,16},{16,18},{18... | collective-permute-start | bytes 3145736 | tf_op jit(solution)/shard_map/ppermute | solution.py:584
  10.0 2.6 %collective-permute-start = (bf16[2,8,16,128]{3,2,1,0:T(8,128)(2,1)S(1)}, bf16[2,8,16,128]{3,2,1,0:T(8,128)(2,1)S(1)}, u32[]{:S(2)}, u32[]{:S(2)}) collective-permute-start(bf16[2,8,16,128]{3,2,1,0:T(8,128)(2,1)S(1)} %get-tuple-element.55.rows_ref), channel_id=1, source_target_pairs={{0,8},{2,10},{4,12},{6,14},{8,0},{10,2},{12,4},{14,6},{16,24},{18,... | collective-permute-start | bytes 196616 | tf_op jit(solution)/shard_map/ppermute | solution.py:569
  12.5 0.0 copy-done.1
  12.5 3.3 %shard_map.103 = (bf16[8,512,128]{2,1,0:T(8,128)(2,1)S(1)}, bf16[8,512,512]{2,1,0:T(8,128)(2,1)S(1)}, f32[8,512,128]{2,1,0:T(8,128)S(1)}, f32[8,512,128]{2,1,0:T...) custom-call(s32[4]{0:T(128)S(1)} %pad_add_fusion.info, s32[8]{0:T(128)S(1)} %copy-done.5, ...), custom_call_target="tpu_custom_call" | custom-call | bytes 12000000 | tf_op jit(solution)/shard_map/pallas_call | solution.py:515
  15.9 0.0 collective-permute-done
  15.9 2.6 %collective-permute-start.1 = (bf16[2,8,32,128]{3,2,1,0:T(8,128)(2,1)S(1)}, bf16[2,8,32,128]{3,2,1,0:T(8,128)(2,1)S(1)}, u32[]{:S(2)}, u32[]{:S(2)}) collective-permute-start(bf16[2,8,32,128]{3,2,1,0:T(8,128)(2,1)S(1)} %pad_maximum_fusion.6), channel_id=1, source_target_pairs={{0,16},{2,18},{4,20},{6,22},{8,24},{10,26},{12,28},{14,30},{16,0},... | collective-permute-start | bytes 393224 | tf_op jit(solution)/shard_map/ppermute | solution.py:569
  18.6 3.4 %shard_map.104 = (bf16[8,512,128]{2,1,0:T(8,128)(2,1)S(1)}, bf16[8,512,512]{2,1,0:T(8,128)(2,1)S(1)}, f32[8,512,128]{2,1,0:T(8,128)S(1)}, f32[8,512,128]{2,1,0:T...) custom-call(s32[4]{0:T(128)S(1)} %pad_add_fusion.info, ...), custom_call_target="tpu_custom_call", output_to_operand_aliasing={{0}: (8, {}), {1}: (9, {}), {2}: (10, {}), {3}: (11, {}), {... | custom-call | bytes 12000000 | tf_op jit(solution)/shard_map/pallas_call | solution.py:515
  21.9 3.8 %collective-permute-done.1 = bf16[2,8,32,128]{3,2,1,0:T(8,128)(2,1)S(1)} collective-permute-done((bf16[2,8,32,128]{3,2,1,0:T(8,128)(2,1)S(1)}, bf16[2,8,32,128]{3,2,1,0:T(8,128)(2,1)S(1)}, u32[]{:S(2)}, u32[]{:S(2)}) %collective-permute-start.1) | collective-permute-done | bytes 131104 | tf_op jit(solution)/shard_map/ppermute | solution.py:569
  25.7 0.1 collective-permute-start.3
  25.8 6.4 %collective-permute-done.3 = bf16[2,8,64,128]{3,2,1,0:T(8,128)(2,1)S(1)} collective-permute-done((bf16[2,8,64,128]{3,2,1,0:T(8,128)(2,1)S(1)}, bf16[2,8,64,128]{3,2,1,0:T(8,128)(2,1)S(1)}, u32[]{:S(2)}, u32[]{:S(2)}) %collective-permute-start.3) | collective-permute-done | bytes 262176 | tf_op jit(solution)/shard_map/ppermute | solution.py:569
  32.2 0.0 collective-permute-done.2.kv_ref
  32.2 0.0 copy-start
  32.2 0.0 copy-start.4
  32.2 3.8 %shard_map.105 = (f32[8,512,128]{2,1,0:T(8,128)S(1)}, f32[8,512,128]{2,1,0:T(8,128)S(1)}, f32[4,512,128]{2,1,0:T(8,128)S(1)}, bf16[4,512,512]{2,1,0:T(8,128)(2,1)S(1)}, f32[4,512,128]{2,1,0:T(8,128)S(1)}) custom-call(s32[4]{0:T(128)S(1)} %pad_add_fusion.info, ...), custom_call_target="tpu_custom_call", output_to_operand_aliasing={{0}: (4, {}), {1}: (6, {})} | custom-call | bytes 12000000 | tf_op jit(solution)/shard_map/pallas_call | solution.py:515
  36.1 5.8 %collective-permute-start.4 = (bf16[2,8,128,128]{3,2,1,0:T(8,128)(2,1)S(1)}, bf16[2,8,128,128]{3,2,1,0:T(8,128)(2,1)S(1)}, u32[]{:S(2)}, u32[]{:S(2)}) collective-permute-start(bf16[2,8,128,128]{3,2,1,0:T(8,128)(2,1)S(1)} %pad_maximum_fusion.1.ga_ref), channel_id=1, source_target_pairs={{0,2},{2,0},{4,6},{6,4},{8,10},{10,8},{12,14},{14,12},{16,18},{18,... | collective-permute-start | bytes 1572872 | tf_op jit(solution)/shard_map/ppermute | solution.py:569
  41.9 1.5 %collective-permute-done.4.gb_ref = bf16[2,8,128,128]{3,2,1,0:T(8,128)(2,1)S(1)} collective-permute-done((bf16[2,8,128,128]{3,2,1,0:T(8,128)(2,1)S(1)}, bf16[2,8,128,128]{3,2,1,0:T(8,128)(2,1)S(1)}, u32[]{:S(2)}, u32[]{:S(2)}) %collective-permute-start.4) | collective-permute-done | bytes 524320 | tf_op jit(solution)/shard_map/ppermute | solution.py:569
  43.4 0.0 copy-done
  43.4 0.0 copy-done.4
  43.4 5.8 %shard_map.106 = (bf16[8,512,128]{2,1,0:T(8,128)(2,1)S(1)}, f32[8,512,128]{2,1,0:T(8,128)S(1)}, bf16[8,16,256]{2,1,0:T(8,128)(2,1)S(1)}, f32[8,16,128]{2,1,0:T(8...) custom-call(s32[4]{0:T(128)S(1)} %pad_add_fusion.info, ...), custom_call_target="tpu_custom_call" | custom-call | bytes 12000000 | tf_op jit(solution)/shard_map/pallas_call | solution.py:515
  49.2 1.5 %collective-permute-start.5 = (f32[8,128]{1,0:T(8,128)S(1)}, f32[8,128]{1,0:T(8,128)S(1)}, u32[]{:S(2)}, u32[]{:S(2)}) collective-permute-start(f32[8,128]{1,0:T(8,128)S(1)} %get-tuple-element.79.stat_ref), channel_id=1, source_target_pairs={{0,1},{1,0},{2,3},{3,2},{4,5},{5,4},{6,7},{7,6},{8,9},{9,8},{10,11... | collective-permute-start | bytes 12296 | tf_op jit(solution)/shard_map/ppermute | solution.py:666
  50.8 2.1 %collective-permute-done.5.other_ref = f32[8,128]{1,0:T(8,128)S(1)} collective-permute-done((f32[8,128]{1,0:T(8,128)S(1)}, f32[8,128]{1,0:T(8,128)S(1)}, u32[]{:S(2)}, u32[]{:S(2)}) %collective-permute-start.5) | collective-permute-done | bytes 4128 | tf_op jit(solution)/shard_map/ppermute | solution.py:666
  52.9 1.1 %shard_map.107 = bf16[3,8,16,128]{3,2,1,0:T(8,128)(2,1)S(1)} custom-call(s32[8]{0:T(128)S(1)} %copy-done.5, f32[4,128]{1,0:T(4,128)S(1)} %get-tuple-element.108.begin_ref, f32[8,128]{1,0:T(8,128)S(1)} %get-tuple-element.79.stat_ref, f32[8,128]{1,0:T(8,128)S(1)} %collective-permute-done.5.other_ref, bf16[8,16,128]{2,1,0:T(8,128)(2,1)S(1)} %get-tuple-element.80.ar_ref, ...), custom_call_target="tpu_custom_call" | custom-call | bytes 12000000 | tf_op jit(solution)/shard_map/pallas_call | solution.py:515
  54.0 2.2 %collective-permute-start.6 = (bf16[3,8,16,128]{3,2,1,0:T(8,128)(2,1)S(1)}, bf16[3,8,16,128]{3,2,1,0:T(8,128)(2,1)S(1)}, u32[]{:S(2)}, u32[]{:S(2)}) collective-permute-start(bf16[3,8,16,128]{3,2,1,0:T(8,128)(2,1)S(1)} %shard_map.107), channel_id=1, source_target_pairs={{0,8},{2,10},{4,12},{6,14},{8,0},{10,2},{12,4},{14,6},{16,24},{18,... | collective-permute-start | bytes 294920 | tf_op jit(solution)/shard_map/ppermute | solution.py:569
  56.2 4.5 %shard_map.108 = (bf16[2,4,512,128]{3,2,1,0:T(8,128)(2,1)S(1)}, f32[4,512,128]{2,1,0:T(8,128)S(1)}) custom-call(s32[4]{0:T(128)S(1)} %pad_add_fusion.info, f32[8,128]{1,0:T(8,128)S(1)} %get-tuple-element.79.stat_ref, f32[8,128]{1,0:T(8,128)S(1)} %collective-permute-done.5.other_ref, bf16[8,512,128]{2,1,0:T(8,128)(2,1)S(1)} %get-tuple-element.69.q_ref, ...), custom_call_target="tpu_custom_call" | custom-call | bytes 12000000 | tf_op jit(solution)/shard_map/pallas_call | solution.py:515
  60.7 0.0 collective-permute-done.6
  60.7 2.4 %collective-permute-start.7 = (bf16[3,8,32,128]{3,2,1,0:T(8,128)(2,1)S(1)}, bf16[3,8,32,128]{3,2,1,0:T(8,128)(2,1)S(1)}, u32[]{:S(2)}, u32[]{:S(2)}) collective-permute-start(bf16[3,8,32,128]{3,2,1,0:T(8,128)(2,1)S(1)} %pad_maximum_fusion.4), channel_id=1, source_target_pairs={{0,16},{2,18},{4,20},{6,22},{8,24},{10,26},{12,28},{14,30},{16,0},... | collective-permute-start | bytes 589832 | tf_op jit(solution)/shard_map/ppermute | solution.py:569
  63.1 6.7 %shard_map.109 = (bf16[8,512,128]{2,1,0:T(8,128)(2,1)}, bf16[8,512,128]{2,1,0:T(8,128)(2,1)}, f32[8,512,128]{2,1,0:T(8,128)S(1)}, f32[8,512,128]{2,1,0:T(8,128)S(1)}) custom-call(s32[4]{0:T(128)S(1)} %pad_add_fusion.info, s32[8]{0:T(128)S(1)} %copy-done.5, f32[8,128]{1,0:T(8,128)S(1)} %get-tuple-element.79.stat_ref, ...), custom_call_target="tpu_custom_call" | custom-call | bytes 12000000 | tf_op jit(solution)/shard_map/pallas_call | solution.py:515
  69.8 1.5 %collective-permute-done.7 = bf16[3,8,32,128]{3,2,1,0:T(8,128)(2,1)S(1)} collective-permute-done((bf16[3,8,32,128]{3,2,1,0:T(8,128)(2,1)S(1)}, bf16[3,8,32,128]{3,2,1,0:T(8,128)(2,1)S(1)}, u32[]{:S(2)}, u32[]{:S(2)}) %collective-permute-start.7) | collective-permute-done | bytes 196640 | tf_op jit(solution)/shard_map/ppermute | solution.py:569
  71.4 1.8 %collective-permute-start.9 = (bf16[3,8,64,128]{3,2,1,0:T(8,128)(2,1)S(1)}, bf16[3,8,64,128]{3,2,1,0:T(8,128)(2,1)S(1)}, u32[]{:S(2)}, u32[]{:S(2)}) collective-permute-start(bf16[3,8,64,128]{3,2,1,0:T(8,128)(2,1)S(1)} %pad_maximum_fusion.2), channel_id=1, source_target_pairs={{0,4},{2,6},{4,0},{6,2},{8,12},{10,14},{12,8},{14,10},{16,20},{18,... | collective-permute-start | bytes 1179656 | tf_op jit(solution)/shard_map/ppermute | solution.py:569
  73.2 1.3 %collective-permute-start.8 = (bf16[2,4,512,128]{3,2,1,0:T(8,128)(2,1)S(1)}, bf16[2,4,512,128]{3,2,1,0:T(8,128)(2,1)S(1)}, u32[]{:S(2)}, u32[]{:S(2)}) collective-permute-start(bf16[2,4,512,128]{3,2,1,0:T(8,128)(2,1)S(1)} %get-tuple-element.102), channel_id=1, source_target_pairs={{2,0},{4,2},{6,4},{8,6},{10,8},{12,10},{14,12},{16,14},{18,16},{20... | collective-permute-start | bytes 3145736 | tf_op jit(solution)/shard_map/ppermute | solution.py:696
  74.5 7.5 %shard_map.110 = (bf16[8,512,128]{2,1,0:T(8,128)(2,1)}, bf16[8,512,128]{2,1,0:T(8,128)(2,1)}, f32[8,512,128]{2,1,0:T(8,128)S(1)}, f32[8,512,128]{2,1,0:T(8,128)S(1)}) custom-call(s32[4]{0:T(128)S(1)} %pad_add_fusion.info, s32[8]{0:T(128)S(1)} %copy-done.5, ...), custom_call_target="tpu_custom_call", output_to_operand_aliasing={{0}: (19, {}), {1}: (20, {}), {2}: (21, {}), {3}: (22, {})} | custom-call | bytes 12000000 | tf_op jit(solution)/shard_map/pallas_call | solution.py:515
  82.0 11.0 %collective-permute-done.9 = bf16[3,8,64,128]{3,2,1,0:T(8,128)(2,1)S(1)} collective-permute-done((bf16[3,8,64,128]{3,2,1,0:T(8,128)(2,1)S(1)}, bf16[3,8,64,128]{3,2,1,0:T(8,128)(2,1)S(1)}, u32[]{:S(2)}, u32[]{:S(2)}) %collective-permute-start.9) | collective-permute-done | bytes 393248 | tf_op jit(solution)/shard_map/ppermute | solution.py:569
  93.0 0.1 pad_maximum_fusion.sa_ref
  93.1 0.1 collective-permute-start.10
  93.2 0.0 collective-permute-done.8.back_ref
  93.2 2.3 %collective-permute-done.10.sb_ref = bf16[3,8,128,128]{3,2,1,0:T(8,128)(2,1)S(1)} collective-permute-done((bf16[3,8,128,128]{3,2,1,0:T(8,128)(2,1)S(1)}, bf16[3,8,128,128]{3,2,1,0:T(8,128)(2,1)S(1)}, u32[]{:S(2)}, u32[]{:S(2)}) %collective-permute-start.10) | collective-permute-done | bytes 786464 | tf_op jit(solution)/shard_map/ppermute | solution.py:569
  95.4 5.2 %shard_map.111 = (bf16[8,512,128]{2,1,0:T(8,128)(2,1)}, bf16[8,512,128]{2,1,0:T(8,128)(2,1)}) custom-call(s32[4]{0:T(128)S(1)} %pad_add_fusion.info, s32[8]{0:T(128)S(1)} %copy-done.5, f32[8,512,128]{2,1,0:T(8,128)S(1)} %get-tuple-element.100.dk_ref, f32[8,512,128]{2,1,0:T(8,128)S(1)} %get-tuple-element.101.dv_ref, ...), custom_call_target="tpu_custom_call" | custom-call | bytes 12000000 | tf_op jit(solution)/shard_map/pallas_call | solution.py:515
  (8 shorter events, 0.1 us)
Async XLA Ops:
  0.6 11.9 %copy-start.1 = (bf16[8,512,128]{2,1,0:T(8,128)(2,1)S(1)}, bf16[8,512,128]{2,1,0:T(8,128)(2,1)}, u32[]{:S(2)}) copy-start(bf16[8,512,128]{2,1,0:T(8,128)(2,1)} %q_ref.2) | copy-start | bytes 3145732
  2.3 1.2 %copy-start.2 = (bf16[8,512,128]{2,1,0:T(8,128)(2,1)S(1)}, bf16[8,512,128]{2,1,0:T(8,128)(2,1)}, u32[]{:S(2)}) copy-start(bf16[8,512,128]{2,1,0:T(8,128)(2,1)} %k_ref.1) | copy-start | bytes 3145732
  3.5 1.2 %copy-start.3 = (bf16[8,512,128]{2,1,0:T(8,128)(2,1)S(1)}, bf16[8,512,128]{2,1,0:T(8,128)(2,1)}, u32[]{:S(2)}) copy-start(bf16[8,512,128]{2,1,0:T(8,128)(2,1)} %v_ref.1) | copy-start | bytes 3145732
  4.7 0.7 copy-start.5
  7.5 24.7 %collective-permute-start.2 = (bf16[2,4,512,128]{3,2,1,0:T(8,128)(2,1)S(1)}, bf16[2,4,512,128]{3,2,1,0:T(8,128)(2,1)S(1)}, u32[]{:S(2)}, u32[]{:S(2)}) collective-permute-start(bf16[2,4,512,128]{3,2,1,0:T(8,128)(2,1)S(1)} %get-tuple-element.70), channel_id=1, source_target_pairs={{0,2},{2,4},{4,6},{6,8},{8,10},{10,12},{12,14},{14,16},{16,18},{18... | collective-permute-start | bytes 3145736 | tf_op jit(solution)/shard_map/ppermute | solution.py:584
  10.0 5.9 %collective-permute-start = (bf16[2,8,16,128]{3,2,1,0:T(8,128)(2,1)S(1)}, bf16[2,8,16,128]{3,2,1,0:T(8,128)(2,1)S(1)}, u32[]{:S(2)}, u32[]{:S(2)}) collective-permute-start(bf16[2,8,16,128]{3,2,1,0:T(8,128)(2,1)S(1)} %get-tuple-element.55.rows_ref), channel_id=1, source_target_pairs={{0,8},{2,10},{4,12},{6,14},{8,0},{10,2},{12,4},{14,6},{16,24},{18,... | collective-permute-start | bytes 196616 | tf_op jit(solution)/shard_map/ppermute | solution.py:569
  15.9 9.8 %collective-permute-start.1 = (bf16[2,8,32,128]{3,2,1,0:T(8,128)(2,1)S(1)}, bf16[2,8,32,128]{3,2,1,0:T(8,128)(2,1)S(1)}, u32[]{:S(2)}, u32[]{:S(2)}) collective-permute-start(bf16[2,8,32,128]{3,2,1,0:T(8,128)(2,1)S(1)} %pad_maximum_fusion.6), channel_id=1, source_target_pairs={{0,16},{2,18},{4,20},{6,22},{8,24},{10,26},{12,28},{14,30},{16,0},... | collective-permute-start | bytes 393224 | tf_op jit(solution)/shard_map/ppermute | solution.py:569
  25.7 6.4 %collective-permute-start.3 = (bf16[2,8,64,128]{3,2,1,0:T(8,128)(2,1)S(1)}, bf16[2,8,64,128]{3,2,1,0:T(8,128)(2,1)S(1)}, u32[]{:S(2)}, u32[]{:S(2)}) collective-permute-start(bf16[2,8,64,128]{3,2,1,0:T(8,128)(2,1)S(1)} %pad_maximum_fusion.3), channel_id=1, source_target_pairs={{0,4},{2,6},{4,0},{6,2},{8,12},{10,14},{12,8},{14,10},{16,20},{18,... | collective-permute-start | bytes 786440 | tf_op jit(solution)/shard_map/ppermute | solution.py:569
  32.2 11.2 %copy-start = (bf16[8,512,128]{2,1,0:T(8,128)(2,1)S(1)}, bf16[8,512,128]{2,1,0:T(8,128)(2,1)}, u32[]{:S(2)}) copy-start(bf16[8,512,128]{2,1,0:T(8,128)(2,1)} %og_ref.7) | copy-start | bytes 3145732
  32.2 11.2 %copy-start.4 = (f32[8,128]{1,0:T(8,128)S(1)}, f32[8,128]{1,0:T(8,128)}, u32[]{:S(2)}) copy-start(f32[8,128]{1,0:T(8,128)} %param.11) | copy-start | bytes 12292
  36.1 7.3 %collective-permute-start.4 = (bf16[2,8,128,128]{3,2,1,0:T(8,128)(2,1)S(1)}, bf16[2,8,128,128]{3,2,1,0:T(8,128)(2,1)S(1)}, u32[]{:S(2)}, u32[]{:S(2)}) collective-permute-start(bf16[2,8,128,128]{3,2,1,0:T(8,128)(2,1)S(1)} %pad_maximum_fusion.1.ga_ref), channel_id=1, source_target_pairs={{0,2},{2,0},{4,6},{6,4},{8,10},{10,8},{12,14},{14,12},{16,18},{18,... | collective-permute-start | bytes 1572872 | tf_op jit(solution)/shard_map/ppermute | solution.py:569
  49.2 3.7 %collective-permute-start.5 = (f32[8,128]{1,0:T(8,128)S(1)}, f32[8,128]{1,0:T(8,128)S(1)}, u32[]{:S(2)}, u32[]{:S(2)}) collective-permute-start(f32[8,128]{1,0:T(8,128)S(1)} %get-tuple-element.79.stat_ref), channel_id=1, source_target_pairs={{0,1},{1,0},{2,3},{3,2},{4,5},{5,4},{6,7},{7,6},{8,9},{9,8},{10,11... | collective-permute-start | bytes 12296 | tf_op jit(solution)/shard_map/ppermute | solution.py:666
  54.0 6.7 %collective-permute-start.6 = (bf16[3,8,16,128]{3,2,1,0:T(8,128)(2,1)S(1)}, bf16[3,8,16,128]{3,2,1,0:T(8,128)(2,1)S(1)}, u32[]{:S(2)}, u32[]{:S(2)}) collective-permute-start(bf16[3,8,16,128]{3,2,1,0:T(8,128)(2,1)S(1)} %shard_map.107), channel_id=1, source_target_pairs={{0,8},{2,10},{4,12},{6,14},{8,0},{10,2},{12,4},{14,6},{16,24},{18,... | collective-permute-start | bytes 294920 | tf_op jit(solution)/shard_map/ppermute | solution.py:569
  60.7 10.7 %collective-permute-start.7 = (bf16[3,8,32,128]{3,2,1,0:T(8,128)(2,1)S(1)}, bf16[3,8,32,128]{3,2,1,0:T(8,128)(2,1)S(1)}, u32[]{:S(2)}, u32[]{:S(2)}) collective-permute-start(bf16[3,8,32,128]{3,2,1,0:T(8,128)(2,1)S(1)} %pad_maximum_fusion.4), channel_id=1, source_target_pairs={{0,16},{2,18},{4,20},{6,22},{8,24},{10,26},{12,28},{14,30},{16,0},... | collective-permute-start | bytes 589832 | tf_op jit(solution)/shard_map/ppermute | solution.py:569
  71.4 21.6 %collective-permute-start.9 = (bf16[3,8,64,128]{3,2,1,0:T(8,128)(2,1)S(1)}, bf16[3,8,64,128]{3,2,1,0:T(8,128)(2,1)S(1)}, u32[]{:S(2)}, u32[]{:S(2)}) collective-permute-start(bf16[3,8,64,128]{3,2,1,0:T(8,128)(2,1)S(1)} %pad_maximum_fusion.2), channel_id=1, source_target_pairs={{0,4},{2,6},{4,0},{6,2},{8,12},{10,14},{12,8},{14,10},{16,20},{18,... | collective-permute-start | bytes 1179656 | tf_op jit(solution)/shard_map/ppermute | solution.py:569
  73.2 19.9 %collective-permute-start.8 = (bf16[2,4,512,128]{3,2,1,0:T(8,128)(2,1)S(1)}, bf16[2,4,512,128]{3,2,1,0:T(8,128)(2,1)S(1)}, u32[]{:S(2)}, u32[]{:S(2)}) collective-permute-start(bf16[2,4,512,128]{3,2,1,0:T(8,128)(2,1)S(1)} %get-tuple-element.102), channel_id=1, source_target_pairs={{2,0},{4,2},{6,4},{8,6},{10,8},{12,10},{14,12},{16,14},{18,16},{20... | collective-permute-start | bytes 3145736 | tf_op jit(solution)/shard_map/ppermute | solution.py:696
  93.1 2.4 %collective-permute-start.10 = (bf16[3,8,128,128]{3,2,1,0:T(8,128)(2,1)S(1)}, bf16[3,8,128,128]{3,2,1,0:T(8,128)(2,1)S(1)}, u32[]{:S(2)}, u32[]{:S(2)}) collective-permute-start(bf16[3,8,128,128]{3,2,1,0:T(8,128)(2,1)S(1)} %pad_maximum_fusion.sa_ref), channel_id=1, source_target_pairs={{0,2},{2,0},{4,6},{6,4},{8,10},{10,8},{12,14},{14,12},{16,18},{18,... | collective-permute-start | bytes 2359304 | tf_op jit(solution)/shard_map/ppermute | solution.py:569

commit v3 on v2

v3 whole, which is shorter than its diff:
```python
import math

import jax
import jax.numpy as jnp
from jax import lax
from jax.experimental import pallas as pl
from jax.experimental.pallas import tpu as pltpu
from jax.sharding import PartitionSpec as P

HEADS = 16
SEL = 256
theta_base = 10000.0
eps_norm = 1e-06
NEG = -1e30
f32 = jnp.float32
bf16 = jnp.bfloat16


def dot_nn(a, b):
    return lax.dot_general(a, b, (((1,), (0,)), ((), ())), preferred_element_type=f32)


def dot_nt(a, b):
    return lax.dot_general(a, b, (((1,), (1,)), ((), ())), preferred_element_type=f32)


def dot_tn(a, b):
    return lax.dot_general(a, b, (((0,), (0,)), ((), ())), preferred_element_type=f32)


def lanes_of(shape):
    return lax.broadcasted_iota(jnp.int32, shape, len(shape) - 1)


def rows_of(shape):
    return lax.broadcasted_iota(jnp.int32, shape, len(shape) - 2)


def low_half(x):
    return jnp.where(lanes_of(x.shape) < 64, x, pltpu.roll(x, 64, 1))


def high_half(x):
    return jnp.where(lanes_of(x.shape) < 64, pltpu.roll(x, 64, 1), x)


def unpack_tables(cos_ref, sin_ref):
    c, s = cos_ref[...], sin_ref[...]
    cos = jnp.concatenate([low_half(c), high_half(c)], axis=0)
    sin = jnp.concatenate([low_half(s), high_half(s)], axis=0)
    sin = jnp.where(lanes_of(sin.shape) < 64, -sin, sin)
    return cos, sin


def rot(x, cos, sin):
    return x * cos + pltpu.roll(x, 64, 1) * sin


def spread(row):
    parts = []
    for i in range(row.shape[0]):
        parts.append(jnp.broadcast_to(row[i : i + 1, :], (128, 128)).T)
    return jnp.concatenate(parts, axis=0)


def compact(x):
    eye = rows_of((128, 128)) == lanes_of((128, 128))
    parts = []
    for i in range(x.shape[0] // 128):
        block = x[i * 128 : (i + 1) * 128, :]
        parts.append(jnp.sum(jnp.where(eye, block, 0.0), axis=0, keepdims=True))
    return jnp.concatenate(parts, axis=0)


def row_sum(x):
    return jnp.broadcast_to(jnp.sum(x, axis=1, keepdims=True), x.shape)


def prep_kernel(info, k_ref, v_ref, cos_ref, sin_ref, kr_ref, rows_ref):
    g = pl.program_id(0)
    tok = k_ref.shape[1]
    nb = rows_ref.shape[2]
    rate = tok // nb
    cos, sin = unpack_tables(cos_ref, sin_ref)
    for hh in range(2):
        h = 2 * g + hh
        hot = (lanes_of((nb, tok)) == info[4 + h] + rate * rows_of((nb, tok))).astype(bf16)
        kr = rot(k_ref[h].astype(f32), cos, sin).astype(bf16)
        kr_ref[h] = kr
        rows_ref[0, hh] = dot_nn(hot, kr).astype(bf16)
        rows_ref[1, hh] = dot_nn(hot, v_ref[h]).astype(bf16)


def make_own_kernel(first, aliased):
    def own_kernel(info, start_ref, q_ref, k_ref, v_ref, cos_ref, sin_ref, *refs):
        refs = refs[aliased:]
        qr_ref, e_ref, acc_ref, m_ref, l_ref, rows_ref, bias_ref = refs
        tok = q_ref.shape[1]
        nb = rows_ref.shape[1]
        rate = tok // nb
        half = tok // 2
        scale = 1.0 / math.sqrt(q_ref.shape[2])

        @pl.when(pl.program_id(0) == 0)
        def _():
            start = spread(start_ref[...])
            for c in range(tok // 128):
                key = lanes_of((tok, 128)) + c * 128
                ok = (key <= rows_of((tok, 128))) & (key.astype(f32) >= start)
                bias_ref[:, c * 128 : (c + 1) * 128] = jnp.where(ok, 0.0, NEG)

        cos, sin = unpack_tables(cos_ref, sin_ref)
        for hh in range(2):
            h = 2 * (pl.program_id(0) + first) + hh
            q = rot(q_ref[hh].astype(f32), cos, sin).astype(bf16)
            qr_ref[h] = q
            hot = (lanes_of((nb, tok)) == info[4 + h] + rate * rows_of((nb, tok))).astype(bf16)
            rows_ref[hh] = dot_nn(hot, q).astype(bf16)
            vals = jnp.concatenate([v_ref[h], jnp.ones((tok, 128), bf16)], axis=1)
            for c in range(2):
                lo, n = c * half, (c + 1) * half
                z = dot_nt(q[lo:n], k_ref[h, :n, :]) * scale + bias_ref[lo:n, :n]
                m = jnp.max(z, axis=1, keepdims=True)
                e = jnp.exp(z - m).astype(bf16)
                e_ref[h, lo:n, :n] = e
                out = dot_nn(e, vals[:n])
                acc_ref[h, lo:n, :] = out[:, :128]
                l_ref[h, lo:n, :] = out[:, 128:]
                m_ref[h, lo:n, :] = jnp.broadcast_to(m, (half, 128))

    return own_kernel


def split3(x):
    hi = x.astype(bf16).astype(f32)
    mid = (x - hi).astype(bf16).astype(f32)
    return hi, mid, x - hi - mid


def pack3(parts, rows):
    stack = [p for x in parts for p in split3(x)]
    used = sum(p.shape[0] for p in stack)
    if used < rows:
        stack.append(jnp.zeros((rows - used, 128), f32))
    return jnp.concatenate(stack, axis=0).astype(bf16)


def unpack3(block, n, which):
    x = block.astype(f32)
    i = 3 * n * which
    return x[i : i + n] + x[i + n : i + 2 * n] + x[i + 2 * n : i + 3 * n]


def next_kernel(info, start_ref, q_ref, k_ref, v_ref, cos_ref, sin_ref, o_ref, e_ref, qn_ref, bias_ref, m_s, l_s):
    g = pl.program_id(0)
    tok = q_ref.shape[1]
    half = tok // 2
    scale = 1.0 / math.sqrt(q_ref.shape[2])
    h = 2 * g + info[1]

    @pl.when(g == 0)
    def _():
        start = spread(start_ref[...])
        for c in range(tok // 128):
            key = (lanes_of((tok, 128)) + c * 128).astype(f32)
            bias_ref[:, c * 128 : (c + 1) * 128] = jnp.where(key >= start, 0.0, NEG)

    cos, sin = unpack_tables(cos_ref, sin_ref)
    q = rot(q_ref[0].astype(f32), cos, sin).astype(bf16)
    qn_ref[g] = q
    vals = jnp.concatenate([v_ref[h], jnp.ones((tok, 128), bf16)], axis=1)
    for c in range(2):
        sl = slice(c * half, (c + 1) * half)
        z = dot_nt(q[sl], k_ref[h]) * scale + bias_ref[sl, :]
        m = jnp.max(z, axis=1, keepdims=True)
        e = jnp.exp(z - m).astype(bf16)
        e_ref[g, sl, :] = e
        out = dot_nn(e, vals)
        o_ref[0, sl, :] = out[:, :128].astype(bf16)
        m_s[sl, :] = jnp.broadcast_to(m, (half, 128))
        l_s[sl, :] = out[:, 128:]
    o_ref[0, tok:, :] = pack3((compact(m_s[...]), compact(l_s[...])), o_ref.shape[1] - tok)


def key_order(index, codes, nb, part, count):
    col = lanes_of((1, count)) + part * count
    slot = col // nb
    dev = jnp.full((1, count), index, jnp.int32)
    for b, code in enumerate(codes):
        dev = dev ^ (((slot >> b) & 1) * code)
    return dev * nb + col % nb


def make_join_kernel(codes):
    def join_kernel(
        info, start_ref, acc_ref, m_ref, l_ref, on_ref, q1_ref, ga_ref, gb_ref, og_ref, gain_ref,
        attn_ref, rr_ref, e1_ref, rs_ref, ar_ref, or_ref, stat_ref,
        start_s, m_s, l_s, acc_s, sq_s, cr_s,
    ):
        g = pl.program_id(0)
        index, sel = info[0], info[2]
        tok = og_ref.shape[1]
        nb = q1_ref.shape[1]
        rate = tok // nb
        count = ga_ref.shape[2]
        scale = 1.0 / math.sqrt(og_ref.shape[2])

        @pl.when(g == 0)
        def _():
            start_s[...] = spread(start_ref[...])
            sq_s[...] = jnp.zeros_like(sq_s)
            cr_s[...] = jnp.zeros_like(cr_s)

        stats = on_ref[0, tok:, :]
        n = tok // 128
        ok = index > 0
        m_prev = jnp.where(ok, spread(unpack3(stats, n, 0)), NEG)
        l_prev = spread(unpack3(stats, n, 1))
        m_own = m_ref[2 * g + sel]
        mn = jnp.maximum(m_own, m_prev)
        a_own = jnp.exp(m_own - mn)
        a_prev = jnp.where(ok, jnp.exp(m_prev - mn), 0.0)
        m_s[sel] = mn
        l_s[sel] = a_own * l_ref[2 * g + sel] + a_prev * l_prev
        acc_s[sel] = a_own * acc_ref[2 * g + sel] + a_prev * on_ref[0, :tok, :].astype(f32)
        m_s[1 - sel] = m_ref[2 * g + 1 - sel]
        l_s[1 - sel] = l_ref[2 * g + 1 - sel]
        acc_s[1 - sel] = acc_ref[2 * g + 1 - sel]

        for hh in range(2):
            h = 2 * g + hh
            off = info[4 + h]
            rows = pl.ds(off, nb, stride=rate)
            here = sel == hh
            m_own = m_ref[h]

            q1 = q1_ref[hh]
            start1 = start_s[rows, :][:, :1]
            qb = index * nb + rows_of((nb, count))
            zs = []
            for part, ref in enumerate((ga_ref, gb_ref)):
                kb = key_order(index, codes, nb, part, count)
                pos = (off + rate * kb - index * tok).astype(f32)
                ok = (kb <= qb) & (pos >= start1)
                zs.append(jnp.where(ok, dot_nt(q1, ref[0, hh]) * scale, NEG))
            m1 = jnp.maximum(jnp.max(zs[0], axis=1, keepdims=True), jnp.max(zs[1], axis=1, keepdims=True))
            o1 = jnp.zeros((nb, 256), f32)
            for part, ref in enumerate((ga_ref, gb_ref)):
                e1 = jnp.exp(zs[part] - m1).astype(bf16)
                e1_ref[hh, :, part * count : (part + 1) * count] = e1
                v1 = jnp.concatenate([ref[1, hh], jnp.ones((count, 128), bf16)], axis=1)
                o1 = o1 + dot_nn(e1, v1)

            mr = m_s[hh, rows, :]
            lr = l_s[hh, rows, :]
            ar = acc_s[hh, rows, :]
            m1b = jnp.broadcast_to(m1, (nb, 128))
            mn = jnp.maximum(mr, m1b)
            b0 = jnp.exp(mr - mn)
            b1 = jnp.exp(m1b - mn)
            ln = b0 * lr + b1 * o1[:, 128:]
            m_s[hh, rows, :] = mn
            l_s[hh, rows, :] = ln
            acc_s[hh, rows, :] = b0 * ar + b1 * o1[:, :128]
            lse1 = mn + jnp.log(ln)
            rs_ref[hh] = jnp.where(lanes_of((nb, 128)) < 64, lse1, b1 / ln)

            inv = 1.0 / l_s[hh]
            attn = (acc_s[hh] * inv).astype(bf16)
            attn_ref[h] = attn
            both = jnp.where((lanes_of((tok, 128)) < 64) | jnp.logical_not(here), m_own, m_prev)
            rr_ref[h] = jnp.exp(both - m_s[hh]) * inv
            af = attn.astype(f32)
            gd = og_ref[hh].astype(f32) * gain_ref[hh]
            sq_s[...] += af * af
            cr_s[...] += gd * af
            hot = (lanes_of((nb, tok)) == off + rate * rows_of((nb, tok))).astype(bf16)
            ar_ref[hh] = dot_nn(hot, attn).astype(bf16)
            or_ref[hh] = dot_nn(hot, og_ref[hh]).astype(bf16)

        @pl.when(g == pl.num_programs(0) - 1)
        def _():
            stat_ref[...] = jnp.concatenate([compact(row_sum(sq_s[...])), compact(row_sum(cr_s[...]))], axis=0)

    return join_kernel


def norm_terms(stat_ref, other_ref, feats):
    total = stat_ref[...] + other_ref[...]
    n = total.shape[0] // 2
    rinv = lax.rsqrt(total[:n] / feats + eps_norm)
    return rinv, rinv * rinv * total[n:] / feats


def split3(x):
    hi = x.astype(bf16).astype(f32)
    mid = (x - hi).astype(bf16).astype(f32)
    return hi, mid, x - hi - mid


def grad_terms(attn, og, gain, rinv, cc):
    af = attn.astype(f32)
    gd = og.astype(f32) * gain
    ag = (rinv * (gd - af * cc)).astype(bf16).astype(f32)
    return af, ag, row_sum(ag * af)


def make_rows_kernel(feats):
    def rows_kernel(
        info, begin_ref, stat_ref, other_ref, ar_ref, or_ref, q1_ref, gain_ref, rs_ref, attn_ref, rr_ref, og_ref,
        out_ref, st_ref, do_ref, rinv_s, cc_s, st_s,
    ):
        g = pl.program_id(0)
        sel = info[2]
        nb = ar_ref.shape[1]
        tok = og_ref.shape[1]
        rate = tok // nb

        @pl.when(g == 0)
        def _():
            rinv, cc = norm_terms(stat_ref, other_ref, feats)
            rinv_s[...] = spread(rinv)
            cc_s[...] = spread(cc)
            st_s[...] = spread(begin_ref[...])
            st_ref[...] = jnp.zeros_like(st_ref)

        for hh in range(2):
            rows = pl.ds(info[4 + 2 * g + hh], nb, stride=rate)
            af = ar_ref[hh].astype(f32)
            gd = or_ref[hh].astype(f32) * gain_ref[hh]
            ag = (rinv_s[rows, :] * (gd - af * cc_s[rows, :])).astype(bf16)
            delta = row_sum(ag.astype(f32) * af)
            out_ref[0, hh] = ag
            lane = lanes_of((nb, 128))
            spot = lane == (2 * g + hh) * nb + rows_of((nb, 128))
            for i, x in enumerate(split3(low_half(rs_ref[hh])) + split3(delta) + split3(st_s[rows, :])):
                st_ref[i : i + 1, :] += jnp.sum(jnp.where(spot, x, 0.0), axis=0, keepdims=True)
            out_ref[1, hh] = q1_ref[hh]

        h = 2 * g + sel
        af, ag, delta = grad_terms(attn_ref[h], og_ref[0], gain_ref[sel], rinv_s[...], cc_s[...])
        r = high_half(rr_ref[h])
        do_ref[0, :tok, :] = (ag * r).astype(bf16)
        do_ref[0, tok:, :] = pack3((compact(delta * r),), do_ref.shape[1] - tok)

    return rows_kernel


def next_back_kernel(info, do_ref, q_ref, k_ref, v_ref, e_ref, dq_ref, dk_ref, dv_ref):
    g = pl.program_id(0)
    h = 2 * g + info[1]
    tok = q_ref.shape[1]
    half = tok // 2
    scale = 1.0 / math.sqrt(q_ref.shape[2])
    dl = spread(unpack3(do_ref[0, tok:, :], tok // 128, 0))
    dk = jnp.zeros((128, tok), f32)
    dv = jnp.zeros((128, tok), f32)
    for c in range(2):
        sl = slice(c * half, (c + 1) * half)
        e = e_ref[g, sl, :]
        do = do_ref[0, sl, :]
        dp = dot_nt(do, v_ref[h])
        ds = (e.astype(f32) * (dp - jnp.concatenate([dl[sl]] * (tok // 128), axis=1))).astype(bf16)
        dq_ref[0, sl, :] = (dot_nn(ds, k_ref[h]) * scale).astype(bf16)
        dk = dk + dot_tn(q_ref[g, sl, :], ds)
        dv = dv + dot_tn(do, e)
    dk_ref[g] = dk.T
    dv_ref[g] = dv.T


def make_back_own_kernel(feats, first, aliased):
    def back_own_kernel(
        info, stat_ref, other_ref, q_ref, k_ref, v_ref, attn_ref, rr_ref, e_ref,
        og_ref, gain_ref, e1_ref, rs_ref, ga_ref, gb_ref, *refs
    ):
        normed_ref, dq_ref, dk_ref, dv_ref, rinv_s, cc_s, ag_s, de_s = refs[aliased:]
        step = pl.program_id(0)
        h = step + first
        tok = q_ref.shape[1]
        nb = e1_ref.shape[1]
        rate = tok // nb
        count = ga_ref.shape[2]
        half = tok // 2

        @pl.when(step == 0)
        def _():
            rinv, cc = norm_terms(stat_ref, other_ref, feats)
            rinv_s[...] = spread(rinv)
            cc_s[...] = spread(cc)

        rinv = rinv_s[...]
        af, ag, delta = grad_terms(attn_ref[h], og_ref[0], gain_ref[0], rinv, cc_s[...])
        normed_ref[0] = (af * rinv * gain_ref[0]).astype(bf16)
        ag_s[...] = ag
        de_s[...] = delta
        r = low_half(rr_ref[h])
        do = (ag * r).astype(bf16)
        dl = delta * r
        dks = []
        for c in range(2):
            lo, n = c * half, (c + 1) * half
            sl = slice(lo, n)
            e = e_ref[h, sl, :n]
            dp = dot_nt(do[sl], v_ref[h, :n, :])
            ds = (e.astype(f32) * (dp - jnp.concatenate([dl[sl]] * (n // 128), axis=1))).astype(bf16)
            dq_ref[h, sl, :] = dot_nn(ds, k_ref[h, :n, :])
            dks.append((dot_tn(q_ref[h, sl, :], ds), dot_tn(do[sl], e)))
        for i, ref in enumerate((dk_ref, dv_ref)):
            ref[h, :half, :] = (dks[0][i] + dks[1][i][:, :half]).T
            ref[h, half:, :] = dks[1][i][:, half:].T

        rows = pl.ds(info[4 + h], nb, stride=rate)
        r1 = high_half(rs_ref[0])
        g1 = (ag_s[rows, :] * r1).astype(bf16)
        d1 = (de_s[rows, :] * r1)[:, :1]
        dq1 = jnp.zeros((nb, 128), f32)
        for part, ref in enumerate((ga_ref, gb_ref)):
            dp1 = dot_nt(g1, ref[1, 0])
            ds1 = (e1_ref[0, :, part * count : (part + 1) * count].astype(f32) * (dp1 - d1)).astype(bf16)
            dq1 = dq1 + dot_nn(ds1, ref[0, 0])
        dq_ref[h, rows, :] += dq1

    return back_own_kernel


def make_final_kernel(codes):
    def final_kernel(
        info, dq_ref, dk_ref, dv_ref, dkn_ref, dvn_ref, dqn_ref, rows_ref, sa_ref, sb_ref, ta_ref, tb_ref, cos_ref, sin_ref,
        gq_ref, gk_ref, gv_ref, dk_s, dv_s,
    ):
        g = pl.program_id(0)
        index, par, sel = info[0], info[1], info[2]
        tok = dk_ref.shape[1]
        nb = rows_ref.shape[2]
        rate = tok // nb
        count = sa_ref.shape[2]
        scale = 1.0 / math.sqrt(dk_ref.shape[2])
        cos, sin = unpack_tables(cos_ref, sin_ref)
        kb = index * nb + rows_of((nb, count))
        slots = ta_ref.shape[0]
        keep = rows_of((slots * 16, count)) // 16 == lanes_of((slots * 16, count)) // nb
        fold = (rows_of((16, slots * 16)) == lanes_of((16, slots * 16)) % 16).astype(bf16)
        for hh in range(2):
            h = 2 * g + hh
            off = info[4 + h]
            dq = dq_ref[h] * scale + jnp.where(sel == hh, dqn_ref[0].astype(f32), 0.0)
            gq_ref[hh] = rot(dq, cos, -sin).astype(bf16)
            here = par == hh
            dk_s[hh] = (dk_ref[h] + jnp.where(here, dkn_ref[g], 0.0)) * scale
            dv_s[hh] = dv_ref[h] + jnp.where(here, dvn_ref[g], 0.0)
            k1 = rows_ref[0, hh]
            v1 = rows_ref[1, hh]
            kpos = (off + rate * kb).astype(f32)
            dk1 = jnp.zeros((nb, 128), f32)
            dv1 = jnp.zeros((nb, 128), f32)
            pick = (rows_of((128, count)) == h * nb + lanes_of((128, count)) % nb).astype(bf16)
            for part, (s, t) in enumerate(((sa_ref, ta_ref), (sb_ref, tb_ref))):
                qb = key_order(index, codes, nb, part, count)
                each = dot_nn(t[...].reshape(slots * 16, 128), pick)
                st = dot_nn(fold, jnp.where(keep, each, 0.0).astype(bf16))
                lse = st[0:1] + st[1:2] + st[2:3]
                delta = st[3:4] + st[4:5] + st[5:6]
                start = st[6:7] + st[7:8] + st[8:9]
                ok = (kb <= qb) & (kpos >= start)
                z = jnp.where(ok, dot_nt(k1, s[1, hh]) * scale - lse, NEG)
                p = jnp.exp(z).astype(bf16)
                dp = dot_nt(v1, s[0, hh])
                ds = (p.astype(f32) * (dp - delta)).astype(bf16)
                dk1 = dk1 + dot_nn(ds, s[1, hh])
                dv1 = dv1 + dot_nn(p, s[0, hh])
            rows = pl.ds(off, nb, stride=rate)
            dk_s[hh, rows, :] += dk1 * scale
            dv_s[hh, rows, :] += dv1
            gk_ref[hh] = rot(dk_s[hh], cos, -sin).astype(bf16)
            gv_ref[hh] = dv_s[hh].astype(bf16)

    return final_kernel


def call(kernel, prefetch, grid, ins, outs, scratch=(), alias=(), cost=None):
    arrays, in_specs = [], []
    for a, b, m in ins:
        if b is None:
            arrays.append(pltpu.with_memory_space_constraint(a, pltpu.VMEM))
            in_specs.append(pl.BlockSpec(memory_space=pltpu.VMEM))
        else:
            arrays.append(a)
            in_specs.append(pl.BlockSpec(b, m))
    out_shape, out_specs = [], []
    for s, d, b, m in outs:
        if b is None:
            out_shape.append(pltpu.VMEM(s, d))
            out_specs.append(pl.BlockSpec(memory_space=pltpu.VMEM))
        else:
            out_shape.append(jax.ShapeDtypeStruct(s, d))
            out_specs.append(pl.BlockSpec(b, m))
    us = 4
    return pl.pallas_call(
        kernel,
        out_shape=out_shape,
        grid_spec=pltpu.PrefetchScalarGridSpec(
            num_scalar_prefetch=len(prefetch),
            grid=grid,
            in_specs=in_specs,
            out_specs=out_specs,
            scratch_shapes=list(scratch),
        ),
        input_output_aliases={len(prefetch) + i: o for i, o in alias},
        cost_estimate=pl.CostEstimate(flops=0, transcendentals=0, bytes_accessed=int(us * 3.0e6)),
        compiler_params=pltpu.CompilerParams(
            dimension_semantics=("arbitrary",) * len(grid), vmem_limit_bytes=24 << 20
        ),
    )(*prefetch, *arrays)


def after(x, *deps):
    return lax.optimization_barrier((x, *deps))[0]


def body(queries, keys, values, out_grad, norm_gain, doc_start, head_offsets):
    heads, tok, width = queries.shape
    ctx = lax.axis_size("ctx")
    rate = ctx * tok // SEL
    nb = tok // rate
    feats = float(HEADS * width)
    pairs = heads // 2
    index = lax.axis_index("ctx")
    base = index * tok
    codes = [1 << b for b in range(2, ctx.bit_length() - 1)] + [2, 1]

    starts = lax.dynamic_slice_in_dim(doc_start, base, tok)
    position = base + jnp.arange(tok, dtype=jnp.int32)
    rel = (position - starts).astype(f32)
    freq = theta_base ** (-2.0 * jnp.arange(width // 2).astype(f32) / width)

    def tables(rel):
        angle = jnp.concatenate([rel[: tok // 2, None] * freq, rel[tok // 2 :, None] * freq], axis=1)
        return jnp.cos(angle), jnp.sin(angle)

    cos, sin = tables(rel)
    begin = starts.astype(f32).reshape(tok // 128, 128)
    after_starts = lax.dynamic_slice_in_dim(doc_start, jnp.minimum(base + tok, (ctx - 1) * tok), tok)
    next_start = (after_starts - base).astype(f32).reshape(tok // 128, 128)
    rel_next = (position + tok - after_starts).astype(f32)
    cos_next, sin_next = tables(rel_next)
    start_rel = (starts - base).astype(f32).reshape(tok // 128, 128)
    spot = jnp.arange(4 + heads, dtype=jnp.int32)
    info = jnp.pad(head_offsets, (4, 0)).astype(jnp.int32)
    info = info + jnp.where(spot == 0, index, 0) + jnp.where(spot == 1, index % 2, 0) + jnp.where(spot == 2, (index + 1) % 2, 0)
    gain = norm_gain.reshape(heads, 1, width)

    pair3 = (2, tok, width)
    one3 = (1, tok, width)
    full = queries.shape
    const = lambda n: (lambda i, *s: (0,) * n)
    whole = lambda a: (a, a.shape, const(a.ndim))
    vm = lambda a: (a, None, None)
    hbm = lambda a: pltpu.with_memory_space_constraint(a, pltpu.HBM)
    gp = lambda g, *s: (g, 0, 0)
    g4 = lambda g, *s: (0, g, 0, 0)

    def swap(x, code):
        return lax.ppermute(x, "ctx", [(i, i ^ code) for i in range(ctx)])

    half_count = SEL // 2

    up = [(i, i + 1) for i in range(ctx - 1)]
    down = [(i + 1, i) for i in range(ctx - 1)]
    mine = lambda g, s, *_: (2 * g + s[2], 0, 0)
    lead, z_code, y_code, core = codes[:-3], codes[-3], codes[-2], codes[-1]

    def join2(x, code, *deps):
        y = swap(x, code)
        return jnp.concatenate([x, after(y, *deps) if deps else y], axis=2)

    q_send = lax.dynamic_index_in_dim(queries.reshape(pairs, 2, tok, width), (index + 1) % 2, 1, keepdims=False)
    q_raw = lax.ppermute(q_send, "ctx", down)
    k_rot, rows = call(
        prep_kernel, (info,), (pairs,),
        [vm(keys), vm(values), whole(cos), whole(sin)],
        [
            (full, bf16, None, None),
            ((2, heads, nb, width), bf16, (2, 2, nb, width), g4),
        ],
    )
    vals = values
    x = rows
    for code in lead[:-1]:
        x = join2(x, code)
    ahead = [swap(x, code) for code in lead[-1:]]

    def own(first, n, qs, prior):
        outs = [
            (full, bf16, None, None),
            ((heads, tok, tok), bf16, None, None),
            (full, f32, None, None),
            (full, f32, None, None),
            (full, f32, None, None),
            ((heads, nb, width), bf16, (2, nb, width), lambda g, *s: (g + first, 0, 0)),
        ]
        ins = [
            whole(start_rel),
            (qs, pair3, lambda g, *s: (g + first, 0, 0)),
            vm(k_rot), vm(vals), whole(cos), whole(sin),
        ]
        alias = []
        for i, a in enumerate(prior):
            alias.append((len(ins), i))
            ins.append(vm(a) if i < 5 else (a, (2, nb, width), lambda g, *s: (first, 0, 0)))
        return call(
            make_own_kernel(first, len(prior)), (info,), (n,), ins, outs,
            [pltpu.VMEM((tok, tok), f32)], alias,
        )

    part = own(0, pairs // 2, queries, [])
    for a in ahead:
        x = jnp.concatenate([x, after(a, part[3])], axis=2)
    x = after(x, part[3])
    pending = swap(x, z_code)
    extra = -(-6 * (tok // 128) // 16) * 16
    o_send, e_next, q_next = call(
        next_kernel, (info,), (pairs,),
        [
            whole(next_start),
            (after(q_raw, x), one3, gp),
            vm(k_rot), vm(vals), whole(cos_next), whole(sin_next),
        ],
        [
            ((pairs, tok + extra, width), bf16, (1, tok + extra, width), gp),
            ((pairs, tok, tok), bf16, None, None),
            ((pairs, tok, width), bf16, None, None),
        ],
        [pltpu.VMEM((tok, tok), f32)] + [pltpu.VMEM((tok, 128), f32)] * 2,
    )
    y = jnp.concatenate([x, after(pending, e_next)], axis=2)
    pending = swap(y, y_code)
    o_prev = lax.ppermute(o_send, "ctx", up)
    q_rot, e_own, acc, m_own, lsum, q1 = own(pairs // 2, pairs - pairs // 2, after(queries, y), part)
    ga = jnp.concatenate([y, after(pending, m_own)], axis=2)
    gb = swap(ga, core)

    attn, rr, e1, rs, attn_rows, og_rows, stat = call(
        make_join_kernel(codes), (info,), (pairs,),
        [
            whole(start_rel), vm(acc), vm(m_own), vm(lsum),
            (o_prev, (1, tok + extra, width), gp),
            (q1, (2, nb, width), gp),
            (ga, (2, 2, half_count, width), g4),
            (gb, (2, 2, half_count, width), g4),
            (out_grad, pair3, gp),
            (gain, (2, 1, width), gp),
        ],
        [
            (full, bf16, None, None),
            (full, f32, None, None),
            ((heads, nb, SEL), bf16, (2, nb, SEL), gp),
            ((heads, nb, width), f32, (2, nb, width), gp),
            ((heads, nb, width), bf16, (2, nb, width), gp),
            ((heads, nb, width), bf16, (2, nb, width), gp),
            ((2 * tok // 128, 128), f32, (2 * tok // 128, 128), const(2)),
        ],
        [pltpu.VMEM((tok, 128), f32)] + [pltpu.VMEM((2, tok, 128), f32)] * 3 + [pltpu.VMEM((tok, 128), f32)] * 2,
    )
    other = lax.ppermute(stat, "head", [(0, 1), (1, 0)])

    more = -(-3 * (tok // 128) // 16) * 16
    rows1, stats1, do_send = call(
        make_rows_kernel(feats), (info,), (pairs,),
        [
            whole(begin), whole(stat), whole(other),
            (attn_rows, (2, nb, width), gp),
            (og_rows, (2, nb, width), gp),
            (q1, (2, nb, width), gp),
            (gain, (2, 1, width), gp),
            (rs, (2, nb, width), gp),
            vm(attn), vm(rr),
            (out_grad, one3, mine),
        ],
        [
            ((2, heads, nb, width), bf16, (2, 2, nb, width), g4),
            ((16, 128), f32, (16, 128), const(2)),
            ((pairs, tok + more, width), bf16, (1, tok + more, width), gp),
        ],
        [pltpu.VMEM((tok, 128), f32)] * 3,
    )
    flat = jnp.concatenate([rows1.reshape(2 * heads * nb, width), stats1.astype(bf16)], axis=0)[None]

    def join0(x, y):
        return jnp.concatenate([x, y], axis=0)

    x = flat
    for code in lead[:-1]:
        x = join0(x, swap(x, code))
    ahead = [swap(x, code) for code in lead[-1:]]
    do_next = lax.ppermute(do_send, "ctx", down)

    def back_own(first, n, deps, prior):
        hp = lambda h, *s: (h + first, 0, 0)
        hg = lambda h, *s: (0, h + first, 0, 0)
        ins = [
            whole(stat), whole(after(other, *deps)),
            vm(q_rot), vm(k_rot), vm(vals), vm(attn), vm(rr), vm(e_own),
            (out_grad, one3, hp),
            (gain, (1, 1, width), hp),
            (e1, (1, nb, SEL), hp),
            (rs, (1, nb, width), hp),
            (ga, (2, 1, half_count, width), hg),
            (gb, (2, 1, half_count, width), hg),
        ]
        alias = []
        for i, a in enumerate(prior):
            alias.append((len(ins), i))
            ins.append(vm(a) if i >= 1 else (a, (1, 16, width), lambda h, *s: (first, 0, 0)))
        return call(
            make_back_own_kernel(feats, first, len(prior)), (info,), (n,), ins,
            [
                (full, bf16, one3, hp),
                (full, f32, None, None),
                (full, f32, None, None),
                (full, f32, None, None),
            ],
            [pltpu.VMEM((tok, 128), f32)] * 4,
            alias,
        )

    cut = heads // 2 + 1
    part = back_own(0, cut, (flat,), [])
    for a in ahead:
        x = join0(x, after(a, part[2]))
    x = after(x, part[2])
    pending = swap(x, z_code)

    dq_send, dk_next, dv_next = call(
        next_back_kernel, (info,), (pairs,),
        [
            (after(do_next, x), (1, tok + more, width), gp),
            vm(q_next), vm(k_rot), vm(vals), vm(e_next),
        ],
        [
            ((pairs, tok, width), bf16, one3, gp),
            ((pairs, tok, width), f32, None, None),
            ((pairs, tok, width), f32, None, None),
        ],
    )
    y = join0(x, after(pending, dk_next))
    pending = swap(y, y_code)
    dq_prev = lax.ppermute(dq_send, "ctx", up)
    normed, dq_own, dk_own, dv_own = back_own(cut, heads - cut, (y,), part)
    sa = after(join0(y, after(pending, dk_own)), dq_prev)
    sb = swap(sa, core)

    def sort(x):
        slots = x.shape[0]
        near = x[:, : 2 * heads * nb].reshape(slots, 2, heads, nb, width)
        near = near.transpose(1, 2, 0, 3, 4).reshape(2, heads, slots * nb, width)
        return near, x[:, 2 * heads * nb :]

    (sa, ta), (sb, tb) = sort(sa), sort(sb)
    grad_queries, grad_keys, grad_values = call(
        make_final_kernel(codes), (info,), (pairs,),
        [
            vm(dq_own), vm(dk_own), vm(dv_own), vm(dk_next), vm(dv_next),
            (dq_prev, one3, gp),
            (rows, (2, 2, nb, width), g4),
            (sa, (2, 2, half_count, width), g4),
            (sb, (2, 2, half_count, width), g4),
            whole(ta), whole(tb),
            whole(cos), whole(sin),
        ],
        [
            (full, bf16, pair3, gp),
            (full, bf16, pair3, gp),
            (full, bf16, pair3, gp),
        ],
        [pltpu.VMEM((2, tok, 128), f32)] * 2,
    )
    return (normed, grad_queries, grad_keys, grad_values)


def solution(mesh):
    return jax.shard_map(
        body,
        mesh=mesh,
        in_specs=(
            P("head", "ctx", None),
            P("head", "ctx", None),
            P("head", "ctx", None),
            P("head", "ctx", None),
            P("head", None),
            P(),
            P("head"),
        ),
        out_specs=(
            P("head", "ctx", None),
            P("head", "ctx", None),
            P("head", "ctx", None),
            P("head", "ctx", None),
        ),
        check_vma=False,
    )
```

time: 101 us -> 91.3 us (0.904)
  waiting for transfers between devices: 28.7 us -> 13.5 us
  starting transfers between devices: 22.9 us -> 27 us
    ppermute x8, waiting for transfers between devices: 26.5 us -> 11.3 us  [swap(): return lax.ppermute(x, 'ctx', [(i, i ^ code) for i in range(ctx)])]
    unnamed x12 -> x15, local copies, waits for them, and re-layouts: 3.12 us -> 0.14 us
    ppermute x8, starting transfers between devices: 17.6 us -> 19.8 us  [swap(): return lax.ppermute(x, 'ctx', [(i, i ^ code) for i in range(ctx)])]
    squeeze x0 -> x1, local copies, waits for them, and re-layouts: none -> 2.03 us  [body(): lax.dynamic_index_in_dim(queries.reshape(pairs, 2, tok, width), (index +...]
    ppermute x2 -> x4, starting transfers between devices: 3.75 us -> 5.65 us  [the longest x1 1.76 us: body(): o_prev = lax.ppermute(o_send, 'ctx', up)]
  transfers between devices with their start and end apart: 11 -> 13, of which waited for: 7 -> 8; matrix products, arithmetic and copies ran while one was open for 0% -> 3% of each run, Pallas kernels for 25% -> 33%
where the time goes in v3:
time: 91.3 us; the launch traced here: 90.3 us
  Pallas kernels  44.1 us (48%)
  starting transfers between devices  27 us (30%)
  waiting for transfers between devices  13.5 us (15%)
  local copies, waits for them, and re-layouts  2.39 us (3%)
  other arithmetic  2.31 us (3%)
  between operations  0.96 us (1%)
    pallas_call x10, Pallas kernels, call(): pl.pallas_call(kernel, out_shape=out_shape, grid_spec=pltpu.PrefetchScala...  44.1 us
    ppermute x8, starting transfers between devices, swap(): return lax.ppermute(x, 'ctx', [(i, i ^ code) for i in range(ctx)])  19.8 us
    ppermute x8, waiting for transfers between devices, swap(): return lax.ppermute(x, 'ctx', [(i, i ^ code) for i in range(ctx)])  11.3 us
    ppermute x1, waiting for transfers between devices, body(): other = lax.ppermute(stat, 'head', [(0, 1), (1, 0)])  2.16 us
    squeeze x1, local copies, waits for them, and re-layouts, body(): lax.dynamic_index_in_dim(queries.reshape(pairs, 2, tok, width), (index +...  2.03 us
  transfers between devices with their start and end apart: 13, of which 8 were waited for; matrix products, arithmetic and copies ran while one was open for 3% of the time, Pallas kernels for 33%

profile of v3, /device:TPU:0, one launch (start us, length us, event | category | flops | bytes accessed | tf_op | source)
XLA Modules:
  0.0 90.3 jit_solution(15735544311247450196)
XLA Ops:
  0.7 0.0 copy-start.2
  0.7 2.0 %dynamic-slice_bitcast_fusion = bf16[4,512,128]{2,1,0:T(8,128)(2,1)} fusion(bf16[4,2,512,128]{3,2,1,0:T(8,128)(2,1)} %bitcast.23, s32[]{:T(128)S(6)} %select_n.40), kind=kLoop, calls=%fused_computation.1 | loop fusion | bytes 1048580 | tf_op jit(solution)/shard_map/jit(dynamic_index_in_dim)/squeeze | solution.py:576
  2.7 1.3 %collective-permute-start.2 = (bf16[4,512,128]{2,1,0:T(8,128)(2,1)}, bf16[4,512,128]{2,1,0:T(8,128)(2,1)}, u32[]{:S(2)}, u32[]{:S(2)}) collective-permute-start(bf16[4,512,128]{2,1,0:T(8,128)(2,1)} %dynamic-slice_bitcast_fusion), channel_id=1, source_target_pairs={{2,0},{4,2},{6,4},{8,6},{10,8},{12,10},{14,12},{16,14},{18,16},{20... | collective-permute-start | bytes 1572872 | tf_op jit(solution)/shard_map/ppermute | solution.py:577
  4.0 0.9 convert_bitcast_fusion
  4.9 0.2 broadcast_multiply_fusion.1
  5.1 0.5 fusion.2
  5.7 0.0 copy-done.5
  5.7 0.1 fusion.6.info
  5.8 2.1 %shard_map.102 = (bf16[8,512,128]{2,1,0:T(8,128)(2,1)S(1)}, bf16[2,8,16,128]{3,2,1,0:T(8,128)(2,1)S(1)}) custom-call(s32[12]{0:T(128)S(1)} %fusion.6.info, bf16[8,512,128]{2,1,0:T(8,128)(2,1)S(1)} %copy-done.3, bf16[8,512,128]{2,1,0:T(8,128)(2,1)S(1)} %copy-done, f32[256,128]{1,0:T(8,128)S(1)} %get-tuple-element.117.cos_ref, ...), custom_call_target="tpu_custom_call" | custom-call | bytes 12000000 | tf_op jit(solution)/shard_map/pallas_call | solution.py:498
  7.8 4.6 %collective-permute-start = (bf16[2,8,16,128]{3,2,1,0:T(8,128)(2,1)S(1)}, bf16[2,8,16,128]{3,2,1,0:T(8,128)(2,1)S(1)}, u32[]{:S(2)}, u32[]{:S(2)}) collective-permute-start(bf16[2,8,16,128]{3,2,1,0:T(8,128)(2,1)S(1)} %get-tuple-element.59.rows_ref), channel_id=1, source_target_pairs={{0,8},{2,10},{4,12},{6,14},{8,0},{10,2},{12,4},{14,6},{16,24},{18,... | collective-permute-start | bytes 196616 | tf_op jit(solution)/shard_map/ppermute | solution.py:563
  12.4 3.3 %shard_map.103 = (bf16[8,512,128]{2,1,0:T(8,128)(2,1)S(1)}, bf16[8,512,512]{2,1,0:T(8,128)(2,1)S(1)}, f32[8,512,128]{2,1,0:T(8,128)S(1)}, f32[8,512,128]{2,1,0:T...) custom-call(s32[12]{0:T(128)S(1)} %fusion.6.info, f32[4,128]{1,0:T(4,128)S(1)} %get-tuple-element.126.start_ref, ...), custom_call_target="tpu_custom_call" | custom-call | bytes 12000000 | tf_op jit(solution)/shard_map/pallas_call | solution.py:498
  15.7 1.5 %collective-permute-done = bf16[2,8,16,128]{3,2,1,0:T(8,128)(2,1)S(1)} collective-permute-done((bf16[2,8,16,128]{3,2,1,0:T(8,128)(2,1)S(1)}, bf16[2,8,16,128]{3,2,1,0:T(8,128)(2,1)S(1)}, u32[]{:S(2)}, u32[]{:S(2)}) %collective-permute-start) | collective-permute-done | bytes 65568 | tf_op jit(solution)/shard_map/ppermute | solution.py:563
  17.3 3.4 %collective-permute-start.1 = (bf16[2,8,32,128]{3,2,1,0:T(8,128)(2,1)S(1)}, bf16[2,8,32,128]{3,2,1,0:T(8,128)(2,1)S(1)}, u32[]{:S(2)}, u32[]{:S(2)}) collective-permute-start(bf16[2,8,32,128]{3,2,1,0:T(8,128)(2,1)S(1)} %pad_maximum_fusion.3), channel_id=1, source_target_pairs={{0,16},{2,18},{4,20},{6,22},{8,24},{10,26},{12,28},{14,30},{16,0},... | collective-permute-start | bytes 393224 | tf_op jit(solution)/shard_map/ppermute | solution.py:563
  20.7 0.5 fusion
  21.3 0.0 collective-permute-done.2.q_ref
  21.3 5.0 %shard_map.104 = (bf16[4,544,128]{2,1,0:T(8,128)(2,1)S(1)}, bf16[4,512,512]{2,1,0:T(8,128)(2,1)S(1)}, bf16[4,512,128]{2,1,0:T(8,128)(2,1)S(1)}) custom-call(s32[12]{0:T(128)S(1)} %fusion.6.info, f32[4,128]{1,0:T(4,128)S(1)} %get-tuple-element.125.start_ref, bf16[4,512,128]{2,1,0:T(8,128)(2,1)} %collective-permute-done.2.q_ref, ...), custom_call_target="tpu_custom_call" | custom-call | bytes 12000000 | tf_op jit(solution)/shard_map/pallas_call | solution.py:498
  26.3 0.0 collective-permute-done.1
  26.4 0.1 constant_dynamic-update-slice_fusion.3
  26.4 0.2 collective-permute-start.4
  26.6 1.8 %collective-permute-start.3 = (bf16[4,544,128]{2,1,0:T(8,128)(2,1)S(1)}, bf16[4,544,128]{2,1,0:T(8,128)(2,1)S(1)}, u32[]{:S(2)}, u32[]{:S(2)}) collective-permute-start(bf16[4,544,128]{2,1,0:T(8,128)(2,1)S(1)} %get-tuple-element.76), channel_id=1, source_target_pairs={{0,2},{2,4},{4,6},{6,8},{8,10},{10,12},{12,14},{14,16},{16,18},{18... | collective-permute-start | bytes 1671176 | tf_op jit(solution)/shard_map/ppermute | solution.py:637
  28.3 0.0 copy-start.1
  28.4 0.0 copy-start.4
  28.4 3.4 %shard_map.105 = (bf16[8,512,128]{2,1,0:T(8,128)(2,1)S(1)}, bf16[8,512,512]{2,1,0:T(8,128)(2,1)S(1)}, f32[8,512,128]{2,1,0:T(8,128)S(1)}, f32[8,512,128]{2,1,0:T...) custom-call(s32[12]{0:T(128)S(1)} %fusion.6.info, ...), custom_call_target="tpu_custom_call", output_to_operand_aliasing={{0}: (7, {}), {1}: (8, {}), {2}: (9, {}), {3}: (10, {}), {4... | custom-call | bytes 12000000 | tf_op jit(solution)/shard_map/pallas_call | solution.py:498
  31.7 1.5 %collective-permute-done.4 = bf16[2,8,64,128]{3,2,1,0:T(8,128)(2,1)S(1)} collective-permute-done((bf16[2,8,64,128]{3,2,1,0:T(8,128)(2,1)S(1)}, bf16[2,8,64,128]{3,2,1,0:T(8,128)(2,1)S(1)}, u32[]{:S(2)}, u32[]{:S(2)}) %collective-permute-start.4) | collective-permute-done | bytes 262176 | tf_op jit(solution)/shard_map/ppermute | solution.py:563
  33.3 0.7 collective-permute-start.5
  34.0 0.0 collective-permute-done.3.on_ref
  34.0 1.5 %collective-permute-done.5.gb_ref = bf16[2,8,128,128]{3,2,1,0:T(8,128)(2,1)S(1)} collective-permute-done((bf16[2,8,128,128]{3,2,1,0:T(8,128)(2,1)S(1)}, bf16[2,8,128,128]{3,2,1,0:T(8,128)(2,1)S(1)}, u32[]{:S(2)}, u32[]{:S(2)}) %collective-permute-start.5) | collective-permute-done | bytes 524320 | tf_op jit(solution)/shard_map/ppermute | solution.py:563
  35.6 6.4 %shard_map.106 = (bf16[8,512,128]{2,1,0:T(8,128)(2,1)S(1)}, f32[8,512,128]{2,1,0:T(8,128)S(1)}, bf16[8,16,256]{2,1,0:T(8,128)(2,1)S(1)}, f32[8,16,128]{2,1,0:T(8...) custom-call(s32[12]{0:T(128)S(1)} %fusion.6.info, ...), custom_call_target="tpu_custom_call" | custom-call | bytes 12000000 | tf_op jit(solution)/shard_map/pallas_call | solution.py:498
  42.0 1.5 %collective-permute-start.6 = (f32[8,128]{1,0:T(8,128)S(1)}, f32[8,128]{1,0:T(8,128)S(1)}, u32[]{:S(2)}, u32[]{:S(2)}) collective-permute-start(f32[8,128]{1,0:T(8,128)S(1)} %get-tuple-element.79.stat_ref), channel_id=1, source_target_pairs={{0,1},{1,0},{2,3},{3,2},{4,5},{5,4},{6,7},{7,6},{8,9},{9,8},{10,11... | collective-permute-start | bytes 12296 | tf_op jit(solution)/shard_map/ppermute | solution.py:664
  43.5 2.2 %collective-permute-done.6.other_ref = f32[8,128]{1,0:T(8,128)S(1)} collective-permute-done((f32[8,128]{1,0:T(8,128)S(1)}, f32[8,128]{1,0:T(8,128)S(1)}, u32[]{:S(2)}, u32[]{:S(2)}) %collective-permute-start.6) | collective-permute-done | bytes 4128 | tf_op jit(solution)/shard_map/ppermute | solution.py:664
  45.6 2.2 %shard_map.107 = (bf16[2,8,16,128]{3,2,1,0:T(8,128)(2,1)S(1)}, f32[16,128]{1,0:T(8,128)S(1)}, bf16[4,528,128]{2,1,0:T(8,128)(2,1)S(1)}) custom-call(s32[12]{0:T(128)S(1)} %fusion.6.info, f32[4,128]{1,0:T(4,128)S(1)} %get-tuple-element.122.begin_ref, f32[8,128]{1,0:T(8,128)S(1)} %get-tuple-element.79.stat_ref, f32[8,128]{1,0:T(8,128)S(1)} %collective-permute-done.6.other_ref, ...), custom_call_target="tpu_custom_call" | custom-call | bytes 12000000 | tf_op jit(solution)/shard_map/pallas_call | solution.py:498
  47.8 1.3 %collective-permute-start.9 = (bf16[4,528,128]{2,1,0:T(8,128)(2,1)S(1)}, bf16[4,528,128]{2,1,0:T(8,128)(2,1)S(1)}, u32[]{:S(2)}, u32[]{:S(2)}) collective-permute-start(bf16[4,528,128]{2,1,0:T(8,128)(2,1)S(1)} %get-tuple-element.94), channel_id=1, source_target_pairs={{2,0},{4,2},{6,4},{8,6},{10,8},{12,10},{14,12},{16,14},{18,16},{20... | collective-permute-start | bytes 1622024 | tf_op jit(solution)/shard_map/ppermute | solution.py:695
  49.1 5.6 %collective-permute-start.7 = (bf16[1,272,128]{2,1,0:T(8,128)(2,1)S(1)}, bf16[1,272,128]{2,1,0:T(8,128)(2,1)S(1)}, u32[]{:S(2)}, u32[]{:S(2)}) collective-permute-start(bf16[1,272,128]{2,1,0:T(8,128)(2,1)S(1)} %maximum_bitcast_fusion), channel_id=1, source_target_pairs={{0,8},{2,10},{4,12},{6,14},{8,0},{10,2},{12,4},{14,6},{16,24},{18,... | collective-permute-start | bytes 208904 | tf_op jit(solution)/shard_map/ppermute | solution.py:563
  54.7 6.8 %shard_map.108 = (bf16[8,512,128]{2,1,0:T(8,128)(2,1)}, f32[8,512,128]{2,1,0:T(8,128)S(1)}, f32[8,512,128]{2,1,0:T(8,128)S(1)}, f32[8,512,128]{2,1,0:T(8,128)S(1)}) custom-call(s32[12]{0:T(128)S(1)} %fusion.6.info, f32[8,128]{1,0:T(8,128)S(1)} %get-tuple-element.79.stat_ref, f32[8,128]{1,0:T(8,128)S(1)} %collective-permute-done.6.other_ref, ...), custom_call_target="tpu_custom_call" | custom-call | bytes 12000000 | tf_op jit(solution)/shard_map/pallas_call | solution.py:498
  61.6 1.8 %collective-permute-done.7 = bf16[1,272,128]{2,1,0:T(8,128)(2,1)S(1)} collective-permute-done((bf16[1,272,128]{2,1,0:T(8,128)(2,1)S(1)}, bf16[1,272,128]{2,1,0:T(8,128)(2,1)S(1)}, u32[]{:S(2)}, u32[]{:S(2)}) %collective-permute-start.7) | collective-permute-done | bytes 69664 | tf_op jit(solution)/shard_map/ppermute | solution.py:563
  63.4 1.2 %collective-permute-start.8 = (bf16[2,272,128]{2,1,0:T(8,128)(2,1)S(1)}, bf16[2,272,128]{2,1,0:T(8,128)(2,1)S(1)}, u32[]{:S(2)}, u32[]{:S(2)}) collective-permute-start(bf16[2,272,128]{2,1,0:T(8,128)(2,1)S(1)} %pad_maximum_fusion.1), channel_id=1, source_target_pairs={{0,16},{2,18},{4,20},{6,22},{8,24},{10,26},{12,28},{14,30},{16,0},... | collective-permute-start | bytes 417800 | tf_op jit(solution)/shard_map/ppermute | solution.py:563
  64.6 0.0 collective-permute-done.9.do_ref
  64.6 3.9 %shard_map.109 = (bf16[4,512,128]{2,1,0:T(8,128)(2,1)S(1)}, f32[4,512,128]{2,1,0:T(8,128)S(1)}, f32[4,512,128]{2,1,0:T(8,128)S(1)}) custom-call(s32[12]{0:T(128)S(1)} %fusion.6.info, bf16[4,528,128]{2,1,0:T(8,128)(2,1)S(1)} %collective-permute-done.9.do_ref, bf16[4,512,128]{2,1,0:T(8,128)(2,1)S(1)} %get-tuple-element.96.q_ref, ...), custom_call_target="tpu_custom_call" | custom-call | bytes 12000000 | tf_op jit(solution)/shard_map/pallas_call | solution.py:498
  68.6 1.3 %collective-permute-start.10 = (bf16[4,512,128]{2,1,0:T(8,128)(2,1)S(1)}, bf16[4,512,128]{2,1,0:T(8,128)(2,1)S(1)}, u32[]{:S(2)}, u32[]{:S(2)}) collective-permute-start(bf16[4,512,128]{2,1,0:T(8,128)(2,1)S(1)} %get-tuple-element.108), channel_id=1, source_target_pairs={{0,2},{2,4},{4,6},{6,8},{8,10},{10,12},{12,14},{14,16},{16,18},{18... | collective-permute-start | bytes 1572872 | tf_op jit(solution)/shard_map/ppermute | solution.py:747
  69.9 1.2 %collective-permute-done.8 = bf16[2,272,128]{2,1,0:T(8,128)(2,1)S(1)} collective-permute-done((bf16[2,272,128]{2,1,0:T(8,128)(2,1)S(1)}, bf16[2,272,128]{2,1,0:T(8,128)(2,1)S(1)}, u32[]{:S(2)}, u32[]{:S(2)}) %collective-permute-start.8) | collective-permute-done | bytes 139296 | tf_op jit(solution)/shard_map/ppermute | solution.py:563
  71.1 1.1 %collective-permute-start.11 = (bf16[4,272,128]{2,1,0:T(8,128)(2,1)S(1)}, bf16[4,272,128]{2,1,0:T(8,128)(2,1)S(1)}, u32[]{:S(2)}, u32[]{:S(2)}) collective-permute-start(bf16[4,272,128]{2,1,0:T(8,128)(2,1)S(1)} %constant_dynamic-update-slice_fusion.5), channel_id=1, source_target_pairs={{0,4},{2,6},{4,0},{6,2},{8,12},{10,14},{12,8},{14,10},{16,20},{18,... | collective-permute-start | bytes 835592 | tf_op jit(solution)/shard_map/ppermute | solution.py:563
  72.1 5.1 %shard_map.110 = (bf16[8,512,128]{2,1,0:T(8,128)(2,1)}, f32[8,512,128]{2,1,0:T(8,128)S(1)}, f32[8,512,128]{2,1,0:T(8,128)S(1)}, f32[8,512,128]{2,1,0:T(8,128)S(1)}) custom-call(s32[12]{0:T(128)S(1)} %fusion.6.info, f32[8,128]{1,0:T(8,128)S(1)} %get-tuple-element.79.stat_ref, ...), custom_call_target="tpu_custom_call", output_to_operand_aliasing={{0}: (15, {}), {1}: (16, {}), {2}: (17, {}), {3}: (18, {})} | custom-call | bytes 12000000 | tf_op jit(solution)/shard_map/pallas_call | solution.py:498
  77.3 2.2 %collective-permute-done.11 = bf16[4,272,128]{2,1,0:T(8,128)(2,1)S(1)} collective-permute-done((bf16[4,272,128]{2,1,0:T(8,128)(2,1)S(1)}, bf16[4,272,128]{2,1,0:T(8,128)(2,1)S(1)}, u32[]{:S(2)}, u32[]{:S(2)}) %collective-permute-start.11) | collective-permute-done | bytes 278560 | tf_op jit(solution)/shard_map/ppermute | solution.py:563
  79.5 0.1 pad_maximum_fusion
  79.6 0.0 collective-permute-done.10.dqn_ref
  79.6 3.0 %collective-permute-start.12 = (bf16[8,272,128]{2,1,0:T(8,128)(2,1)S(1)}, bf16[8,272,128]{2,1,0:T(8,128)(2,1)S(1)}, u32[]{:S(2)}, u32[]{:S(2)}) collective-permute-start(bf16[8,272,128]{2,1,0:T(8,128)(2,1)S(1)} %pad_maximum_fusion), channel_id=1, source_target_pairs={{0,2},{2,0},{4,6},{6,4},{8,10},{10,8},{12,14},{14,12},{16,18},{18,... | collective-permute-start | bytes 1671176 | tf_op jit(solution)/shard_map/ppermute | solution.py:563
  82.7 1.5 %collective-permute-done.12 = bf16[8,272,128]{2,1,0:T(8,128)(2,1)S(1)} collective-permute-done((bf16[8,272,128]{2,1,0:T(8,128)(2,1)S(1)}, bf16[8,272,128]{2,1,0:T(8,128)(2,1)S(1)}, u32[]{:S(2)}, u32[]{:S(2)}) %collective-permute-start.12) | collective-permute-done | bytes 557088 | tf_op jit(solution)/shard_map/ppermute | solution.py:563
  84.3 5.9 %shard_map.111 = (bf16[8,512,128]{2,1,0:T(8,128)(2,1)}, bf16[8,512,128]{2,1,0:T(8,128)(2,1)}, bf16[8,512,128]{2,1,0:T(8,128)(2,1)}) custom-call(s32[12]{0:T(128)S(1)} %fusion.6.info, f32[8,512,128]{2,1,0:T(8,128)S(1)} %get-tuple-element.104.dq_ref, f32[8,512,128]{2,1,0:T(8,128)S(1)} %get-tuple-element.105.dk_ref, ...), custom_call_target="tpu_custom_call" | custom-call | bytes 12000000 | tf_op jit(solution)/shard_map/pallas_call | solution.py:498
  (24 shorter events, 0.3 us)
Async XLA Ops:
  0.6 5.0 %copy-start.5 = (s32[8]{0:T(128)S(1)}, s32[8]{0:T(128)}, u32[]{:S(2)}) copy-start(s32[8]{0:T(128)} %param.13) | copy-start | bytes 100
  0.6 5.1 %copy-start = (bf16[8,512,128]{2,1,0:T(8,128)(2,1)S(1)}, bf16[8,512,128]{2,1,0:T(8,128)(2,1)}, u32[]{:S(2)}) copy-start(bf16[8,512,128]{2,1,0:T(8,128)(2,1)} %v_ref.13) | copy-start | bytes 3145732
  0.7 5.1 %copy-start.3 = (bf16[8,512,128]{2,1,0:T(8,128)(2,1)S(1)}, bf16[8,512,128]{2,1,0:T(8,128)(2,1)}, u32[]{:S(2)}) copy-start(bf16[8,512,128]{2,1,0:T(8,128)(2,1)} %k_ref.1) | copy-start | bytes 3145732
  0.7 11.7 %copy-start.2 = (bf16[8,512,128]{2,1,0:T(8,128)(2,1)S(1)}, bf16[8,512,128]{2,1,0:T(8,128)(2,1)}, u32[]{:S(2)}) copy-start(bf16[8,512,128]{2,1,0:T(8,128)(2,1)} %q_ref.2) | copy-start | bytes 3145732
  2.7 18.6 %collective-permute-start.2 = (bf16[4,512,128]{2,1,0:T(8,128)(2,1)}, bf16[4,512,128]{2,1,0:T(8,128)(2,1)}, u32[]{:S(2)}, u32[]{:S(2)}) collective-permute-start(bf16[4,512,128]{2,1,0:T(8,128)(2,1)} %dynamic-slice_bitcast_fusion), channel_id=1, source_target_pairs={{2,0},{4,2},{6,4},{8,6},{10,8},{12,10},{14,12},{16,14},{18,16},{20... | collective-permute-start | bytes 1572872 | tf_op jit(solution)/shard_map/ppermute | solution.py:577
  7.8 9.4 %collective-permute-start = (bf16[2,8,16,128]{3,2,1,0:T(8,128)(2,1)S(1)}, bf16[2,8,16,128]{3,2,1,0:T(8,128)(2,1)S(1)}, u32[]{:S(2)}, u32[]{:S(2)}) collective-permute-start(bf16[2,8,16,128]{3,2,1,0:T(8,128)(2,1)S(1)} %get-tuple-element.59.rows_ref), channel_id=1, source_target_pairs={{0,8},{2,10},{4,12},{6,14},{8,0},{10,2},{12,4},{14,6},{16,24},{18,... | collective-permute-start | bytes 196616 | tf_op jit(solution)/shard_map/ppermute | solution.py:563
  17.3 9.1 %collective-permute-start.1 = (bf16[2,8,32,128]{3,2,1,0:T(8,128)(2,1)S(1)}, bf16[2,8,32,128]{3,2,1,0:T(8,128)(2,1)S(1)}, u32[]{:S(2)}, u32[]{:S(2)}) collective-permute-start(bf16[2,8,32,128]{3,2,1,0:T(8,128)(2,1)S(1)} %pad_maximum_fusion.3), channel_id=1, source_target_pairs={{0,16},{2,18},{4,20},{6,22},{8,24},{10,26},{12,28},{14,30},{16,0},... | collective-permute-start | bytes 393224 | tf_op jit(solution)/shard_map/ppermute | solution.py:563
  26.4 6.9 %collective-permute-start.4 = (bf16[2,8,64,128]{3,2,1,0:T(8,128)(2,1)S(1)}, bf16[2,8,64,128]{3,2,1,0:T(8,128)(2,1)S(1)}, u32[]{:S(2)}, u32[]{:S(2)}) collective-permute-start(bf16[2,8,64,128]{3,2,1,0:T(8,128)(2,1)S(1)} %get-tuple-element.119), channel_id=1, source_target_pairs={{0,4},{2,6},{4,0},{6,2},{8,12},{10,14},{12,8},{14,10},{16,20},{18,... | collective-permute-start | bytes 786440 | tf_op jit(solution)/shard_map/ppermute | solution.py:563
  26.6 7.5 %collective-permute-start.3 = (bf16[4,544,128]{2,1,0:T(8,128)(2,1)S(1)}, bf16[4,544,128]{2,1,0:T(8,128)(2,1)S(1)}, u32[]{:S(2)}, u32[]{:S(2)}) collective-permute-start(bf16[4,544,128]{2,1,0:T(8,128)(2,1)S(1)} %get-tuple-element.76), channel_id=1, source_target_pairs={{0,2},{2,4},{4,6},{6,8},{8,10},{10,12},{12,14},{14,16},{16,18},{18... | collective-permute-start | bytes 1671176 | tf_op jit(solution)/shard_map/ppermute | solution.py:637
  28.3 7.2 %copy-start.1 = (bf16[8,512,128]{2,1,0:T(8,128)(2,1)S(1)}, bf16[8,512,128]{2,1,0:T(8,128)(2,1)}, u32[]{:S(2)}) copy-start(bf16[8,512,128]{2,1,0:T(8,128)(2,1)} %og_ref.7) | copy-start | bytes 3145732
  28.4 7.2 %copy-start.4 = (f32[8,128]{1,0:T(8,128)S(1)}, f32[8,128]{1,0:T(8,128)}, u32[]{:S(2)}) copy-start(f32[8,128]{1,0:T(8,128)} %param.11) | copy-start | bytes 12292
  33.3 2.3 %collective-permute-start.5 = (bf16[2,8,128,128]{3,2,1,0:T(8,128)(2,1)S(1)}, bf16[2,8,128,128]{3,2,1,0:T(8,128)(2,1)S(1)}, u32[]{:S(2)}, u32[]{:S(2)}) collective-permute-start(bf16[2,8,128,128]{3,2,1,0:T(8,128)(2,1)S(1)} %constant_dynamic-update-slice_fusion.2.ga_ref), channel_id=1, source_target_pairs={{0,2},{2,0},{4,6},{6,4},{8,10},{10,8},{12,14},{14,12},{16,18},{18,... | collective-permute-start | bytes 1572872 | tf_op jit(solution)/shard_map/ppermute | solution.py:563
  42.0 3.7 %collective-permute-start.6 = (f32[8,128]{1,0:T(8,128)S(1)}, f32[8,128]{1,0:T(8,128)S(1)}, u32[]{:S(2)}, u32[]{:S(2)}) collective-permute-start(f32[8,128]{1,0:T(8,128)S(1)} %get-tuple-element.79.stat_ref), channel_id=1, source_target_pairs={{0,1},{1,0},{2,3},{3,2},{4,5},{5,4},{6,7},{7,6},{8,9},{9,8},{10,11... | collective-permute-start | bytes 12296 | tf_op jit(solution)/shard_map/ppermute | solution.py:664
  47.8 16.8 %collective-permute-start.9 = (bf16[4,528,128]{2,1,0:T(8,128)(2,1)S(1)}, bf16[4,528,128]{2,1,0:T(8,128)(2,1)S(1)}, u32[]{:S(2)}, u32[]{:S(2)}) collective-permute-start(bf16[4,528,128]{2,1,0:T(8,128)(2,1)S(1)} %get-tuple-element.94), channel_id=1, source_target_pairs={{2,0},{4,2},{6,4},{8,6},{10,8},{12,10},{14,12},{16,14},{18,16},{20... | collective-permute-start | bytes 1622024 | tf_op jit(solution)/shard_map/ppermute | solution.py:695
  49.1 14.2 %collective-permute-start.7 = (bf16[1,272,128]{2,1,0:T(8,128)(2,1)S(1)}, bf16[1,272,128]{2,1,0:T(8,128)(2,1)S(1)}, u32[]{:S(2)}, u32[]{:S(2)}) collective-permute-start(bf16[1,272,128]{2,1,0:T(8,128)(2,1)S(1)} %maximum_bitcast_fusion), channel_id=1, source_target_pairs={{0,8},{2,10},{4,12},{6,14},{8,0},{10,2},{12,4},{14,6},{16,24},{18,... | collective-permute-start | bytes 208904 | tf_op jit(solution)/shard_map/ppermute | solution.py:563
  63.4 7.7 %collective-permute-start.8 = (bf16[2,272,128]{2,1,0:T(8,128)(2,1)S(1)}, bf16[2,272,128]{2,1,0:T(8,128)(2,1)S(1)}, u32[]{:S(2)}, u32[]{:S(2)}) collective-permute-start(bf16[2,272,128]{2,1,0:T(8,128)(2,1)S(1)} %pad_maximum_fusion.1), channel_id=1, source_target_pairs={{0,16},{2,18},{4,20},{6,22},{8,24},{10,26},{12,28},{14,30},{16,0},... | collective-permute-start | bytes 417800 | tf_op jit(solution)/shard_map/ppermute | solution.py:563
  68.6 11.0 %collective-permute-start.10 = (bf16[4,512,128]{2,1,0:T(8,128)(2,1)S(1)}, bf16[4,512,128]{2,1,0:T(8,128)(2,1)S(1)}, u32[]{:S(2)}, u32[]{:S(2)}) collective-permute-start(bf16[4,512,128]{2,1,0:T(8,128)(2,1)S(1)} %get-tuple-element.108), channel_id=1, source_target_pairs={{0,2},{2,4},{4,6},{6,8},{8,10},{10,12},{12,14},{14,16},{16,18},{18... | collective-permute-start | bytes 1572872 | tf_op jit(solution)/shard_map/ppermute | solution.py:747
  71.1 8.4 %collective-permute-start.11 = (bf16[4,272,128]{2,1,0:T(8,128)(2,1)S(1)}, bf16[4,272,128]{2,1,0:T(8,128)(2,1)S(1)}, u32[]{:S(2)}, u32[]{:S(2)}) collective-permute-start(bf16[4,272,128]{2,1,0:T(8,128)(2,1)S(1)} %constant_dynamic-update-slice_fusion.5), channel_id=1, source_target_pairs={{0,4},{2,6},{4,0},{6,2},{8,12},{10,14},{12,8},{14,10},{16,20},{18,... | collective-permute-start | bytes 835592 | tf_op jit(solution)/shard_map/ppermute | solution.py:563
  79.6 4.6 %collective-permute-start.12 = (bf16[8,272,128]{2,1,0:T(8,128)(2,1)S(1)}, bf16[8,272,128]{2,1,0:T(8,128)(2,1)S(1)}, u32[]{:S(2)}, u32[]{:S(2)}) collective-permute-start(bf16[8,272,128]{2,1,0:T(8,128)(2,1)S(1)} %pad_maximum_fusion), channel_id=1, source_target_pairs={{0,2},{2,0},{4,6},{6,4},{8,10},{10,8},{12,14},{14,12},{16,18},{18,... | collective-permute-start | bytes 1671176 | tf_op jit(solution)/shard_map/ppermute | solution.py:563

commit v4 on v3

--- a/solution.py
+++ b/solution.py
@@ -76,7 +76,7 @@
     return jnp.broadcast_to(jnp.sum(x, axis=1, keepdims=True), x.shape)
 
 
-def prep_kernel(info, k_ref, v_ref, cos_ref, sin_ref, kr_ref, rows_ref):
+def prep_kernel(info, k_ref, v_ref, cos_ref, sin_ref, kr_ref, send_ref, rows_ref):
     g = pl.program_id(0)
     tok = k_ref.shape[1]
     nb = rows_ref.shape[2]
@@ -89,12 +89,15 @@
         kr_ref[h] = kr
         rows_ref[0, hh] = dot_nn(hot, kr).astype(bf16)
         rows_ref[1, hh] = dot_nn(hot, v_ref[h]).astype(bf16)
+    par = info[1]
+    send_ref[0, 0] = kr_ref[2 * g + par]
+    send_ref[1, 0] = v_ref[2 * g + par]
 
 
 def make_own_kernel(first, aliased):
     def own_kernel(info, start_ref, q_ref, k_ref, v_ref, cos_ref, sin_ref, *refs):
         refs = refs[aliased:]
-        qr_ref, e_ref, acc_ref, m_ref, l_ref, rows_ref, bias_ref = refs
+        qr_ref, qt_ref, e_ref, acc_ref, m_ref, l_ref, rows_ref, bias_ref = refs
         tok = q_ref.shape[1]
         nb = rows_ref.shape[1]
         rate = tok // nb
@@ -114,6 +117,7 @@
             h = 2 * (pl.program_id(0) + first) + hh
             q = rot(q_ref[hh].astype(f32), cos, sin).astype(bf16)
             qr_ref[h] = q
+            qt_ref[h] = q.T
             hot = (lanes_of((nb, tok)) == info[4 + h] + rate * rows_of((nb, tok))).astype(bf16)
             rows_ref[hh] = dot_nn(hot, q).astype(bf16)
             vals = jnp.concatenate([v_ref[h], jnp.ones((tok, 128), bf16)], axis=1)
@@ -167,7 +171,7 @@
 
     cos, sin = unpack_tables(cos_ref, sin_ref)
     q = rot(q_ref[0].astype(f32), cos, sin).astype(bf16)
-    qn_ref[g] = q
+    qn_ref[g] = q.T
     vals = jnp.concatenate([v_ref[h], jnp.ones((tok, 128), bf16)], axis=1)
     for c in range(2):
         sl = slice(c * half, (c + 1) * half)
@@ -194,7 +198,7 @@
 def make_join_kernel(codes):
     def join_kernel(
         info, start_ref, acc_ref, m_ref, l_ref, on_ref, q1_ref, ga_ref, gb_ref, og_ref, gain_ref,
-        attn_ref, rr_ref, e1_ref, rs_ref, ar_ref, or_ref, stat_ref,
+        attn_ref, rr_ref, ls_ref, e1_ref, rs_ref, ar_ref, or_ref, stat_ref,
         start_s, m_s, l_s, acc_s, sq_s, cr_s,
     ):
         g = pl.program_id(0)
@@ -278,6 +282,8 @@
             ar_ref[hh] = dot_nn(hot, attn).astype(bf16)
             or_ref[hh] = dot_nn(hot, og_ref[hh]).astype(bf16)
 
+        ls_ref[g] = m_s[sel] + jnp.log(l_s[sel])
+
         @pl.when(g == pl.num_programs(0) - 1)
         def _():
             stat_ref[...] = jnp.concatenate([compact(row_sum(sq_s[...])), compact(row_sum(cr_s[...]))], axis=0)
@@ -346,12 +352,11 @@
     return rows_kernel
 
 
-def next_back_kernel(info, do_ref, q_ref, k_ref, v_ref, e_ref, dq_ref, dk_ref, dv_ref):
+def next_back_kernel(info, do_ref, q_ref, v_ref, e_ref, dk_ref, dv_ref):
     g = pl.program_id(0)
     h = 2 * g + info[1]
-    tok = q_ref.shape[1]
+    tok = e_ref.shape[1]
     half = tok // 2
-    scale = 1.0 / math.sqrt(q_ref.shape[2])
     dl = spread(unpack3(do_ref[0, tok:, :], tok // 128, 0))
     dk = jnp.zeros((128, tok), f32)
     dv = jnp.zeros((128, tok), f32)
@@ -361,11 +366,49 @@
         do = do_ref[0, sl, :]
         dp = dot_nt(do, v_ref[h])
         ds = (e.astype(f32) * (dp - jnp.concatenate([dl[sl]] * (tok // 128), axis=1))).astype(bf16)
-        dq_ref[0, sl, :] = (dot_nn(ds, k_ref[h]) * scale).astype(bf16)
-        dk = dk + dot_tn(q_ref[g, sl, :], ds)
+        dk = dk + dot_nn(q_ref[g, :, sl], ds)
         dv = dv + dot_tn(do, e)
     dk_ref[g] = dk.T
     dv_ref[g] = dv.T
+
+
+def make_prev_back_kernel(feats):
+    def prev_back_kernel(
+        info, start_ref, stat_ref, other_ref, q_ref, attn_ref, ls_ref, og_ref, gain_ref, kv_ref,
+        dq_ref, bias_ref, rinv_s, cc_s,
+    ):
+        g = pl.program_id(0)
+        index, sel = info[0], info[2]
+        tok = q_ref.shape[1]
+        half = tok // 2
+        scale = 1.0 / math.sqrt(q_ref.shape[2])
+        h = 2 * g + sel
+
+        @pl.when(g == 0)
+        def _():
+            rinv, cc = norm_terms(stat_ref, other_ref, feats)
+            rinv_s[...] = spread(rinv)
+            cc_s[...] = spread(cc)
+            start = spread(start_ref[...])
+            first = jnp.where(index == 0, float(tok), 0.0)
+            for c in range(tok // 128):
+                key = (lanes_of((tok, 128)) + c * 128).astype(f32)
+                ok = (key - tok >= start) & (key >= first)
+                bias_ref[:, c * 128 : (c + 1) * 128] = jnp.where(ok, 0.0, NEG)
+
+        af, ag, delta = grad_terms(attn_ref[h], og_ref[0], gain_ref[0], rinv_s[...], cc_s[...])
+        do = ag.astype(bf16)
+        lse = ls_ref[g]
+        for c in range(2):
+            sl = slice(c * half, (c + 1) * half)
+            wide = lambda x: jnp.concatenate([x[sl]] * (tok // 128), axis=1)
+            z = dot_nt(q_ref[h, sl, :], kv_ref[0, 0]) * scale + bias_ref[sl, :]
+            prob = jnp.exp(z - wide(lse)).astype(bf16)
+            dp = dot_nt(do[sl], kv_ref[1, 0])
+            ds = (prob.astype(f32) * (dp - wide(delta))).astype(bf16)
+            dq_ref[g, sl, :] = dot_nn(ds, kv_ref[0, 0])
+
+    return prev_back_kernel
 
 
 def make_back_own_kernel(feats, first, aliased):
@@ -375,8 +418,7 @@
     ):
         normed_ref, dq_ref, dk_ref, dv_ref, rinv_s, cc_s, ag_s, de_s = refs[aliased:]
         step = pl.program_id(0)
-        h = step + first
-        tok = q_ref.shape[1]
+        tok = og_ref.shape[1]
         nb = e1_ref.shape[1]
         rate = tok // nb
         count = ga_ref.shape[2]
@@ -388,37 +430,39 @@
             rinv_s[...] = spread(rinv)
             cc_s[...] = spread(cc)
 
-        rinv = rinv_s[...]
-        af, ag, delta = grad_terms(attn_ref[h], og_ref[0], gain_ref[0], rinv, cc_s[...])
-        normed_ref[0] = (af * rinv * gain_ref[0]).astype(bf16)
-        ag_s[...] = ag
-        de_s[...] = delta
-        r = low_half(rr_ref[h])
-        do = (ag * r).astype(bf16)
-        dl = delta * r
-        dks = []
-        for c in range(2):
-            lo, n = c * half, (c + 1) * half
-            sl = slice(lo, n)
-            e = e_ref[h, sl, :n]
-            dp = dot_nt(do[sl], v_ref[h, :n, :])
-            ds = (e.astype(f32) * (dp - jnp.concatenate([dl[sl]] * (n // 128), axis=1))).astype(bf16)
-            dq_ref[h, sl, :] = dot_nn(ds, k_ref[h, :n, :])
-            dks.append((dot_tn(q_ref[h, sl, :], ds), dot_tn(do[sl], e)))
-        for i, ref in enumerate((dk_ref, dv_ref)):
-            ref[h, :half, :] = (dks[0][i] + dks[1][i][:, :half]).T
-            ref[h, half:, :] = dks[1][i][:, half:].T
-
-        rows = pl.ds(info[4 + h], nb, stride=rate)
-        r1 = high_half(rs_ref[0])
-        g1 = (ag_s[rows, :] * r1).astype(bf16)
-        d1 = (de_s[rows, :] * r1)[:, :1]
-        dq1 = jnp.zeros((nb, 128), f32)
-        for part, ref in enumerate((ga_ref, gb_ref)):
-            dp1 = dot_nt(g1, ref[1, 0])
-            ds1 = (e1_ref[0, :, part * count : (part + 1) * count].astype(f32) * (dp1 - d1)).astype(bf16)
-            dq1 = dq1 + dot_nn(ds1, ref[0, 0])
-        dq_ref[h, rows, :] += dq1
+        for hh in range(2):
+            h = 2 * (step + first) + hh
+            rinv = rinv_s[...]
+            af, ag, delta = grad_terms(attn_ref[h], og_ref[hh], gain_ref[hh], rinv, cc_s[...])
+            normed_ref[hh] = (af * rinv * gain_ref[hh]).astype(bf16)
+            ag_s[hh] = ag
+            de_s[hh] = delta
+            r = low_half(rr_ref[h])
+            do = (ag * r).astype(bf16)
+            dl = delta * r
+            dks = []
+            for c in range(2):
+                lo, n = c * half, (c + 1) * half
+                sl = slice(lo, n)
+                e = e_ref[h, sl, :n]
+                dp = dot_nt(do[sl], v_ref[h, :n, :])
+                ds = (e.astype(f32) * (dp - jnp.concatenate([dl[sl]] * (n // 128), axis=1))).astype(bf16)
+                dq_ref[h, sl, :] = dot_nn(ds, k_ref[h, :n, :])
+                dks.append((dot_nn(q_ref[h, :, sl], ds), dot_tn(do[sl], e)))
+            for i, ref in enumerate((dk_ref, dv_ref)):
+                ref[h, :half, :] = (dks[0][i] + dks[1][i][:, :half]).T
+                ref[h, half:, :] = dks[1][i][:, half:].T
+
+            rows = pl.ds(info[4 + h], nb, stride=rate)
+            r1 = high_half(rs_ref[hh])
+            g1 = (ag_s[hh, rows, :] * r1).astype(bf16)
+            d1 = (de_s[hh, rows, :] * r1)[:, :1]
+            dq1 = jnp.zeros((nb, 128), f32)
+            for part, ref in enumerate((ga_ref, gb_ref)):
+                dp1 = dot_nt(g1, ref[1, hh])
+                ds1 = (e1_ref[hh, :, part * count : (part + 1) * count].astype(f32) * (dp1 - d1)).astype(bf16)
+                dq1 = dq1 + dot_nn(ds1, ref[0, hh])
+            dq_ref[h, rows, :] += dq1
 
     return back_own_kernel
 
@@ -443,7 +487,7 @@
         for hh in range(2):
             h = 2 * g + hh
             off = info[4 + h]
-            dq = dq_ref[h] * scale + jnp.where(sel == hh, dqn_ref[0].astype(f32), 0.0)
+            dq = dq_ref[h] * scale + jnp.where(sel == hh, dqn_ref[g] * scale, 0.0)
             gq_ref[hh] = rot(dq, cos, -sin).astype(bf16)
             here = par == hh
             dk_s[hh] = (dk_ref[h] + jnp.where(here, dkn_ref[g], 0.0)) * scale
@@ -575,11 +619,12 @@
 
     q_send = lax.dynamic_index_in_dim(queries.reshape(pairs, 2, tok, width), (index + 1) % 2, 1, keepdims=False)
     q_raw = lax.ppermute(q_send, "ctx", down)
-    k_rot, rows = call(
+    k_rot, kv_send, rows = call(
         prep_kernel, (info,), (pairs,),
         [vm(keys), vm(values), whole(cos), whole(sin)],
         [
             (full, bf16, None, None),
+            ((2, pairs, tok, width), bf16, (2, 1, tok, width), g4),
             ((2, heads, nb, width), bf16, (2, 2, nb, width), g4),
         ],
     )
@@ -592,6 +637,7 @@
     def own(first, n, qs, prior):
         outs = [
             (full, bf16, None, None),
+            ((heads, width, tok), bf16, None, None),
             ((heads, tok, tok), bf16, None, None),
             (full, f32, None, None),
             (full, f32, None, None),
@@ -606,13 +652,14 @@
         alias = []
         for i, a in enumerate(prior):
             alias.append((len(ins), i))
-            ins.append(vm(a) if i < 5 else (a, (2, nb, width), lambda g, *s: (first, 0, 0)))
+            ins.append(vm(a) if i < 6 else (a, (2, nb, width), lambda g, *s: (first, 0, 0)))
         return call(
             make_own_kernel(first, len(prior)), (info,), (n,), ins, outs,
             [pltpu.VMEM((tok, tok), f32)], alias,
         )
 
-    part = own(0, pairs // 2, queries, [])
+    cut = pairs // 2
+    part = own(0, cut, queries, [])
     for a in ahead:
         x = jnp.concatenate([x, after(a, part[3])], axis=2)
     x = after(x, part[3])
@@ -628,18 +675,19 @@
         [
             ((pairs, tok + extra, width), bf16, (1, tok + extra, width), gp),
             ((pairs, tok, tok), bf16, None, None),
-            ((pairs, tok, width), bf16, None, None),
+            ((pairs, width, tok), bf16, None, None),
         ],
         [pltpu.VMEM((tok, tok), f32)] + [pltpu.VMEM((tok, 128), f32)] * 2,
     )
     y = jnp.concatenate([x, after(pending, e_next)], axis=2)
     pending = swap(y, y_code)
     o_prev = lax.ppermute(o_send, "ctx", up)
-    q_rot, e_own, acc, m_own, lsum, q1 = own(pairs // 2, pairs - pairs // 2, after(queries, y), part)
+    q_rot, q_t, e_own, acc, m_own, lsum, q1 = own(cut, pairs - cut, after(queries, y), part)
     ga = jnp.concatenate([y, after(pending, m_own)], axis=2)
     gb = swap(ga, core)
-
-    attn, rr, e1, rs, attn_rows, og_rows, stat = call(
+    kv_prev = lax.ppermute(after(kv_send, gb, o_prev), "ctx", up)
+
+    attn, rr, lse, e1, rs, attn_rows, og_rows, stat = call(
         make_join_kernel(codes), (info,), (pairs,),
         [
             whole(start_rel), vm(acc), vm(m_own), vm(lsum),
@@ -653,6 +701,7 @@
         [
             (full, bf16, None, None),
             (full, f32, None, None),
+            ((pairs, tok, width), f32, None, None),
             ((heads, nb, SEL), bf16, (2, nb, SEL), gp),
             ((heads, nb, width), f32, (2, nb, width), gp),
             ((heads, nb, width), bf16, (2, nb, width), gp),
@@ -699,54 +748,63 @@
         hg = lambda h, *s: (0, h + first, 0, 0)
         ins = [
             whole(stat), whole(after(other, *deps)),
-            vm(q_rot), vm(k_rot), vm(vals), vm(attn), vm(rr), vm(e_own),
-            (out_grad, one3, hp),
-            (gain, (1, 1, width), hp),
-            (e1, (1, nb, SEL), hp),
-            (rs, (1, nb, width), hp),
-            (ga, (2, 1, half_count, width), hg),
-            (gb, (2, 1, half_count, width), hg),
+            vm(q_t), vm(k_rot), vm(vals), vm(attn), vm(rr), vm(e_own),
+            (out_grad, pair3, hp),
+            (gain, (2, 1, width), hp),
+            (e1, (2, nb, SEL), hp),
+            (rs, (2, nb, width), hp),
+            (ga, (2, 2, half_count, width), hg),
+            (gb, (2, 2, half_count, width), hg),
         ]
         alias = []
         for i, a in enumerate(prior):
             alias.append((len(ins), i))
-            ins.append(vm(a) if i >= 1 else (a, (1, 16, width), lambda h, *s: (first, 0, 0)))
+            ins.append(vm(a) if i >= 1 else (a, (1, 16, width), lambda h, *s: (2 * first, 0, 0)))
         return call(
             make_back_own_kernel(feats, first, len(prior)), (info,), (n,), ins,
             [
-                (full, bf16, one3, hp),
+                (full, bf16, pair3, hp),
                 (full, f32, None, None),
                 (full, f32, None, None),
                 (full, f32, None, None),
             ],
-            [pltpu.VMEM((tok, 128), f32)] * 4,
+            [pltpu.VMEM((tok, 128), f32)] * 2 + [pltpu.VMEM((2, tok, 128), f32)] * 2,
             alias,
         )
 
-    cut = heads // 2 + 1
-    part = back_own(0, cut, (flat,), [])
+    part = back_own(0, cut, (flat, kv_prev), [])
     for a in ahead:
         x = join0(x, after(a, part[2]))
     x = after(x, part[2])
     pending = swap(x, z_code)
-
-    dq_send, dk_next, dv_next = call(
+    normed, dq_own, dk_own, dv_own = back_own(cut, pairs - cut, (x,), part)
+    y = join0(x, after(pending, dk_own))
+    pending = swap(y, y_code)
+
+    dk_next, dv_next = call(
         next_back_kernel, (info,), (pairs,),
         [
-            (after(do_next, x), (1, tok + more, width), gp),
-            vm(q_next), vm(k_rot), vm(vals), vm(e_next),
-        ],
-        [
-            ((pairs, tok, width), bf16, one3, gp),
+            (after(do_next, y), (1, tok + more, width), gp),
+            vm(q_next), vm(vals), vm(e_next),
+        ],
+        [
             ((pairs, tok, width), f32, None, None),
             ((pairs, tok, width), f32, None, None),
         ],
     )
-    y = join0(x, after(pending, dk_next))
-    pending = swap(y, y_code)
-    dq_prev = lax.ppermute(dq_send, "ctx", up)
-    normed, dq_own, dk_own, dv_own = back_own(cut, heads - cut, (y,), part)
-    sa = after(join0(y, after(pending, dk_own)), dq_prev)
+    (dq_prev,) = call(
+        make_prev_back_kernel(feats), (info,), (pairs,),
+        [
+            whole(after(start_rel, dk_next)), whole(stat), whole(other),
+            vm(q_rot), vm(attn), vm(lse),
+            (out_grad, one3, mine),
+            (gain, (1, 1, width), mine),
+            (kv_prev, (2, 1, tok, width), g4),
+        ],
+        [((pairs, tok, width), f32, None, None)],
+        [pltpu.VMEM((tok, tok), f32)] + [pltpu.VMEM((tok, 128), f32)] * 2,
+    )
+    sa = join0(y, after(pending, dq_prev))
     sb = swap(sa, core)
 
     def sort(x):
@@ -759,8 +817,7 @@
     grad_queries, grad_keys, grad_values = call(
         make_final_kernel(codes), (info,), (pairs,),
         [
-            vm(dq_own), vm(dk_own), vm(dv_own), vm(dk_next), vm(dv_next),
-            (dq_prev, one3, gp),
+            vm(dq_own), vm(dk_own), vm(dv_own), vm(dk_next), vm(dv_next), vm(dq_prev),
             (rows, (2, 2, nb, width), g4),
             (sa, (2, 2, half_count, width), g4),
             (sb, (2, 2, half_count, width), g4),

time: 91.3 us -> 89.3 us (0.978)
  starting transfers between devices: 27 us -> 25.6 us
    ppermute x8, starting transfers between devices: 19.8 us -> 14.7 us  [swap(): return lax.ppermute(x, 'ctx', [(i, i ^ code) for i in range(ctx)])]
    ppermute x1, starting transfers between devices: 1.32 us -> 4.92 us  [body(): kv_prev = lax.ppermute(after(kv_send, gb, o_prev), 'ctx', up)]
    pallas_call x10 -> x11, Pallas kernels: 44.1 us -> 44.8 us  [call(): pl.pallas_call(kernel, out_shape=out_shape, grid_spec=pltpu.PrefetchScala...]
  transfers between devices with their start and end apart: 13 -> 13, of which waited for: 8 -> 6; matrix products, arithmetic and copies ran while one was open for 3% -> 3% of each run, Pallas kernels for 33% -> 44%
where the time goes in v4:
time: 89.3 us; the launch traced here: 88.9 us
  Pallas kernels  44.8 us (50%)
  starting transfers between devices  25.6 us (29%)
  waiting for transfers between devices  12.8 us (14%)
  local copies, waits for them, and re-layouts  2.49 us (3%)
  other arithmetic  2.26 us (3%)
  between operations  1.03 us (1%)
    pallas_call x11, Pallas kernels, call(): pl.pallas_call(kernel, out_shape=out_shape, grid_spec=pltpu.PrefetchScala...  44.8 us
    ppermute x8, starting transfers between devices, swap(): return lax.ppermute(x, 'ctx', [(i, i ^ code) for i in range(ctx)])  14.7 us
    ppermute x8, waiting for transfers between devices, swap(): return lax.ppermute(x, 'ctx', [(i, i ^ code) for i in range(ctx)])  10.6 us
    ppermute x1, starting transfers between devices, body(): kv_prev = lax.ppermute(after(kv_send, gb, o_prev), 'ctx', up)  4.92 us
    ppermute x1, waiting for transfers between devices, body(): other = lax.ppermute(stat, 'head', [(0, 1), (1, 0)])  2.12 us
    squeeze x1, local copies, waits for them, and re-layouts, body(): lax.dynamic_index_in_dim(queries.reshape(pairs, 2, tok, width), (index +...  2.03 us
  transfers between devices with their start and end apart: 13, of which 6 were waited for; matrix products, arithmetic and copies ran while one was open for 3% of the time, Pallas kernels for 44%

profile of v4, /device:TPU:0, one launch (start us, length us, event | category | flops | bytes accessed | tf_op | source)
XLA Modules:
  0.0 88.9 jit_solution(18001391553925294098)
XLA Ops:
  0.6 0.0 copy-start.5
  0.7 2.0 %dynamic-slice_bitcast_fusion = bf16[4,512,128]{2,1,0:T(8,128)(2,1)} fusion(bf16[4,2,512,128]{3,2,1,0:T(8,128)(2,1)} %bitcast.23, s32[]{:T(128)S(6)} %select_n.40), kind=kLoop, calls=%fused_computation | loop fusion | bytes 1048580 | tf_op jit(solution)/shard_map/jit(dynamic_index_in_dim)/squeeze | solution.py:620
  2.7 1.3 %collective-permute-start.2 = (bf16[4,512,128]{2,1,0:T(8,128)(2,1)}, bf16[4,512,128]{2,1,0:T(8,128)(2,1)}, u32[]{:S(2)}, u32[]{:S(2)}) collective-permute-start(bf16[4,512,128]{2,1,0:T(8,128)(2,1)} %dynamic-slice_bitcast_fusion), channel_id=1, source_target_pairs={{2,0},{4,2},{6,4},{8,6},{10,8},{12,10},{14,12},{16,14},{18,16},{20... | collective-permute-start | bytes 1572872 | tf_op jit(solution)/shard_map/ppermute | solution.py:621
  4.0 0.9 convert_bitcast_fusion
  4.9 0.2 broadcast_multiply_fusion.1
  5.1 0.5 fusion.2
  5.7 0.1 fusion.6.info
  5.8 2.1 %shard_map.102 = (bf16[8,512,128]{2,1,0:T(8,128)(2,1)S(1)}, bf16[2,4,512,128]{3,2,1,0:T(8,128)(2,1)S(1)}, bf16[2,8,16,128]{3,2,1,0:T(8,128)(2,1)S(1)}) custom-call(s32[12]{0:T(128)S(1)} %fusion.6.info, bf16[8,512,128]{2,1,0:T(8,128)(2,1)S(1)} %copy-done.3, bf16[8,512,128]{2,1,0:T(8,128)(2,1)S(1)} %copy-done, f32[256,128]{1,0:T(8,128)S(1)} %get-tuple-element.125.cos_ref, ...), custom_call_target="tpu_custom_call" | custom-call | bytes 12000000 | tf_op jit(solution)/shard_map/pallas_call | solution.py:542
  7.8 4.6 %collective-permute-start = (bf16[2,8,16,128]{3,2,1,0:T(8,128)(2,1)S(1)}, bf16[2,8,16,128]{3,2,1,0:T(8,128)(2,1)S(1)}, u32[]{:S(2)}, u32[]{:S(2)}) collective-permute-start(bf16[2,8,16,128]{3,2,1,0:T(8,128)(2,1)S(1)} %get-tuple-element.63.rows_ref), channel_id=1, source_target_pairs={{0,8},{2,10},{4,12},{6,14},{8,0},{10,2},{12,4},{14,6},{16,24},{18,... | collective-permute-start | bytes 196616 | tf_op jit(solution)/shard_map/ppermute | solution.py:607
  12.4 3.3 %shard_map.103 = (bf16[8,512,128]{2,1,0:T(8,128)(2,1)S(1)}, bf16[8,128,512]{2,1,0:T(8,128)(2,1)S(1)}, bf16[8,512,512]{2,1,0:T(8,128)(2,1)S(1)}, f32[8,512,128]{2...) custom-call(s32[12]{0:T(128)S(1)} %fusion.6.info, ...), custom_call_target="tpu_custom_call" | custom-call | bytes 12000000 | tf_op jit(solution)/shard_map/pallas_call | solution.py:542
  15.8 1.5 %collective-permute-done = bf16[2,8,16,128]{3,2,1,0:T(8,128)(2,1)S(1)} collective-permute-done((bf16[2,8,16,128]{3,2,1,0:T(8,128)(2,1)S(1)}, bf16[2,8,16,128]{3,2,1,0:T(8,128)(2,1)S(1)}, u32[]{:S(2)}, u32[]{:S(2)}) %collective-permute-start) | collective-permute-done | bytes 65568 | tf_op jit(solution)/shard_map/ppermute | solution.py:607
  17.3 3.4 %collective-permute-start.1 = (bf16[2,8,32,128]{3,2,1,0:T(8,128)(2,1)S(1)}, bf16[2,8,32,128]{3,2,1,0:T(8,128)(2,1)S(1)}, u32[]{:S(2)}, u32[]{:S(2)}) collective-permute-start(bf16[2,8,32,128]{3,2,1,0:T(8,128)(2,1)S(1)} %pad_maximum_fusion.2), channel_id=1, source_target_pairs={{0,16},{2,18},{4,20},{6,22},{8,24},{10,26},{12,28},{14,30},{16,0},... | collective-permute-start | bytes 393224 | tf_op jit(solution)/shard_map/ppermute | solution.py:607
  20.7 0.5 fusion
  21.3 0.0 collective-permute-done.2.q_ref
  21.3 5.0 %shard_map.104 = (bf16[4,544,128]{2,1,0:T(8,128)(2,1)S(1)}, bf16[4,512,512]{2,1,0:T(8,128)(2,1)S(1)}, bf16[4,128,512]{2,1,0:T(8,128)(2,1)S(1)}) custom-call(s32[12]{0:T(128)S(1)} %fusion.6.info, f32[4,128]{1,0:T(4,128)S(1)} %get-tuple-element.137.start_ref, bf16[4,512,128]{2,1,0:T(8,128)(2,1)} %collective-permute-done.2.q_ref, ...), custom_call_target="tpu_custom_call" | custom-call | bytes 12000000 | tf_op jit(solution)/shard_map/pallas_call | solution.py:542
  26.3 0.0 collective-permute-done.1
  26.3 0.1 constant_dynamic-update-slice_fusion.3
  26.4 0.2 collective-permute-start.4
  26.6 1.8 %collective-permute-start.3 = (bf16[4,544,128]{2,1,0:T(8,128)(2,1)S(1)}, bf16[4,544,128]{2,1,0:T(8,128)(2,1)S(1)}, u32[]{:S(2)}, u32[]{:S(2)}) collective-permute-start(bf16[4,544,128]{2,1,0:T(8,128)(2,1)S(1)} %get-tuple-element.81), channel_id=1, source_target_pairs={{0,2},{2,4},{4,6},{6,8},{8,10},{10,12},{12,14},{14,16},{16,18},{18... | collective-permute-start | bytes 1671176 | tf_op jit(solution)/shard_map/ppermute | solution.py:684
  28.4 0.0 copy-start.1
  28.4 0.0 copy-start.4
  28.4 3.4 %shard_map.105 = (bf16[8,512,128]{2,1,0:T(8,128)(2,1)S(1)}, bf16[8,128,512]{2,1,0:T(8,128)(2,1)S(1)}, bf16[8,512,512]{2,1,0:T(8,128)(2,1)S(1)}, f32[8,512,128]{2...) custom-call(s32[12]{0:T(128)S(1)} %fusion.6.info, ...), custom_call_target="tpu_custom_call", output_to_operand_aliasing={{0}: (7, {}), {1}: (8, {}), {2}: (9, {}), {3}: (10, {}), {4... | custom-call | bytes 12000000 | tf_op jit(solution)/shard_map/pallas_call | solution.py:542
  31.7 1.5 %collective-permute-done.4 = bf16[2,8,64,128]{3,2,1,0:T(8,128)(2,1)S(1)} collective-permute-done((bf16[2,8,64,128]{3,2,1,0:T(8,128)(2,1)S(1)}, bf16[2,8,64,128]{3,2,1,0:T(8,128)(2,1)S(1)}, u32[]{:S(2)}, u32[]{:S(2)}) %collective-permute-start.4) | collective-permute-done | bytes 262176 | tf_op jit(solution)/shard_map/ppermute | solution.py:607
  33.3 0.7 collective-permute-start.5
  34.0 0.0 collective-permute-done.3.on_ref
  34.0 1.5 %collective-permute-done.5.gb_ref = bf16[2,8,128,128]{3,2,1,0:T(8,128)(2,1)S(1)} collective-permute-done((bf16[2,8,128,128]{3,2,1,0:T(8,128)(2,1)S(1)}, bf16[2,8,128,128]{3,2,1,0:T(8,128)(2,1)S(1)}, u32[]{:S(2)}, u32[]{:S(2)}) %collective-permute-start.5) | collective-permute-done | bytes 524320 | tf_op jit(solution)/shard_map/ppermute | solution.py:607
  35.6 4.9 %collective-permute-start.8 = (bf16[2,4,512,128]{3,2,1,0:T(8,128)(2,1)S(1)}, bf16[2,4,512,128]{3,2,1,0:T(8,128)(2,1)S(1)}, u32[]{:S(2)}, u32[]{:S(2)}) collective-permute-start(bf16[2,4,512,128]{3,2,1,0:T(8,128)(2,1)S(1)} %get-tuple-element.93), channel_id=1, source_target_pairs={{0,2},{2,4},{4,6},{6,8},{8,10},{10,12},{12,14},{14,16},{16,18},{18... | collective-permute-start | bytes 3145736 | tf_op jit(solution)/shard_map/ppermute | solution.py:688
  40.5 6.5 %shard_map.106 = (bf16[8,512,128]{2,1,0:T(8,128)(2,1)S(1)}, f32[8,512,128]{2,1,0:T(8,128)S(1)}, f32[4,512,128]{2,1,0:T(8,128)S(1)}, bf16[8,16,256]{2,1,0:T(8,128...) custom-call(s32[12]{0:T(128)S(1)} %fusion.6.info, ...), custom_call_target="tpu_custom_call" | custom-call | bytes 12000000 | tf_op jit(solution)/shard_map/pallas_call | solution.py:542
  47.0 1.6 %collective-permute-start.6 = (f32[8,128]{1,0:T(8,128)S(1)}, f32[8,128]{1,0:T(8,128)S(1)}, u32[]{:S(2)}, u32[]{:S(2)}) collective-permute-start(f32[8,128]{1,0:T(8,128)S(1)} %get-tuple-element.84.stat_ref), channel_id=1, source_target_pairs={{0,1},{1,0},{2,3},{3,2},{4,5},{5,4},{6,7},{7,6},{8,9},{9,8},{10,11... | collective-permute-start | bytes 12296 | tf_op jit(solution)/shard_map/ppermute | solution.py:713
  48.6 2.1 %collective-permute-done.6.other_ref = f32[8,128]{1,0:T(8,128)S(1)} collective-permute-done((f32[8,128]{1,0:T(8,128)S(1)}, f32[8,128]{1,0:T(8,128)S(1)}, u32[]{:S(2)}, u32[]{:S(2)}) %collective-permute-start.6) | collective-permute-done | bytes 4128 | tf_op jit(solution)/shard_map/ppermute | solution.py:713
  50.7 2.2 %shard_map.107 = (bf16[2,8,16,128]{3,2,1,0:T(8,128)(2,1)S(1)}, f32[16,128]{1,0:T(8,128)S(1)}, bf16[4,528,128]{2,1,0:T(8,128)(2,1)S(1)}) custom-call(s32[12]{0:T(128)S(1)} %fusion.6.info, f32[4,128]{1,0:T(4,128)S(1)} %get-tuple-element.134.begin_ref, f32[8,128]{1,0:T(8,128)S(1)} %get-tuple-element.84.stat_ref, f32[8,128]{1,0:T(8,128)S(1)} %collective-permute-done.6.other_ref, ...), custom_call_target="tpu_custom_call" | custom-call | bytes 12000000 | tf_op jit(solution)/shard_map/pallas_call | solution.py:542
  52.9 2.1 %collective-permute-start.7 = (bf16[1,272,128]{2,1,0:T(8,128)(2,1)S(1)}, bf16[1,272,128]{2,1,0:T(8,128)(2,1)S(1)}, u32[]{:S(2)}, u32[]{:S(2)}) collective-permute-start(bf16[1,272,128]{2,1,0:T(8,128)(2,1)S(1)} %maximum_bitcast_fusion), channel_id=1, source_target_pairs={{0,8},{2,10},{4,12},{6,14},{8,0},{10,2},{12,4},{14,6},{16,24},{18,... | collective-permute-start | bytes 208904 | tf_op jit(solution)/shard_map/ppermute | solution.py:607
  55.0 1.5 %collective-permute-start.9 = (bf16[4,528,128]{2,1,0:T(8,128)(2,1)S(1)}, bf16[4,528,128]{2,1,0:T(8,128)(2,1)S(1)}, u32[]{:S(2)}, u32[]{:S(2)}) collective-permute-start(bf16[4,528,128]{2,1,0:T(8,128)(2,1)S(1)} %get-tuple-element.109), channel_id=1, source_target_pairs={{2,0},{4,2},{6,4},{8,6},{10,8},{12,10},{14,12},{16,14},{18,16},{20... | collective-permute-start | bytes 1622024 | tf_op jit(solution)/shard_map/ppermute | solution.py:744
  56.5 0.0 collective-permute-done.8.kv_ref
  56.5 4.0 %shard_map.108 = (bf16[8,512,128]{2,1,0:T(8,128)(2,1)}, f32[8,512,128]{2,1,0:T(8,128)S(1)}, f32[8,512,128]{2,1,0:T(8,128)S(1)}, f32[8,512,128]{2,1,0:T(8,128)S(1)}) custom-call(s32[12]{0:T(128)S(1)} %fusion.6.info, f32[8,128]{1,0:T(8,128)S(1)} %get-tuple-element.84.stat_ref, f32[8,128]{1,0:T(8,128)S(1)} %collective-permute-done.6.other_ref, ...), custom_call_target="tpu_custom_call" | custom-call | bytes 12000000 | tf_op jit(solution)/shard_map/pallas_call | solution.py:542
  60.5 0.0 collective-permute-done.7
  60.6 3.5 %collective-permute-start.10 = (bf16[2,272,128]{2,1,0:T(8,128)(2,1)S(1)}, bf16[2,272,128]{2,1,0:T(8,128)(2,1)S(1)}, u32[]{:S(2)}, u32[]{:S(2)}) collective-permute-start(bf16[2,272,128]{2,1,0:T(8,128)(2,1)S(1)} %pad_maximum_fusion), channel_id=1, source_target_pairs={{0,16},{2,18},{4,20},{6,22},{8,24},{10,26},{12,28},{14,30},{16,0},... | collective-permute-start | bytes 417800 | tf_op jit(solution)/shard_map/ppermute | solution.py:607
  64.1 4.7 %shard_map.109 = (bf16[8,512,128]{2,1,0:T(8,128)(2,1)}, f32[8,512,128]{2,1,0:T(8,128)S(1)}, f32[8,512,128]{2,1,0:T(8,128)S(1)}, f32[8,512,128]{2,1,0:T(8,128)S(1)}) custom-call(s32[12]{0:T(128)S(1)} %fusion.6.info, f32[8,128]{1,0:T(8,128)S(1)} %get-tuple-element.84.stat_ref, ...), custom_call_target="tpu_custom_call", output_to_operand_aliasing={{0}: (15, {}), {1}: (16, {}), {2}: (17, {}), {3}: (18, {})} | custom-call | bytes 12000000 | tf_op jit(solution)/shard_map/pallas_call | solution.py:542
  68.8 4.2 %collective-permute-done.10 = bf16[2,272,128]{2,1,0:T(8,128)(2,1)S(1)} collective-permute-done((bf16[2,272,128]{2,1,0:T(8,128)(2,1)S(1)}, bf16[2,272,128]{2,1,0:T(8,128)(2,1)S(1)}, u32[]{:S(2)}, u32[]{:S(2)}) %collective-permute-start.10) | collective-permute-done | bytes 139296 | tf_op jit(solution)/shard_map/ppermute | solution.py:607
  73.0 0.1 constant_dynamic-update-slice_fusion.8
  73.1 0.1 collective-permute-start.11
  73.2 0.0 collective-permute-done.9.do_ref
  73.2 3.4 %shard_map.110 = (f32[4,512,128]{2,1,0:T(8,128)S(1)}, f32[4,512,128]{2,1,0:T(8,128)S(1)}) custom-call(s32[12]{0:T(128)S(1)} %fusion.6.info, bf16[4,528,128]{2,1,0:T(8,128)(2,1)S(1)} %collective-permute-done.9.do_ref, bf16[4,128,512]{2,1,0:T(8,128)(2,1)S(1)} %get-tuple-element.112.q_ref, bf16[8,512,128]{2,1,0:T(8,128)(2,1)S(1)} %copy-done, ...), custom_call_target="tpu_custom_call" | custom-call | bytes 12000000 | tf_op jit(solution)/shard_map/pallas_call | solution.py:542
  76.6 4.1 %shard_map.111.dqn_ref = f32[4,512,128]{2,1,0:T(8,128)S(1)} custom-call(s32[12]{0:T(128)S(1)} %fusion.6.info, f32[4,128]{1,0:T(4,128)S(1)} %get-tuple-element.115.start_ref, f32[8,128]{1,0:T(8,128)S(1)} %get-tuple-element.84.stat_ref, f32[8,128]{1,0:T(8,128)S(1)} %collective-permute-done.6.other_ref, bf16[8,512,128]{2,1,0:T(8,128)(2,1)S(1)} %get-tuple-element.116.q_ref, ...), custom_call_target="tpu_custom_call" | custom-call | bytes 12000000 | tf_op jit(solution)/shard_map/pallas_call | solution.py:542
  80.7 0.0 collective-permute-done.11
  80.7 0.1 collective-permute-start.12
  80.9 1.8 %collective-permute-done.12 = bf16[8,272,128]{2,1,0:T(8,128)(2,1)S(1)} collective-permute-done((bf16[8,272,128]{2,1,0:T(8,128)(2,1)S(1)}, bf16[8,272,128]{2,1,0:T(8,128)(2,1)S(1)}, u32[]{:S(2)}, u32[]{:S(2)}) %collective-permute-start.12) | collective-permute-done | bytes 557088 | tf_op jit(solution)/shard_map/ppermute | solution.py:607
  82.9 6.1 %shard_map.112 = (bf16[8,512,128]{2,1,0:T(8,128)(2,1)}, bf16[8,512,128]{2,1,0:T(8,128)(2,1)}, bf16[8,512,128]{2,1,0:T(8,128)(2,1)}) custom-call(s32[12]{0:T(128)S(1)} %fusion.6.info, f32[8,512,128]{2,1,0:T(8,128)S(1)} %get-tuple-element.106.dq_ref, f32[8,512,128]{2,1,0:T(8,128)S(1)} %get-tuple-element.107.dk_ref, ...), custom_call_target="tpu_custom_call" | custom-call | bytes 12000000 | tf_op jit(solution)/shard_map/pallas_call | solution.py:542
  (25 shorter events, 0.4 us)
Async XLA Ops:
  0.6 5.0 %copy-start.5 = (s32[8]{0:T(128)S(1)}, s32[8]{0:T(128)}, u32[]{:S(2)}) copy-start(s32[8]{0:T(128)} %param.13) | copy-start | bytes 100
  0.6 5.1 %copy-start = (bf16[8,512,128]{2,1,0:T(8,128)(2,1)S(1)}, bf16[8,512,128]{2,1,0:T(8,128)(2,1)}, u32[]{:S(2)}) copy-start(bf16[8,512,128]{2,1,0:T(8,128)(2,1)} %v_ref.13) | copy-start | bytes 3145732
  0.7 5.1 %copy-start.3 = (bf16[8,512,128]{2,1,0:T(8,128)(2,1)S(1)}, bf16[8,512,128]{2,1,0:T(8,128)(2,1)}, u32[]{:S(2)}) copy-start(bf16[8,512,128]{2,1,0:T(8,128)(2,1)} %k_ref.1) | copy-start | bytes 3145732
  0.7 11.7 %copy-start.2 = (bf16[8,512,128]{2,1,0:T(8,128)(2,1)S(1)}, bf16[8,512,128]{2,1,0:T(8,128)(2,1)}, u32[]{:S(2)}) copy-start(bf16[8,512,128]{2,1,0:T(8,128)(2,1)} %q_ref.2) | copy-start | bytes 3145732
  2.7 18.6 %collective-permute-start.2 = (bf16[4,512,128]{2,1,0:T(8,128)(2,1)}, bf16[4,512,128]{2,1,0:T(8,128)(2,1)}, u32[]{:S(2)}, u32[]{:S(2)}) collective-permute-start(bf16[4,512,128]{2,1,0:T(8,128)(2,1)} %dynamic-slice_bitcast_fusion), channel_id=1, source_target_pairs={{2,0},{4,2},{6,4},{8,6},{10,8},{12,10},{14,12},{16,14},{18,16},{20... | collective-permute-start | bytes 1572872 | tf_op jit(solution)/shard_map/ppermute | solution.py:621
  7.8 9.4 %collective-permute-start = (bf16[2,8,16,128]{3,2,1,0:T(8,128)(2,1)S(1)}, bf16[2,8,16,128]{3,2,1,0:T(8,128)(2,1)S(1)}, u32[]{:S(2)}, u32[]{:S(2)}) collective-permute-start(bf16[2,8,16,128]{3,2,1,0:T(8,128)(2,1)S(1)} %get-tuple-element.63.rows_ref), channel_id=1, source_target_pairs={{0,8},{2,10},{4,12},{6,14},{8,0},{10,2},{12,4},{14,6},{16,24},{18,... | collective-permute-start | bytes 196616 | tf_op jit(solution)/shard_map/ppermute | solution.py:607
  17.3 9.0 %collective-permute-start.1 = (bf16[2,8,32,128]{3,2,1,0:T(8,128)(2,1)S(1)}, bf16[2,8,32,128]{3,2,1,0:T(8,128)(2,1)S(1)}, u32[]{:S(2)}, u32[]{:S(2)}) collective-permute-start(bf16[2,8,32,128]{3,2,1,0:T(8,128)(2,1)S(1)} %pad_maximum_fusion.2), channel_id=1, source_target_pairs={{0,16},{2,18},{4,20},{6,22},{8,24},{10,26},{12,28},{14,30},{16,0},... | collective-permute-start | bytes 393224 | tf_op jit(solution)/shard_map/ppermute | solution.py:607
  26.4 6.9 %collective-permute-start.4 = (bf16[2,8,64,128]{3,2,1,0:T(8,128)(2,1)S(1)}, bf16[2,8,64,128]{3,2,1,0:T(8,128)(2,1)S(1)}, u32[]{:S(2)}, u32[]{:S(2)}) collective-permute-start(bf16[2,8,64,128]{3,2,1,0:T(8,128)(2,1)S(1)} %get-tuple-element.131), channel_id=1, source_target_pairs={{0,4},{2,6},{4,0},{6,2},{8,12},{10,14},{12,8},{14,10},{16,20},{18,... | collective-permute-start | bytes 786440 | tf_op jit(solution)/shard_map/ppermute | solution.py:607
  26.6 7.4 %collective-permute-start.3 = (bf16[4,544,128]{2,1,0:T(8,128)(2,1)S(1)}, bf16[4,544,128]{2,1,0:T(8,128)(2,1)S(1)}, u32[]{:S(2)}, u32[]{:S(2)}) collective-permute-start(bf16[4,544,128]{2,1,0:T(8,128)(2,1)S(1)} %get-tuple-element.81), channel_id=1, source_target_pairs={{0,2},{2,4},{4,6},{6,8},{8,10},{10,12},{12,14},{14,16},{16,18},{18... | collective-permute-start | bytes 1671176 | tf_op jit(solution)/shard_map/ppermute | solution.py:684
  28.4 12.1 %copy-start.1 = (bf16[8,512,128]{2,1,0:T(8,128)(2,1)S(1)}, bf16[8,512,128]{2,1,0:T(8,128)(2,1)}, u32[]{:S(2)}) copy-start(bf16[8,512,128]{2,1,0:T(8,128)(2,1)} %og_ref.9) | copy-start | bytes 3145732
  28.4 12.1 %copy-start.4 = (f32[8,128]{1,0:T(8,128)S(1)}, f32[8,128]{1,0:T(8,128)}, u32[]{:S(2)}) copy-start(f32[8,128]{1,0:T(8,128)} %param.11) | copy-start | bytes 12292
  33.3 2.2 %collective-permute-start.5 = (bf16[2,8,128,128]{3,2,1,0:T(8,128)(2,1)S(1)}, bf16[2,8,128,128]{3,2,1,0:T(8,128)(2,1)S(1)}, u32[]{:S(2)}, u32[]{:S(2)}) collective-permute-start(bf16[2,8,128,128]{3,2,1,0:T(8,128)(2,1)S(1)} %constant_dynamic-update-slice_fusion.2.ga_ref), channel_id=1, source_target_pairs={{0,2},{2,0},{4,6},{6,4},{8,10},{10,8},{12,14},{14,12},{16,18},{18,... | collective-permute-start | bytes 1572872 | tf_op jit(solution)/shard_map/ppermute | solution.py:607
  35.6 20.9 %collective-permute-start.8 = (bf16[2,4,512,128]{3,2,1,0:T(8,128)(2,1)S(1)}, bf16[2,4,512,128]{3,2,1,0:T(8,128)(2,1)S(1)}, u32[]{:S(2)}, u32[]{:S(2)}) collective-permute-start(bf16[2,4,512,128]{3,2,1,0:T(8,128)(2,1)S(1)} %get-tuple-element.93), channel_id=1, source_target_pairs={{0,2},{2,4},{4,6},{6,8},{8,10},{10,12},{12,14},{14,16},{16,18},{18... | collective-permute-start | bytes 3145736 | tf_op jit(solution)/shard_map/ppermute | solution.py:688
  47.0 3.7 %collective-permute-start.6 = (f32[8,128]{1,0:T(8,128)S(1)}, f32[8,128]{1,0:T(8,128)S(1)}, u32[]{:S(2)}, u32[]{:S(2)}) collective-permute-start(f32[8,128]{1,0:T(8,128)S(1)} %get-tuple-element.84.stat_ref), channel_id=1, source_target_pairs={{0,1},{1,0},{2,3},{3,2},{4,5},{5,4},{6,7},{7,6},{8,9},{9,8},{10,11... | collective-permute-start | bytes 12296 | tf_op jit(solution)/shard_map/ppermute | solution.py:713
  52.9 7.6 %collective-permute-start.7 = (bf16[1,272,128]{2,1,0:T(8,128)(2,1)S(1)}, bf16[1,272,128]{2,1,0:T(8,128)(2,1)S(1)}, u32[]{:S(2)}, u32[]{:S(2)}) collective-permute-start(bf16[1,272,128]{2,1,0:T(8,128)(2,1)S(1)} %maximum_bitcast_fusion), channel_id=1, source_target_pairs={{0,8},{2,10},{4,12},{6,14},{8,0},{10,2},{12,4},{14,6},{16,24},{18,... | collective-permute-start | bytes 208904 | tf_op jit(solution)/shard_map/ppermute | solution.py:607
  55.0 18.2 %collective-permute-start.9 = (bf16[4,528,128]{2,1,0:T(8,128)(2,1)S(1)}, bf16[4,528,128]{2,1,0:T(8,128)(2,1)S(1)}, u32[]{:S(2)}, u32[]{:S(2)}) collective-permute-start(bf16[4,528,128]{2,1,0:T(8,128)(2,1)S(1)} %get-tuple-element.109), channel_id=1, source_target_pairs={{2,0},{4,2},{6,4},{8,6},{10,8},{12,10},{14,12},{16,14},{18,16},{20... | collective-permute-start | bytes 1622024 | tf_op jit(solution)/shard_map/ppermute | solution.py:744
  60.6 12.5 %collective-permute-start.10 = (bf16[2,272,128]{2,1,0:T(8,128)(2,1)S(1)}, bf16[2,272,128]{2,1,0:T(8,128)(2,1)S(1)}, u32[]{:S(2)}, u32[]{:S(2)}) collective-permute-start(bf16[2,272,128]{2,1,0:T(8,128)(2,1)S(1)} %pad_maximum_fusion), channel_id=1, source_target_pairs={{0,16},{2,18},{4,20},{6,22},{8,24},{10,26},{12,28},{14,30},{16,0},... | collective-permute-start | bytes 417800 | tf_op jit(solution)/shard_map/ppermute | solution.py:607
  73.1 7.6 %collective-permute-start.11 = (bf16[4,272,128]{2,1,0:T(8,128)(2,1)S(1)}, bf16[4,272,128]{2,1,0:T(8,128)(2,1)S(1)}, u32[]{:S(2)}, u32[]{:S(2)}) collective-permute-start(bf16[4,272,128]{2,1,0:T(8,128)(2,1)S(1)} %get-tuple-element.127), channel_id=1, source_target_pairs={{0,4},{2,6},{4,0},{6,2},{8,12},{10,14},{12,8},{14,10},{16,20},{18,... | collective-permute-start | bytes 835592 | tf_op jit(solution)/shard_map/ppermute | solution.py:607
  80.7 2.0 %collective-permute-start.12 = (bf16[8,272,128]{2,1,0:T(8,128)(2,1)S(1)}, bf16[8,272,128]{2,1,0:T(8,128)(2,1)S(1)}, u32[]{:S(2)}, u32[]{:S(2)}) collective-permute-start(bf16[8,272,128]{2,1,0:T(8,128)(2,1)S(1)} %constant_dynamic-update-slice_fusion.7), channel_id=1, source_target_pairs={{0,2},{2,0},{4,6},{6,4},{8,10},{10,8},{12,14},{14,12},{16,18},{18,... | collective-permute-start | bytes 1671176 | tf_op jit(solution)/shard_map/ppermute | solution.py:607
